TPU v7x, 256 devices: a whole 4x4x8 slice. The times are simulated.
256 devices in a mesh: comp: 2 (over core), lat: 32 (over y, z), lon: 4 (over x).
Axes of the slice: x: 4, y: 4, z: 8, core: 2. Of those that a mesh axis runs over, the one named last changes fastest.
Arguments:
- increment: float32 [2, 8, 512, 2048], P('comp', None, 'lat', 'lon'), may hold values from -6 to 6
- diffusivity: float32 [2, 8, 512, 2048], P('comp', None, 'lat', 'lon'), may hold values from 0.03 to 0.24
- innovation: float32 [2, 8, 512, 2048], P('comp', None, 'lat', 'lon'), may hold values from -6 to 6
- land_mask: int32 [512, 2048], P('lat', 'lon'), may hold values 0 or 1
- pull_cells: int32 [2, 32, 4, 32, 1024], P('comp', 'lat', 'lon'), may hold values from 0 to 8191
- put_cells: int32 [2, 32, 4, 32, 1024], P('comp', 'lat', 'lon'), may hold values from 0 to 8191
- pull_weight: float32 [2, 32, 4, 32, 1024], P('comp', 'lat', 'lon'), may hold values from 0.2 to 0.8
- pull_count: int32 [2, 32, 4, 32], P('comp', 'lat', 'lon'), may hold values from 1 to 1024, 16384 in all within a row
Outputs:
- linear_state: float32 [2, 8, 512, 2048], P('comp', None, 'lat', 'lon')
- gradient: float32 [2, 8, 512, 2048], P('comp', None, 'lat', 'lon')
Inputs may be any that keep to these rules, and one draw needn't show every extreme that they name: `pull_count`: for each receiving block the counts over the 32 source bands add up to 16384, and the largest of them is 1024.
All inputs are finite; a program needn't handle non-finite values. No bound on the sum of `land_mask` on one device may be relied on, other than what follows from the above.
Results may differ from a plain program's by a relative error of at most 0.00002.
Values sent between devices are 32-bit elements; how exact they have to be, the bound alone decides.
No kernel may reach another device: no remote copies, remote signals or barrier semaphores. Data moves between devices by JAX's collectives and lax.ppermute only.
A program may use at most 64 MiB of HBM per device.

v0:
```python
import jax
import jax.numpy as jnp
from jax import lax
from jax.sharding import PartitionSpec as P

NSTEP = 4


def partner_2(value, axis, stride):
    mask = 2**stride
    pairs = [(source, source ^ mask) for source in range(lax.axis_size(axis))]
    return lax.ppermute(value, axis, pairs)


def extended(cells, sides, width, closed):
    for axis, dim in sides:
        count = lax.axis_size(axis)
        ends = count if closed else count - 1
        head = lax.slice_in_dim(cells, 0, width, axis=dim)
        tail = lax.slice_in_dim(cells, cells.shape[dim] - width, cells.shape[dim], axis=dim)
        cells = jnp.concatenate(
            [
                lax.ppermute(tail, axis, [(i, (i + 1) % count) for i in range(ends)]),
                cells,
                lax.ppermute(head, axis, [((i + 1) % count, i) for i in range(ends)]),
            ],
            axis=dim,
        )
    return cells


def mirrored(rows):
    partner = rows
    for bit in range(lax.axis_size("lon").bit_length() - 1):
        partner = partner_2(partner, "lon", bit)
    return partner[:, :, :, ::-1]


def at_fold():
    return (lax.axis_index("comp") == 1) & (lax.axis_index("lat") == lax.axis_size("lat") - 1)


def neighbours(field):
    lat_padded = extended(field, (("lat", 2),), 1, False)
    lon_padded = extended(field, (("lon", 3),), 1, True)
    folded = mirrored(field[:, :, -1:, :])[:, :, 0, :]
    north_edge = jnp.where(at_fold(), folded, lat_padded[:, :, -1, :])
    north = jnp.concatenate([lat_padded[:, :, 2:-1, :], north_edge[:, :, None, :]], axis=2)
    east = lon_padded[:, :, :, 2:]
    west = lon_padded[:, :, :, :-2]
    south = lat_padded[:, :, :-2, :]
    return (east, west, south, north)


def advance(field, coefficients):
    east, west, south, north = neighbours(field)
    change = coefficients[0] * (east - field) + coefficients[1] * (west - field)
    change = change + coefficients[2] * (south - field)
    change = change + coefficients[3] * (north - field)
    return field + change


def local(
    increment, diffusivity, innovation, land_mask, pull_cells, put_cells, pull_weight, pull_count
):
    height = increment.shape[2]
    width = increment.shape[3]
    cells = height * width
    bands = lax.axis_size("lat")
    ocean = lax.axis_index("comp") == 1
    mask_plane = jnp.where(
        ocean, land_mask.astype(jnp.float32), jnp.ones_like(land_mask, jnp.float32)
    )
    mask_levels = mask_plane[None, None]
    stacked = jnp.concatenate([diffusivity, mask_levels], axis=1)
    near = neighbours(stacked)
    coefficients = [
        mask_levels * side[:, -1:] * 0.5 * (diffusivity + side[:, :-1]) for side in near
    ]

    def sweep(field):
        for step in range(NSTEP):
            field = advance(field, coefficients)
        return field

    pulled = pull_cells.reshape(bands, -1)
    placed = put_cells.reshape(bands, -1)
    slot_count = pulled.shape[1]
    live = jnp.arange(slot_count, dtype=jnp.int32)[None, :] < pull_count.reshape(bands, 1)
    live_weight = jnp.where(
        live, pull_weight.reshape(bands, -1), jnp.zeros((bands, slot_count), jnp.float32)
    )
    mask_flat = mask_plane.reshape(-1)
    state = sweep(increment)
    surface = mask_flat * state[0, 0].reshape(-1)
    other_surface = partner_2(surface[None, :], "comp", 0)
    chosen = pulled
    values = jnp.take_along_axis(
        lax.all_gather(other_surface, "lat", axis=0, tiled=True), chosen, axis=1
    )
    income = jax.ops.segment_sum(
        (live_weight * values).reshape(-1), placed.reshape(-1), num_segments=cells
    )
    linear_state = state.at[0, 0].add((mask_flat * income).reshape(height, width))
    residual = linear_state - innovation
    residual_surface = mask_flat * residual[0, 0].reshape(-1)
    outgoing = live_weight * jnp.take(residual_surface, placed)
    chosen = pulled
    segment_ids = chosen + (jnp.arange(1 * lax.axis_size("lat"), dtype=jnp.int32) * cells)[:, None]
    summed = jax.ops.segment_sum(
        outgoing.reshape(-1), segment_ids.reshape(-1), num_segments=1 * lax.axis_size("lat") * cells
    )
    band_sums = lax.psum_scatter(
        summed.reshape(1 * lax.axis_size("lat"), cells), "lat", scatter_dimension=0, tiled=True
    )
    returned = partner_2(band_sums, "comp", 0)[0]
    adjoint_state = residual.at[0, 0].add((mask_flat * returned).reshape(height, width))
    adjoint_state = sweep(adjoint_state)
    gradient = adjoint_state + increment
    return (linear_state, gradient)


def solution(mesh):
    placed = (
        P("comp", None, "lat", "lon"),
        P("comp", None, "lat", "lon"),
        P("comp", None, "lat", "lon"),
        P("lat", "lon"),
        P("comp", "lat", "lon", None, None),
        P("comp", "lat", "lon", None, None),
        P("comp", "lat", "lon", None, None),
        P("comp", "lat", "lon", None),
    )
    return jax.shard_map(
        local,
        mesh=mesh,
        in_specs=placed,
        out_specs=(P("comp", None, "lat", "lon"), P("comp", None, "lat", "lon")),
        check_vma=False,
    )
```

profile of v0, /device:TPU:6, one launch (start us, length us, event | category | flops | bytes accessed | tf_op | source)
XLA Modules:
  0.0 1193.2 jit_solution(17627987960869966401)
XLA Ops:
  10.0 3.8 collective-permute-start.4
  16.1 3.8 collective-permute-start.5
  24.8 3.7 collective-permute-done.10
  32.2 4.1 collective-permute-done.7
  36.4 2.4 collective-permute-start.2
  39.4 3.3 collective-permute-start.3
  46.7 2.4 collective-permute-done.15
  49.1 2.8 collective-permute-start.16
  52.0 5.5 collective-permute-start.14
  64.9 2.4 collective-permute-done.21
  67.3 2.7 collective-permute-start.22
  70.1 5.2 collective-permute-start.20
  85.1 2.7 collective-permute-start.28
  87.8 4.3 collective-permute-start.26
  101.7 82.0 %all-gather.3.cloned.1.call-done = f32[32,1,8192]{2,1,0:T(1,128)} async-done(((f32[1,1,8192]{2,1,0:T(1,128)}), f32[32,1,8192]{2,1,0:T(1,128)}) %all-gather.3.cloned.1.call-update) | async-done | bytes 1048592 | tf_op jit(solution)/shard_map/all_gather | solution.py:99
  185.5 258.4 %gather_fusion.1 = f32[32768]{0:T(1024)S(1)} fusion(f32[32,8192]{1,0:T(8,128)S(1)} %bitcast.88, s32[32768]{0:T(1024)S(1)} %bitcast.89), kind=kCustom, calls=%fused_computation.1 | custom fusion | bytes 524288 | tf_op jit(solution)/shard_map/jit(take_along_axis)/gather | solution.py:98
  443.9 171.1 %scatter_custom_fusion = f32[8192]{0:T(1024)S(1)} fusion(s32[32768]{0:T(1024)S(1)} %bitcast.94, f32[32768]{0:T(1024)S(1)} %select_multiply_fusion.1, f32[]{:T(128)} %constant.98.clone.1), kind=kCustom, calls=%fused_computation.200 | custom fusion | flops 32768 | bytes 32772 | tf_op jit(solution)/shard_map/scatter-add | solution.py:101
  616.2 180.5 %gather_fusion = f32[32768]{0:T(1024)S(1)} fusion(f32[8192]{0:T(1024)S(1)} %mul.242, s32[32768]{0:T(1024)S(1)} %broadcast_clamp_fusion), kind=kCustom, calls=%fused_computation | custom fusion | bytes 393216 | tf_op jit(solution)/shard_map/jit(_take)/gather | solution.py:107
  796.8 171.6 %scatter_custom_fusion.1 = f32[262144]{0:T(1024)S(1)} fusion(s32[32768]{0:T(1024)} %bitcast.105, f32[32768]{0:T(1024)S(1)} %select_multiply_fusion, f32[]{:T(128)} %constant.98.clone.1), kind=kCustom, calls=%fused_computation.9 | custom fusion | flops 32768 | bytes 1049088 | tf_op jit(solution)/shard_map/scatter-add | solution.py:110
  970.8 146.1 %all-reduce.3.cloned.1.call-done = f32[32,8192]{1,0:T(8,128)} async-done(((f32[32,8192]{1,0:T(8,128)}), f32[32,8192]{1,0:T(8,128)}) %all-reduce.3.cloned.1.call-update) | async-done | bytes 1048592
  1126.6 2.8 collective-permute-start.34
  1139.3 3.0 collective-permute-start.42
  1142.3 3.9 collective-permute-start.40
  1146.7 2.8 collective-permute-start.39
  1153.5 2.4 collective-permute-done.47
  1155.9 2.7 collective-permute-start.48
  1158.7 4.2 collective-permute-start.46
  1163.4 2.8 collective-permute-start.45
  1170.2 2.4 collective-permute-done.53
  1172.6 2.9 collective-permute-start.54
  1175.6 4.2 collective-permute-start.52
  1180.3 2.8 collective-permute-start.51
  (202 shorter events, 82.4 us)
Async XLA Ops:
  7.2 176.4 %all-gather.3.cloned.1.call-start = ((), (), s32[]{:S(2)}) async-start(), calls=%async_computation | async-start | bytes 1081344 | tf_op jit(solution)/shard_map/all_gather | solution.py:99
  9.0 22.1 %collective-permute-start.6 = (f32[1,9,1,512]{3,2,1,0:T(1,128)S(1)}, f32[1,9,1,512]{3,2,1,0:T(1,128)S(1)}, u32[]{:S(2)}, u32[]{:S(2)}) collective-permute-start(f32[1,9,1,512]{3,2,1,0:T(1,128)S(1)} %get-tuple-element.37), channel_id=1, source_target_pairs={{0,1},{1,0},{2,3},{3,2},{4,5},{5,4},{6,7},{7,6},{8,9},{9,8},{10,11... | collective-permute-start | bytes 55304 | tf_op jit(solution)/shard_map/ppermute | solution.py:12
  10.0 32.7 %collective-permute-start.4 = (f32[1,9,1,512]{3,2,1,0:T(1,128)S(1)}, f32[1,9,1,512]{3,2,1,0:T(1,128)S(1)}, u32[]{:S(2)}, u32[]{:S(2)}) collective-permute-start(f32[1,9,1,512]{3,2,1,0:T(1,128)S(1)} %get-tuple-element.37), channel_id=1, source_target_pairs={{0,4},{4,8},{8,12},{12,16},{16,20},{20,24},{24,28},{28,32},{32,36}... | collective-permute-start | bytes 55304 | tf_op jit(solution)/shard_map/ppermute | solution.py:23
  14.8 8.3 collective-permute-start.9
  16.1 28.7 %collective-permute-start.5 = (f32[1,8,1,512]{3,2,1,0:T(1,128)S(1)}, f32[1,8,1,512]{3,2,1,0:T(1,128)S(1)}, u32[]{:S(2)}, u32[]{:S(2)}) collective-permute-start(f32[1,8,1,512]{3,2,1,0:T(1,128)S(1)} %get-tuple-element.67), channel_id=1, source_target_pairs={{0,4},{4,8},{8,12},{12,16},{16,20},{20,24},{24,28},{28,32},{32,36}... | collective-permute-start | bytes 49160 | tf_op jit(solution)/shard_map/ppermute | solution.py:23
  19.9 10.3 collective-permute-start.11
  28.5 10.8 collective-permute-start.8
  30.2 9.2 collective-permute-start
  36.4 6.3 collective-permute-start.2
  45.4 15.9 %collective-permute-start.17 = (f32[1,8,1,512]{3,2,1,0:T(1,128)S(1)}, f32[1,8,1,512]{3,2,1,0:T(1,128)S(1)}, u32[]{:S(2)}, u32[]{:S(2)}) collective-permute-start(f32[1,8,1,512]{3,2,1,0:T(1,128)S(1)} %get-tuple-element.62), channel_id=1, source_target_pairs={{4,0},{8,4},{12,8},{16,12},{20,16},{24,20},{28,24},{32,28},{36,32}... | collective-permute-start | bytes 49160 | tf_op jit(solution)/shard_map/ppermute | solution.py:25
  49.1 11.7 collective-permute-start.16
  52.0 11.2 collective-permute-start.14
  63.6 15.5 %collective-permute-start.23 = (f32[1,8,1,512]{3,2,1,0:T(1,128)S(1)}, f32[1,8,1,512]{3,2,1,0:T(1,128)S(1)}, u32[]{:S(2)}, u32[]{:S(2)}) collective-permute-start(f32[1,8,1,512]{3,2,1,0:T(1,128)S(1)} %get-tuple-element.58), channel_id=1, source_target_pairs={{4,0},{8,4},{12,8},{16,12},{20,16},{24,20},{28,24},{32,28},{36,32}... | collective-permute-start | bytes 49160 | tf_op jit(solution)/shard_map/ppermute | solution.py:25
  67.3 11.3 collective-permute-start.22
  70.1 10.8 collective-permute-start.20
  81.5 14.3 %collective-permute-start.29 = (f32[1,8,1,512]{3,2,1,0:T(1,128)S(1)}, f32[1,8,1,512]{3,2,1,0:T(1,128)S(1)}, u32[]{:S(2)}, u32[]{:S(2)}) collective-permute-start(f32[1,8,1,512]{3,2,1,0:T(1,128)S(1)} %get-tuple-element.54), channel_id=1, source_target_pairs={{4,0},{8,4},{12,8},{16,12},{20,16},{24,20},{28,24},{32,28},{36,32}... | collective-permute-start | bytes 49160 | tf_op jit(solution)/shard_map/ppermute | solution.py:25
  85.1 10.4 collective-permute-start.28
  87.8 9.8 collective-permute-start.26
  100.0 1017.0 %all-reduce.3.cloned.1.call-start = ((), (), s32[]{:S(2)}) async-start(), calls=%async_computation.1 | async-start | bytes 2097152
  1122.1 11.2 collective-permute-start.37
  1125.0 7.9 collective-permute-start.36
  1126.6 8.5 collective-permute-start.34
  1129.4 5.8 collective-permute-start.32
  1136.6 13.4 %collective-permute-start.43 = (f32[1,8,1,512]{3,2,1,0:T(1,128)S(1)}, f32[1,8,1,512]{3,2,1,0:T(1,128)S(1)}, u32[]{:S(2)}, u32[]{:S(2)}) collective-permute-start(f32[1,8,1,512]{3,2,1,0:T(1,128)S(1)} %get-tuple-element.46), channel_id=1, source_target_pairs={{4,0},{8,4},{12,8},{16,12},{20,16},{24,20},{28,24},{32,28},{36,32}... | collective-permute-start | bytes 49160 | tf_op jit(solution)/shard_map/ppermute | solution.py:25
  1139.3 10.3 collective-permute-start.42
  1142.3 9.5 collective-permute-start.40
  1152.2 14.5 %collective-permute-start.49 = (f32[1,8,1,512]{3,2,1,0:T(1,128)S(1)}, f32[1,8,1,512]{3,2,1,0:T(1,128)S(1)}, u32[]{:S(2)}, u32[]{:S(2)}) collective-permute-start(f32[1,8,1,512]{3,2,1,0:T(1,128)S(1)} %get-tuple-element.42), channel_id=1, source_target_pairs={{4,0},{8,4},{12,8},{16,12},{20,16},{24,20},{28,24},{32,28},{36,32}... | collective-permute-start | bytes 49160 | tf_op jit(solution)/shard_map/ppermute | solution.py:25
  1155.9 10.3 collective-permute-start.48
  1158.7 9.8 collective-permute-start.46
  1168.9 14.7 %collective-permute-start.55 = (f32[1,8,1,512]{3,2,1,0:T(1,128)S(1)}, f32[1,8,1,512]{3,2,1,0:T(1,128)S(1)}, u32[]{:S(2)}, u32[]{:S(2)}) collective-permute-start(f32[1,8,1,512]{3,2,1,0:T(1,128)S(1)} %get-tuple-element.38), channel_id=1, source_target_pairs={{4,0},{8,4},{12,8},{16,12},{20,16},{24,20},{28,24},{32,28},{36,32}... | collective-permute-start | bytes 49160 | tf_op jit(solution)/shard_map/ppermute | solution.py:25
  1172.6 10.5 collective-permute-start.54
  1175.6 9.8 collective-permute-start.52
  (36 other events, 496.9 us)
Sparse Core Ops, SparseCore 0:
  100.1 83.4 all-gather.2
  969.7 147.2 all-reduce.2
where the time goes:
time: 1200 us; the launch traced here: 1190 us
  local copies, waits for them, and re-layouts  453 us (38%)
  other arithmetic  352 us (29%)
  waiting for transfers between devices  268 us (22%)
  starting transfers between devices  105 us (9%)
  between operations  15 us (1%)
    gather x1, local copies, waits for them, and re-layouts, local(): jnp.take_along_axis(lax.all_gather(other_surface, 'lat', axis=0, tiled=Tr...  258 us
    gather x1, local copies, waits for them, and re-layouts, local(): outgoing = live_weight * jnp.take(residual_surface, placed)  181 us
    scatter-add x1, other arithmetic, local(): jax.ops.segment_sum(outgoing.reshape(-1), segment_ids.reshape(-1), num_se...  172 us
    scatter-add x1, other arithmetic, local(): jax.ops.segment_sum((live_weight * values).reshape(-1), placed.reshape(-1...  171 us
    unnamed x3, waiting for transfers between devices  146 us
    all_gather x1, waiting for transfers between devices, local(): lax.all_gather(other_surface, 'lat', axis=0, tiled=True)  82 us
    ppermute x18, starting transfers between devices, extended(): lax.ppermute(tail, axis, [(i, (i + 1) % count) for i in range(ends)])  60.7 us
    ppermute x20, starting transfers between devices, partner_2(): return lax.ppermute(value, axis, pairs)  25.8 us
  transfers between devices with their start and end apart: 58, of which 21 were waited for; matrix products, arithmetic and copies ran while one was open for 1% of the time, Pallas kernels for 0%

commit v1 on v0

v1 whole, which is shorter than its diff:
```python
import jax
import jax.numpy as jnp
from jax import lax
from jax.experimental import pallas as pl
from jax.experimental.pallas import tpu as pltpu
from jax.sharding import PartitionSpec as P

NSTEP = 4
HALO = 4
ROWS, COLS, LEV = 16, 512, 8
XR, XC = 24, 640
BANDS = 32
F32, BF16, I32 = jnp.float32, jnp.bfloat16, jnp.int32


def sds(*shape):
    return jax.ShapeDtypeStruct(shape, F32)


def call(kernel, out_shape, name, scratch=(), flops=100000, nbytes=1000000):
    return pl.pallas_call(
        kernel,
        out_shape=out_shape,
        scratch_shapes=list(scratch),
        name=name,
        cost_estimate=pl.CostEstimate(flops=flops, bytes_accessed=nbytes, transcendentals=0),
        compiler_params=pltpu.CompilerParams(vmem_limit_bytes=48 << 20),
    )


def tile_iota(dim):
    return lax.broadcasted_iota(I32, (8, 128), dim)


def up_and_fold():
    ocean = lax.axis_index("comp") == 1
    up = jnp.logical_not(ocean & (lax.axis_index("lon") >= 2))
    return up, ocean & (lax.axis_index("lat") == BANDS - 1)


def wide_iota(width, dim):
    return lax.broadcasted_iota(I32, (8, width), dim)


def put_edges(pairs, fwd_ref, bwd_ref):
    up, fold = up_and_fold()
    low = wide_iota(COLS, 0) < HALO
    sub = tile_iota(0)
    lane = tile_iota(1)
    for p, (head0, tail0, head1, tail1) in enumerate(pairs):
        head = jnp.where(low, head0, pltpu.roll(head1, HALO, 0))
        tail = jnp.where(low, pltpu.roll(tail0, HALO, 0), tail1)
        fwd_ref[p] = jnp.where(up, tail, head)
        bwd_ref[p] = jnp.where(up, head, tail)

        def mirror(ref, tail=tail, p=p):
            for k in range(4):
                x = tail[:, (3 - k) * 128 : (4 - k) * 128]
                x = jnp.where((sub & 1) == 1, pltpu.roll(x, 1, 0), pltpu.roll(x, 7, 0))
                x = jnp.where((sub & 2) == 2, pltpu.roll(x, 2, 0), pltpu.roll(x, 6, 0))
                ref[p, :, k * 128 : (k + 1) * 128] = jnp.take_along_axis(x, 127 - lane, axis=1)

        @pl.when(fold & up)
        def _():
            mirror(fwd_ref)

        @pl.when(fold & jnp.logical_not(up))
        def _():
            mirror(bwd_ref)


def take_edges(count, fwd_ref, bwd_ref):
    up, _ = up_and_fold()
    low = wide_iota(COLS, 0) < HALO
    halos = []
    for p in range((count + 1) // 2):
        a, b = fwd_ref[p], bwd_ref[p]
        north, south = jnp.where(up, b, a), jnp.where(up, a, b)
        halos.append(jnp.where(low, north, pltpu.roll(south, HALO, 0)))
        if 2 * p + 1 < count:
            halos.append(jnp.where(low, pltpu.roll(north, HALO, 0), south))
    return halos


def put_columns(tiles, east_ref, west_ref):
    lane = tile_iota(1)
    for t in range(3):
        east = jnp.zeros((8, 128), F32)
        west = jnp.zeros((8, 128), F32)
        for f, tile in enumerate(tiles):
            here = (lane >= HALO * f) & (lane < HALO * (f + 1))
            x = tile(t)
            first, last = x[:, 0:128], x[:, COLS - 128 : COLS]
            west = jnp.where(here, first if f == 0 else pltpu.roll(first, HALO * f, 1), west)
            east = jnp.where(here, pltpu.roll(last, (HALO * f + HALO) % 128, 1), east)
        east_ref[8 * t : 8 * t + 8, :] = east
        west_ref[8 * t : 8 * t + 8, :] = west


def side_column(f, from_west, from_east):
    lane = lax.broadcasted_iota(I32, (XR, 128), 1)
    east = pltpu.roll(from_east, lax.rem(128 - HALO * f, 128), 1)
    west = pltpu.roll(from_west, lax.rem(124 - HALO * f + 128, 128), 1)
    return jnp.where(lane < HALO, east, jnp.where(lane >= 128 - HALO, west, jnp.zeros_like(east)))


def extend(main, halo, side):
    return jnp.concatenate([jnp.concatenate([main, halo], axis=0), side], axis=1)


def to_east(x):
    return pltpu.roll(x, XC - 1, 1)


def to_west(x):
    return pltpu.roll(x, 1, 1)


def to_north(x):
    return pltpu.roll(x, XR - 1, 0)


def to_south(x):
    return pltpu.roll(x, 1, 0)


def sweep(f, c_east, c_north):
    c_west, c_south = to_west(c_east), to_south(c_north)
    for _ in range(NSTEP):
        change = c_east * (to_east(f) - f) + c_west * (to_west(f) - f)
        change = change + c_south * (to_south(f) - f)
        change = change + c_north * (to_north(f) - f)
        f = f + change
    return f


def first_pack(inc_ref, diff_ref, land_ref, fwd_ref, bwd_ref, mask_ref):
    ocean = lax.axis_index("comp") == 1
    mask = jnp.where(ocean, land_ref[...].astype(F32), jnp.ones((ROWS, COLS), F32))
    mask_ref[...] = mask
    heads = [inc_ref[l, 0:8, :] for l in range(LEV)] + [diff_ref[l, 0:8, :] for l in range(LEV)]
    tails = [inc_ref[l, 8:16, :] for l in range(LEV)] + [diff_ref[l, 8:16, :] for l in range(LEV)]
    heads += [mask[0:8], mask[0:8]]
    tails += [mask[8:16], mask[8:16]]
    pairs = [(heads[2 * p], tails[2 * p], heads[2 * p + 1], tails[2 * p + 1]) for p in range(LEV + 1)]
    put_edges(pairs, fwd_ref, bwd_ref)


def first_columns(inc_ref, diff_ref, mask_ref, fwd_ref, bwd_ref, halo_ref, east_ref, west_ref):
    halos = take_edges(2 * LEV + 1, fwd_ref, bwd_ref)
    for f, halo in enumerate(halos):
        halo_ref[f] = halo

    def field(f):
        def tile(t):
            if t == 2:
                return halo_ref[f]
            rows = slice(8 * t, 8 * t + 8)
            if f < LEV:
                return inc_ref[f, rows, :]
            if f < 2 * LEV:
                return diff_ref[f - LEV, rows, :]
            return mask_ref[rows, :]

        return tile

    put_columns([field(f) for f in range(2 * LEV + 1)], east_ref, west_ref)


def first_sweep(
    inc_ref, diff_ref, mask_ref, halo_ref, from_west_ref, from_east_ref,
    state_ref, ce_ref, cn_ref, surface_ref,
):
    from_west, from_east = from_west_ref[...], from_east_ref[...]
    mask = extend(mask_ref[...], halo_ref[2 * LEV], side_column(2 * LEV, from_west, from_east))
    mask_e = mask * to_east(mask) * 0.5
    mask_n = mask * to_north(mask) * 0.5

    def level(l, carry):
        diff = extend(diff_ref[l], halo_ref[LEV + l], side_column(LEV + l, from_west, from_east))
        c_east = mask_e * (diff + to_east(diff))
        c_north = mask_n * (diff + to_north(diff))
        ce_ref[l] = c_east
        cn_ref[l] = c_north
        f = extend(inc_ref[l], halo_ref[l], side_column(l, from_west, from_east))
        f = sweep(f, c_east, c_north)
        state_ref[l] = f[:ROWS, :COLS]
        return carry

    lax.fori_loop(0, LEV, level, 0)
    surface_ref[...] = mask_ref[...] * state_ref[0]


def gather_slots(table, cells):
    highs = [lax.shift_right_logical(c, 7) for c in cells]
    lows = [c & 127 for c in cells]
    found = [jnp.zeros((8, 128), F32) for _ in cells]
    for h in range(64):
        row = jnp.broadcast_to(table(h), (8, 128))
        for n in range(len(cells)):
            found[n] = jnp.where(highs[n] == h, jnp.take_along_axis(row, lows[n], axis=1), found[n])
    return found


GROUP = 8


def row_of(ref):
    return lambda h: ref[h // 4 : h // 4 + 1, (h % 4) * 128 : (h % 4) * 128 + 128]


def gather_kernel(cells_ref, table_ref, out_ref):
    def group(g, carry):
        found = gather_slots(row_of(table_ref), [cells_ref[g * GROUP + n] for n in range(GROUP)])
        for n in range(GROUP):
            out_ref[g * GROUP + n] = found[n]
        return carry

    lax.fori_loop(0, BANDS // GROUP, group, 0)


def scatter_band(cells, values):
    high_iota = lax.broadcasted_iota(I32, (64, 128), 0)
    low_iota = lax.broadcasted_iota(I32, (128, 128), 0)
    high, low = lax.shift_right_logical(cells, 7), cells & 127
    coarse = values.astype(BF16).astype(F32)
    fine = values - coarse
    left, right = [], []
    for k in range(8):
        at = high_iota == high[k : k + 1]
        a = jnp.where(at, coarse[k : k + 1], 0.0).astype(BF16)
        b = jnp.where(at, fine[k : k + 1], 0.0).astype(BF16)
        left.append(jnp.concatenate([a, b], axis=0))
        right.append(jnp.where(low_iota == low[k : k + 1], 1.0, 0.0).astype(BF16))
    return lax.dot_general(
        jnp.concatenate(left, axis=1),
        jnp.concatenate(right, axis=1),
        (((1,), (1,)), ((), ())),
        preferred_element_type=F32,
    )


def as_block(sums):
    return jnp.concatenate([sums.reshape(ROWS, 4, 128)[:, k, :] for k in range(4)], axis=1)


def sum_slots(cells_of, values_of, acc_ref):
    acc_ref[...] = jnp.zeros_like(acc_ref)

    def pair(b, carry):
        acc_ref[...] += scatter_band(cells_of(2 * b), values_of(2 * b)) + scatter_band(
            cells_of(2 * b + 1), values_of(2 * b + 1)
        )
        return carry

    lax.fori_loop(0, BANDS // 2, pair, 0)
    return as_block(acc_ref[0:64, :] + acc_ref[64:128, :])


def live_of(b, weight_ref, count_ref):
    slot = tile_iota(0) * 128 + tile_iota(1)
    return jnp.where(slot < count_ref[0, b], weight_ref[b], jnp.zeros((8, 128), F32))


def couple_kernel(
    count_ref, values_ref, cells_ref, weight_ref, mask_ref, state_ref, innov_ref,
    linear_ref, residual_ref, out_ref, acc_ref, table_ref,
):
    income = sum_slots(
        lambda b: cells_ref[b], lambda b: live_of(b, weight_ref, count_ref) * values_ref[b], acc_ref
    )
    mask = mask_ref[...]
    linear = state_ref[...] + mask * income
    residual = linear - innov_ref[...]
    linear_ref[...] = linear
    residual_ref[...] = residual
    table_ref[...] = mask * residual

    def group(g, carry):
        found = gather_slots(row_of(table_ref), [cells_ref[g * GROUP + n] for n in range(GROUP)])
        for n in range(GROUP):
            out_ref[g * GROUP + n] = live_of(g * GROUP + n, weight_ref, count_ref) * found[n]
        return carry

    lax.fori_loop(0, BANDS // GROUP, group, 0)


def collect_kernel(values_ref, cells_ref, out_ref, acc_ref):
    out_ref[...] = sum_slots(lambda b: cells_ref[b], lambda b: values_ref[b], acc_ref)


def second_pack(residual_ref, mask_ref, returned_ref, state_ref, innov_ref, adj_ref, fwd_ref, bwd_ref):
    adj_ref[0] = residual_ref[...] + mask_ref[...] * returned_ref[...]
    for l in range(1, LEV):
        adj_ref[l] = state_ref[l] - innov_ref[l]
    pairs = []
    for p in range(LEV // 2):
        a, b = 2 * p, 2 * p + 1
        pairs.append((adj_ref[a, 0:8], adj_ref[a, 8:16], adj_ref[b, 0:8], adj_ref[b, 8:16]))
    put_edges(pairs, fwd_ref, bwd_ref)


def second_columns(adj_ref, fwd_ref, bwd_ref, halo_ref, east_ref, west_ref):
    halos = take_edges(LEV, fwd_ref, bwd_ref)
    for f, halo in enumerate(halos):
        halo_ref[f] = halo

    def field(f):
        return lambda t: halo_ref[f] if t == 2 else adj_ref[f, 8 * t : 8 * t + 8, :]

    put_columns([field(f) for f in range(LEV)], east_ref, west_ref)


def second_sweep(adj_ref, halo_ref, from_west_ref, from_east_ref, ce_ref, cn_ref, inc_ref, out_ref):
    from_west, from_east = from_west_ref[...], from_east_ref[...]

    def level(l, carry):
        f = extend(adj_ref[l], halo_ref[l], side_column(l, from_west, from_east))
        f = sweep(f, ce_ref[l], cn_ref[l])
        out_ref[l] = f[:ROWS, :COLS] + inc_ref[l]
        return carry

    lax.fori_loop(0, LEV, level, 0)


def chain_pairs():
    lons = lax.axis_size("lon")

    def at(comp, lat, lon):
        return (comp * BANDS + lat) * lons + lon

    pairs = []
    for lon in range(lons):
        for lat in range(BANDS - 1):
            pairs.append((at(0, lat, lon), at(0, lat + 1, lon)))
            if lon < lons // 2:
                pairs.append((at(1, lat, lon), at(1, lat + 1, lon)))
            else:
                pairs.append((at(1, lat + 1, lon), at(1, lat, lon)))
        if lon < lons // 2:
            pairs.append((at(1, BANDS - 1, lon), at(1, BANDS - 1, lons - 1 - lon)))
    return pairs


def across(value):
    return lax.ppermute(value, "comp", [(0, 1), (1, 0)])


def along_chain(fwd, bwd):
    axes = ("comp", "lat", "lon")
    pairs = chain_pairs()
    return (
        lax.ppermute(fwd, axes, pairs),
        lax.ppermute(bwd, axes, [(b, a) for a, b in pairs]),
    )


def around(east, west):
    n = lax.axis_size("lon")
    return (
        lax.ppermute(east, "lon", [(i, (i + 1) % n) for i in range(n)]),
        lax.ppermute(west, "lon", [((i + 1) % n, i) for i in range(n)]),
    )


def exchange(slots):
    return lax.all_to_all(slots, "lat", 0, 0, tiled=True)


def local(
    increment, diffusivity, innovation, land_mask, pull_cells, put_cells, pull_weight, pull_count
):
    inc, diff, innov = increment[0], diffusivity[0], innovation[0]
    pulled = exchange(pull_cells.reshape(BANDS, 8, 128))
    placed = put_cells.reshape(BANDS, 8, 128)
    weight = pull_weight.reshape(BANDS, 8, 128)
    count = pull_count.reshape(1, BANDS)

    edge = sds(LEV + 1, 8, COLS)
    fwd, bwd, mask = call(first_pack, (edge, edge, sds(ROWS, COLS)), "first_pack")(
        inc, diff, land_mask
    )
    fwd, bwd = along_chain(fwd, bwd)
    halo, east, west = call(
        first_columns, (sds(2 * LEV + 1, 8, COLS), sds(XR, 128), sds(XR, 128)), "first_columns"
    )(inc, diff, mask, fwd, bwd)
    from_west, from_east = around(east, west)
    state, c_east, c_north, surface = call(
        first_sweep,
        (sds(LEV, ROWS, COLS), sds(LEV, XR, XC), sds(LEV, XR, XC), sds(ROWS, COLS)),
        "first_sweep",
    )(inc, diff, mask, halo, from_west, from_east)

    slots = sds(BANDS, 8, 128)
    values = exchange(call(gather_kernel, slots, "gather_slots")(pulled, across(surface)))
    acc = pltpu.VMEM((128, 128), F32)
    plane = sds(ROWS, COLS)
    smem = pl.BlockSpec(memory_space=pltpu.SMEM)
    vmem = pl.BlockSpec(memory_space=pltpu.VMEM)
    linear, residual, outgoing = pl.pallas_call(
        couple_kernel,
        out_shape=(plane, plane, slots),
        in_specs=[smem] + [vmem] * 6,
        out_specs=(vmem,) * 3,
        scratch_shapes=[acc, pltpu.VMEM((ROWS, COLS), F32)],
        name="couple",
        compiler_params=pltpu.CompilerParams(vmem_limit_bytes=48 << 20),
    )(count, values, placed, weight, mask, state[0], innov[0])
    returned = across(
        call(collect_kernel, plane, "collect", [acc])(exchange(outgoing), pulled)
    )

    edge = sds(LEV // 2, 8, COLS)
    adj, fwd, bwd = call(second_pack, (sds(LEV, ROWS, COLS), edge, edge), "second_pack")(
        residual, mask, returned, state, innov
    )
    fwd, bwd = along_chain(fwd, bwd)
    halo, east, west = call(
        second_columns, (sds(LEV, 8, COLS), sds(XR, 128), sds(XR, 128)), "second_columns"
    )(adj, fwd, bwd)
    from_west, from_east = around(east, west)
    gradient = call(second_sweep, sds(LEV, ROWS, COLS), "second_sweep")(
        adj, halo, from_west, from_east, c_east, c_north, inc
    )
    linear_state = jnp.concatenate([linear[None], state[1:]], axis=0)
    return (linear_state[None], gradient[None])


def solution(mesh):
    placed = (
        P("comp", None, "lat", "lon"),
        P("comp", None, "lat", "lon"),
        P("comp", None, "lat", "lon"),
        P("lat", "lon"),
        P("comp", "lat", "lon", None, None),
        P("comp", "lat", "lon", None, None),
        P("comp", "lat", "lon", None, None),
        P("comp", "lat", "lon", None),
    )
    return jax.shard_map(
        local,
        mesh=mesh,
        in_specs=placed,
        out_specs=(P("comp", None, "lat", "lon"), P("comp", None, "lat", "lon")),
        check_vma=False,
    )
```

time: 1200 us -> 116 us (0.10)
  local copies, waits for them, and re-layouts: 453 us -> 4.01 us
  other arithmetic: 352 us -> 0.73 us
  waiting for transfers between devices: 268 us -> 28.4 us
  starting transfers between devices: 105 us -> 35.1 us
  Pallas kernels: 0 us -> 32.1 us
  between operations: 15 us -> 0.86 us
  blocking collectives: 0 us -> 13.9 us
    gather x2 -> x0, local copies, waits for them, and re-layouts: 439 us -> none  [the longest x1 258 us: local(): jnp.take_along_axis(lax.all_gather(other_surface, 'lat', axis=0, tiled=Tr...]
    scatter-add x4 -> x0, other arithmetic: 343 us -> none  [the longest x1 172 us: local(): jax.ops.segment_sum(outgoing.reshape(-1), segment_ids.reshape(-1), num_se...]
    unnamed x3 -> x0, waiting for transfers between devices: 146 us -> none
    ppermute x56 -> x10, starting transfers between devices: 105 us -> 13.7 us  [the longest x2 6.75 us: along_chain(): lax.ppermute(fwd, axes, pairs)]
    all_gather x1 -> x0, waiting for transfers between devices: 82 us -> none  [local(): lax.all_gather(other_surface, 'lat', axis=0, tiled=True)]
    pallas_call x0 -> x9, Pallas kernels: none -> 32.1 us  [the longest x1 11.7 us: local(): pl.pallas_call(couple_kernel, out_shape=(plane, plane, slots), in_specs=[...]
    all_to_all x0 -> x2, starting transfers between devices: none -> 21.4 us  [exchange(): return lax.all_to_all(slots, 'lat', 0, 0, tiled=True)]
    ppermute x56 -> x10, waiting for transfers between devices: 39.8 us -> 18.7 us  [the longest x2 7.48 us: along_chain(): lax.ppermute(bwd, axes, [(b, a) for a, b in pairs])]
  transfers between devices with their start and end apart: 58 -> 12, of which waited for: 21 -> 11; matrix products, arithmetic and copies ran while one was open for 1% -> 1% of each run, Pallas kernels for 0% -> 4%
where the time goes in v1:
time: 116 us; the launch traced here: 115 us
  starting transfers between devices  35.1 us (30%)
  Pallas kernels  32.1 us (28%)
  waiting for transfers between devices  28.4 us (24%)
  blocking collectives  13.9 us (12%)
  local copies, waits for them, and re-layouts  4.01 us (3%)
    all_to_all x2, starting transfers between devices, exchange(): return lax.all_to_all(slots, 'lat', 0, 0, tiled=True)  21.4 us
    all_to_all x1, blocking collectives, exchange(): return lax.all_to_all(slots, 'lat', 0, 0, tiled=True)  13.9 us
    pallas_call x1, Pallas kernels, local(): pl.pallas_call(couple_kernel, out_shape=(plane, plane, slots), in_specs=[...  11.7 us
    all_to_all x2, waiting for transfers between devices, exchange(): return lax.all_to_all(slots, 'lat', 0, 0, tiled=True)  9.65 us
    ppermute x2, waiting for transfers between devices, along_chain(): lax.ppermute(bwd, axes, [(b, a) for a, b in pairs])  7.48 us
    ppermute x2, starting transfers between devices, along_chain(): lax.ppermute(fwd, axes, pairs)  6.75 us
    pallas_call x1, Pallas kernels, local(): call(gather_kernel, slots, 'gather_slots')(pulled, across(surface))  6.69 us
    pallas_call x1, Pallas kernels, local(): call(collect_kernel, plane, 'collect', [acc])(exchange(outgoing), pulled)  5.08 us
  transfers between devices with their start and end apart: 12, of which 11 were waited for; matrix products, arithmetic and copies ran while one was open for 1% of the time, Pallas kernels for 4%

profile of v1, /device:TPU:6, one launch (start us, length us, event | category | flops | bytes accessed | tf_op | source)
XLA Modules:
  0.0 115.2 jit_solution(2301745910477959586)
XLA Ops:
  0.6 1.6 %copy.10 = s32[4,8,8,128]{3,2,1,0:T(8,128)} copy(s32[4,8,8,128]{3,1,2,0:T(8,128)} %bitcast.37) | data formatting | bytes 262144
  2.3 11.5 %all-to-all-start = ((s32[32,8,128]{2,1,0:T(8,128)}), s32[32,8,128]{2,1,0:T(8,128)S(1)}, u32[]{:S(2)}, u32[]{:S(2)}) async-start(s32[32,8,128]{2,1,0:T(8,128)} %bitcast.12), calls=%async_computation | async-start | bytes 262144 | tf_op jit(solution)/shard_map/all_to_all | solution.py:367
  13.8 0.7 copy-done.3
  14.7 3.7 %collective-permute-start = (f32[9,8,512]{2,1,0:T(8,128)S(1)}, f32[9,8,512]{2,1,0:T(8,128)S(1)}, u32[]{:S(2)}, u32[]{:S(2)}) collective-permute-start(f32[9,8,512]{2,1,0:T(8,128)S(1)} %get-tuple-element.22), channel_id=1, source_target_pairs={{0,4},{128,132},{4,8},{132,136},{8,12},{136,140},{12,16},{140,144}... | collective-permute-start | bytes 442376 | tf_op jit(solution)/shard_map/ppermute | solution.py:353
  18.4 1.3 %collective-permute-start.1 = (f32[9,8,512]{2,1,0:T(8,128)S(1)}, f32[9,8,512]{2,1,0:T(8,128)S(1)}, u32[]{:S(2)}, u32[]{:S(2)}) collective-permute-start(f32[9,8,512]{2,1,0:T(8,128)S(1)} %get-tuple-element.23), channel_id=1, source_target_pairs={{4,0},{132,128},{8,4},{136,132},{12,8},{140,136},{16,12},{144,140}... | collective-permute-start | bytes 442376 | tf_op jit(solution)/shard_map/ppermute | solution.py:354
  19.7 2.5 %collective-permute-done.fwd_ref = f32[9,8,512]{2,1,0:T(8,128)S(1)} collective-permute-done((f32[9,8,512]{2,1,0:T(8,128)S(1)}, f32[9,8,512]{2,1,0:T(8,128)S(1)}, u32[]{:S(2)}, u32[]{:S(2)}) %collective-permute-start) | collective-permute-done | bytes 147488 | tf_op jit(solution)/shard_map/ppermute | solution.py:353
  22.2 3.2 %collective-permute-done.1.bwd_ref = f32[9,8,512]{2,1,0:T(8,128)S(1)} collective-permute-done((f32[9,8,512]{2,1,0:T(8,128)S(1)}, f32[9,8,512]{2,1,0:T(8,128)S(1)}, u32[]{:S(2)}, u32[]{:S(2)}) %collective-permute-start.1) | collective-permute-done | bytes 147488 | tf_op jit(solution)/shard_map/ppermute | solution.py:354
  25.6 0.6 collective-permute-start.2
  26.2 1.5 %collective-permute-start.3 = (f32[24,128]{1,0:T(8,128)S(1)}, f32[24,128]{1,0:T(8,128)S(1)}, u32[]{:S(2)}, u32[]{:S(2)}) collective-permute-start(f32[24,128]{1,0:T(8,128)S(1)} %get-tuple-element.26), channel_id=1, source_target_pairs={{1,0},{2,1},{3,2},{0,3},{5,4},{6,5},{7,6},{4,7},{9,8},{10,9},{11,1... | collective-permute-start | bytes 36872 | tf_op jit(solution)/shard_map/ppermute | solution.py:362
  27.7 1.7 %collective-permute-done.2.from_west_ref = f32[24,128]{1,0:T(8,128)S(1)} collective-permute-done((f32[24,128]{1,0:T(8,128)S(1)}, f32[24,128]{1,0:T(8,128)S(1)}, u32[]{:S(2)}, u32[]{:S(2)}) %collective-permute-start.2) | collective-permute-done | bytes 12320 | tf_op jit(solution)/shard_map/ppermute | solution.py:361
  29.4 1.7 %collective-permute-done.3.from_east_ref = f32[24,128]{1,0:T(8,128)S(1)} collective-permute-done((f32[24,128]{1,0:T(8,128)S(1)}, f32[24,128]{1,0:T(8,128)S(1)}, u32[]{:S(2)}, u32[]{:S(2)}) %collective-permute-start.3) | collective-permute-done | bytes 12320 | tf_op jit(solution)/shard_map/ppermute | solution.py:362
  31.1 4.1 %first_sweep.1 = (f32[8,16,512]{2,1,0:T(8,128)S(1)}, f32[8,24,640]{2,1,0:T(8,128)S(1)}, f32[8,24,640]{2,1,0:T(8,128)S(1)}, f32[16,512]{1,0:T(8,128)S(1)}) custom-call(f32[8,16,512]{2,1,0:T(8,128)S(1)} %bitcast.26, f32[8,16,512]{2,1,0:T(8,128)S(1)} %bitcast.30, f32[16,512]{1,0:T(8,128)S(1)} %get-tuple-element.21.mask_ref, ...), custom_call_target="tpu_custom_call" | custom-call | flops 100000 | bytes 1000000 | tf_op jit(solution)/shard_map/first_sweep/pallas_call | solution.py:388
  35.3 1.2 %collective-permute-done.4.table_ref = f32[16,512]{1,0:T(8,128)S(1)} collective-permute-done((f32[16,512]{1,0:T(8,128)S(1)}, f32[16,512]{1,0:T(8,128)S(1)}, u32[]{:S(2)}, u32[]{:S(2)}) %collective-permute-start.4) | collective-permute-done | bytes 32800 | tf_op jit(solution)/shard_map/ppermute | solution.py:346
  36.5 6.7 %gather_slots.1 = f32[32,8,128]{2,1,0:T(8,128)} custom-call(s32[32,8,128]{2,1,0:T(8,128)S(1)} %all-to-all-done.cells_ref, f32[16,512]{1,0:T(8,128)S(1)} %collective-permute-done.4.table_ref), custom_call_target="tpu_custom_call" | custom-call | flops 100000 | bytes 1000000 | tf_op jit(solution)/shard_map/gather_slots/pallas_call | solution.py:395
  43.2 9.9 %all-to-all-start.1 = ((f32[32,8,128]{2,1,0:T(8,128)}), f32[32,8,128]{2,1,0:T(8,128)S(1)}, u32[]{:S(2)}, u32[]{:S(2)}) async-start(f32[32,8,128]{2,1,0:T(8,128)} %gather_slots.1), calls=%async_computation.1 | async-start | bytes 262144 | tf_op jit(solution)/shard_map/all_to_all | solution.py:367
  53.2 0.9 copy-done.6
  54.1 9.6 %all-to-all-done.1.values_ref = f32[32,8,128]{2,1,0:T(8,128)S(1)} async-done(((f32[32,8,128]{2,1,0:T(8,128)}), f32[32,8,128]{2,1,0:T(8,128)S(1)}, u32[]{:S(2)}, u32[]{:S(2)}) %all-to-all-start.1) | async-done | bytes 131104 | tf_op jit(solution)/shard_map/all_to_all | solution.py:367
  63.7 0.7 copy-done.4
  64.4 11.7 %couple.1 = (f32[16,512]{1,0:T(8,128)S(1)}, f32[16,512]{1,0:T(8,128)S(1)}, f32[32,8,128]{2,1,0:T(8,128)S(1)}) custom-call(s32[1,32]{1,0:T(1,128)S(1)} %bitcast.35, f32[32,8,128]{2,1,0:T(8,128)S(1)} %all-to-all-done.1.values_ref, s32[32,8,128]{2,1,0:T(8,128)S(1)} %bitcast.31, f32[32,8,128]{2,1,0:T(8,128)S(1)} %bitcast.32, ...), custom_call_target="tpu_custom_call" | custom-call | tf_op jit(solution)/shard_map/couple/pallas_call | solution.py:400
  76.0 13.9 %all_to_all.15.values_ref = f32[32,8,128]{2,1,0:T(8,128)S(1)} all-to-all(f32[32,8,128]{2,1,0:T(8,128)S(1)} %get-tuple-element.31), channel_id=1, replica_groups=mesh['comp'=2,'lat'=32,'lon'=4] {'lat'}, dimensions={0} | all-to-all | bytes 262144 | tf_op jit(solution)/shard_map/all_to_all | solution.py:367
  90.0 5.1 %collect.1 = f32[16,512]{1,0:T(8,128)S(1)} custom-call(f32[32,8,128]{2,1,0:T(8,128)S(1)} %all_to_all.15.values_ref, s32[32,8,128]{2,1,0:T(8,128)S(1)} %all-to-all-done.cells_ref), custom_call_target="tpu_custom_call" | custom-call | flops 100000 | bytes 1000000 | tf_op jit(solution)/shard_map/collect/pallas_call | solution.py:410
  95.2 1.2 %collective-permute-done.5.returned_ref = f32[16,512]{1,0:T(8,128)S(1)} collective-permute-done((f32[16,512]{1,0:T(8,128)S(1)}, f32[16,512]{1,0:T(8,128)S(1)}, u32[]{:S(2)}, u32[]{:S(2)}) %collective-permute-start.5) | collective-permute-done | bytes 32800 | tf_op jit(solution)/shard_map/ppermute | solution.py:346
  96.4 3.0 %collective-permute-start.6 = (f32[4,8,512]{2,1,0:T(8,128)S(1)}, f32[4,8,512]{2,1,0:T(8,128)S(1)}, u32[]{:S(2)}, u32[]{:S(2)}) collective-permute-start(f32[4,8,512]{2,1,0:T(8,128)S(1)} %get-tuple-element.33), channel_id=1, source_target_pairs={{0,4},{128,132},{4,8},{132,136},{8,12},{136,140},{12,16},{140,144}... | collective-permute-start | bytes 196616 | tf_op jit(solution)/shard_map/ppermute | solution.py:353
  99.5 1.3 %collective-permute-start.7 = (f32[4,8,512]{2,1,0:T(8,128)S(1)}, f32[4,8,512]{2,1,0:T(8,128)S(1)}, u32[]{:S(2)}, u32[]{:S(2)}) collective-permute-start(f32[4,8,512]{2,1,0:T(8,128)S(1)} %get-tuple-element.34), channel_id=1, source_target_pairs={{4,0},{132,128},{8,4},{136,132},{12,8},{140,136},{16,12},{144,140}... | collective-permute-start | bytes 196616 | tf_op jit(solution)/shard_map/ppermute | solution.py:354
  100.8 0.6 collective-permute-done.6.fwd_ref
  101.4 4.3 %collective-permute-done.7.bwd_ref = f32[4,8,512]{2,1,0:T(8,128)S(1)} collective-permute-done((f32[4,8,512]{2,1,0:T(8,128)S(1)}, f32[4,8,512]{2,1,0:T(8,128)S(1)}, u32[]{:S(2)}, u32[]{:S(2)}) %collective-permute-start.7) | collective-permute-done | bytes 65568 | tf_op jit(solution)/shard_map/ppermute | solution.py:354
  105.8 0.4 collective-permute-start.8
  106.1 1.8 %collective-permute-start.9 = (f32[24,128]{1,0:T(8,128)S(1)}, f32[24,128]{1,0:T(8,128)S(1)}, u32[]{:S(2)}, u32[]{:S(2)}) collective-permute-start(f32[24,128]{1,0:T(8,128)S(1)} %get-tuple-element.37), channel_id=1, source_target_pairs={{1,0},{2,1},{3,2},{0,3},{5,4},{6,5},{7,6},{4,7},{9,8},{10,9},{11,1... | collective-permute-start | bytes 36872 | tf_op jit(solution)/shard_map/ppermute | solution.py:362
  107.9 0.7 maximum_bitcast_fusion
  108.6 0.9 collective-permute-done.8.from_west_ref
  109.6 1.5 %collective-permute-done.9.from_east_ref = f32[24,128]{1,0:T(8,128)S(1)} collective-permute-done((f32[24,128]{1,0:T(8,128)S(1)}, f32[24,128]{1,0:T(8,128)S(1)}, u32[]{:S(2)}, u32[]{:S(2)}) %collective-permute-start.9) | collective-permute-done | bytes 12320 | tf_op jit(solution)/shard_map/ppermute | solution.py:362
  111.0 4.1 %second_sweep.1 = f32[8,16,512]{2,1,0:T(8,128)} custom-call(f32[8,16,512]{2,1,0:T(8,128)S(1)} %get-tuple-element.32.adj_ref, f32[8,8,512]{2,1,0:T(8,128)S(1)} %get-tuple-element.35.halo_ref, f32[24,128]{1,0:T(8,128)S(1)} %collective-permute-done.8.from_west_ref, f32[24,128]{1,0:T(8,128)S(1)} %collective-permute-done.9.from_east_ref, ...), custom_call_target="tpu_custom_call" | custom-call | flops 100000 | bytes 1000000 | tf_op jit(solution)/shard_map/second_sweep/pallas_call | solution.py:422
  (23 shorter events, 0.7 us)
Async XLA Ops:
  0.6 13.2 %copy-start = (f32[1,8,16,512]{3,2,1,0:T(8,128)S(1)}, f32[1,8,16,512]{3,2,1,0:T(8,128)}, u32[]{:S(2)}) copy-start(f32[1,8,16,512]{3,2,1,0:T(8,128)} %param.8) | copy-start | bytes 786436
  0.6 13.2 %copy-start.1 = (f32[1,8,16,512]{3,2,1,0:T(8,128)S(1)}, f32[1,8,16,512]{3,2,1,0:T(8,128)}, u32[]{:S(2)}) copy-start(f32[1,8,16,512]{3,2,1,0:T(8,128)} %param.9) | copy-start | bytes 786436
  2.3 34.2 %all-to-all-start = ((s32[32,8,128]{2,1,0:T(8,128)}), s32[32,8,128]{2,1,0:T(8,128)S(1)}, u32[]{:S(2)}, u32[]{:S(2)}) async-start(s32[32,8,128]{2,1,0:T(8,128)} %bitcast.12), calls=%async_computation | async-start | bytes 262144 | tf_op jit(solution)/shard_map/all_to_all | solution.py:367
  13.8 0.8 copy-start.3
  14.7 7.5 %collective-permute-start = (f32[9,8,512]{2,1,0:T(8,128)S(1)}, f32[9,8,512]{2,1,0:T(8,128)S(1)}, u32[]{:S(2)}, u32[]{:S(2)}) collective-permute-start(f32[9,8,512]{2,1,0:T(8,128)S(1)} %get-tuple-element.22), channel_id=1, source_target_pairs={{0,4},{128,132},{4,8},{132,136},{8,12},{136,140},{12,16},{140,144}... | collective-permute-start | bytes 442376 | tf_op jit(solution)/shard_map/ppermute | solution.py:353
  18.4 7.0 %collective-permute-start.1 = (f32[9,8,512]{2,1,0:T(8,128)S(1)}, f32[9,8,512]{2,1,0:T(8,128)S(1)}, u32[]{:S(2)}, u32[]{:S(2)}) collective-permute-start(f32[9,8,512]{2,1,0:T(8,128)S(1)} %get-tuple-element.23), channel_id=1, source_target_pairs={{4,0},{132,128},{8,4},{136,132},{12,8},{140,136},{16,12},{144,140}... | collective-permute-start | bytes 442376 | tf_op jit(solution)/shard_map/ppermute | solution.py:354
  25.6 3.8 %collective-permute-start.2 = (f32[24,128]{1,0:T(8,128)S(1)}, f32[24,128]{1,0:T(8,128)S(1)}, u32[]{:S(2)}, u32[]{:S(2)}) collective-permute-start(f32[24,128]{1,0:T(8,128)S(1)} %get-tuple-element.25), channel_id=1, source_target_pairs={{0,1},{1,2},{2,3},{3,0},{4,5},{5,6},{6,7},{7,4},{8,9},{9,10},{10,1... | collective-permute-start | bytes 36872 | tf_op jit(solution)/shard_map/ppermute | solution.py:361
  26.2 4.9 %collective-permute-start.3 = (f32[24,128]{1,0:T(8,128)S(1)}, f32[24,128]{1,0:T(8,128)S(1)}, u32[]{:S(2)}, u32[]{:S(2)}) collective-permute-start(f32[24,128]{1,0:T(8,128)S(1)} %get-tuple-element.26), channel_id=1, source_target_pairs={{1,0},{2,1},{3,2},{0,3},{5,4},{6,5},{7,6},{4,7},{9,8},{10,9},{11,1... | collective-permute-start | bytes 36872 | tf_op jit(solution)/shard_map/ppermute | solution.py:362
  35.2 17.9 %copy-start.2 = (f32[1,8,16,512]{3,2,1,0:T(8,128)S(1)}, f32[1,8,16,512]{3,2,1,0:T(8,128)}, u32[]{:S(2)}) copy-start(f32[1,8,16,512]{3,2,1,0:T(8,128)} %param.10) | copy-start | bytes 786436
  35.2 1.3 %collective-permute-start.4 = (f32[16,512]{1,0:T(8,128)S(1)}, f32[16,512]{1,0:T(8,128)S(1)}, u32[]{:S(2)}, u32[]{:S(2)}) collective-permute-start(f32[16,512]{1,0:T(8,128)S(1)} %get-tuple-element.27), channel_id=1, source_target_pairs={{0,128},{128,0},{1,129},{129,1},{2,130},{130,2},{3,131},{131,3},{4... | collective-permute-start | bytes 98312 | tf_op jit(solution)/shard_map/ppermute | solution.py:346
  43.2 9.9 %copy-start.5 = (s32[1,1,1,32,1024]{4,3,2,1,0:T(8,128)S(1)}, s32[1,1,1,32,1024]{4,3,2,1,0:T(8,128)}, u32[]{:S(2)}) copy-start(s32[1,1,1,32,1024]{4,3,2,1,0:T(8,128)} %param.13) | copy-start | bytes 393220
  43.2 20.5 %all-to-all-start.1 = ((f32[32,8,128]{2,1,0:T(8,128)}), f32[32,8,128]{2,1,0:T(8,128)S(1)}, u32[]{:S(2)}, u32[]{:S(2)}) async-start(f32[32,8,128]{2,1,0:T(8,128)} %gather_slots.1), calls=%async_computation.1 | async-start | bytes 262144 | tf_op jit(solution)/shard_map/all_to_all | solution.py:367
  53.1 0.9 copy-start.6
  63.7 0.7 copy-start.4
  95.1 1.3 %collective-permute-start.5 = (f32[16,512]{1,0:T(8,128)S(1)}, f32[16,512]{1,0:T(8,128)S(1)}, u32[]{:S(2)}, u32[]{:S(2)}) collective-permute-start(f32[16,512]{1,0:T(8,128)S(1)} %collect.1), channel_id=1, source_target_pairs={{0,128},{128,0},{1,129},{129,1},{2,130},{130,2},{3,131},{131,3},{4... | collective-permute-start | bytes 98312 | tf_op jit(solution)/shard_map/ppermute | solution.py:346
  96.4 4.9 %collective-permute-start.6 = (f32[4,8,512]{2,1,0:T(8,128)S(1)}, f32[4,8,512]{2,1,0:T(8,128)S(1)}, u32[]{:S(2)}, u32[]{:S(2)}) collective-permute-start(f32[4,8,512]{2,1,0:T(8,128)S(1)} %get-tuple-element.33), channel_id=1, source_target_pairs={{0,4},{128,132},{4,8},{132,136},{8,12},{136,140},{12,16},{140,144}... | collective-permute-start | bytes 196616 | tf_op jit(solution)/shard_map/ppermute | solution.py:353
  99.5 6.2 %collective-permute-start.7 = (f32[4,8,512]{2,1,0:T(8,128)S(1)}, f32[4,8,512]{2,1,0:T(8,128)S(1)}, u32[]{:S(2)}, u32[]{:S(2)}) collective-permute-start(f32[4,8,512]{2,1,0:T(8,128)S(1)} %get-tuple-element.34), channel_id=1, source_target_pairs={{4,0},{132,128},{8,4},{136,132},{12,8},{140,136},{16,12},{144,140}... | collective-permute-start | bytes 196616 | tf_op jit(solution)/shard_map/ppermute | solution.py:354
  105.8 3.8 %collective-permute-start.8 = (f32[24,128]{1,0:T(8,128)S(1)}, f32[24,128]{1,0:T(8,128)S(1)}, u32[]{:S(2)}, u32[]{:S(2)}) collective-permute-start(f32[24,128]{1,0:T(8,128)S(1)} %get-tuple-element.36), channel_id=1, source_target_pairs={{0,1},{1,2},{2,3},{3,0},{4,5},{5,6},{6,7},{7,4},{8,9},{9,10},{10,1... | collective-permute-start | bytes 36872 | tf_op jit(solution)/shard_map/ppermute | solution.py:361
  106.1 4.9 %collective-permute-start.9 = (f32[24,128]{1,0:T(8,128)S(1)}, f32[24,128]{1,0:T(8,128)S(1)}, u32[]{:S(2)}, u32[]{:S(2)}) collective-permute-start(f32[24,128]{1,0:T(8,128)S(1)} %get-tuple-element.37), channel_id=1, source_target_pairs={{1,0},{2,1},{3,2},{0,3},{5,4},{6,5},{7,6},{4,7},{9,8},{10,9},{11,1... | collective-permute-start | bytes 36872 | tf_op jit(solution)/shard_map/ppermute | solution.py:362

commit v2 on v1

v2 whole, which is shorter than its diff:
```python
import jax
import jax.numpy as jnp
from jax import lax
from jax.experimental import pallas as pl
from jax.experimental.pallas import tpu as pltpu
from jax.sharding import PartitionSpec as P

NSTEP = 4
HALO = 4
ROWS, COLS, LEV = 16, 512, 8
XR, XC = 24, 640
BANDS = 32
F32, BF16, I32 = jnp.float32, jnp.bfloat16, jnp.int32


def sds(*shape):
    return jax.ShapeDtypeStruct(shape, F32)


def call(kernel, out_shape, name, scratch=(), flops=100000, nbytes=1000000):
    return pl.pallas_call(
        kernel,
        out_shape=out_shape,
        scratch_shapes=list(scratch),
        name=name,
        cost_estimate=pl.CostEstimate(flops=flops, bytes_accessed=nbytes, transcendentals=0),
        compiler_params=pltpu.CompilerParams(vmem_limit_bytes=48 << 20),
    )


def tile_iota(dim):
    return lax.broadcasted_iota(I32, (8, 128), dim)


def wide_iota(width, dim):
    return lax.broadcasted_iota(I32, (8, width), dim)


def put_edges(pairs, head_ref, tail_ref, mirror_ref):
    fold = (lax.axis_index("comp") == 1) & (lax.axis_index("lat") == BANDS - 1)
    low = wide_iota(COLS, 0) < HALO
    sub = tile_iota(0)
    lane = tile_iota(1)
    for p, (head0, tail0, head1, tail1) in enumerate(pairs):
        head_ref[p] = jnp.where(low, head0, pltpu.roll(head1, HALO, 0))
        tail = jnp.where(low, pltpu.roll(tail0, HALO, 0), tail1)
        tail_ref[p] = tail
        mirror_ref[p] = tail

    @pl.when(fold)
    def _():
        for p in range(len(pairs)):
            for k in range(4):
                x = tail_ref[p, :, (3 - k) * 128 : (4 - k) * 128]
                x = jnp.where((sub & 1) == 1, pltpu.roll(x, 1, 0), pltpu.roll(x, 7, 0))
                x = jnp.where((sub & 2) == 2, pltpu.roll(x, 2, 0), pltpu.roll(x, 6, 0))
                mirror_ref[p, :, k * 128 : (k + 1) * 128] = jnp.take_along_axis(
                    x, 127 - lane, axis=1
                )


def take_edges(count, from_south_ref, from_north_ref, from_fold_ref):
    ocean = lax.axis_index("comp") == 1
    band = lax.axis_index("lat")
    first, last = band == 0, band == BANDS - 1
    zero = jnp.zeros((8, COLS), F32)
    low = wide_iota(COLS, 0) < HALO
    halos = []
    for p in range((count + 1) // 2):
        north = jnp.where(last, jnp.where(ocean, from_fold_ref[p], zero), from_north_ref[p])
        south = jnp.where(first, zero, from_south_ref[p])
        halos.append(jnp.where(low, north, pltpu.roll(south, HALO, 0)))
        if 2 * p + 1 < count:
            halos.append(jnp.where(low, pltpu.roll(north, HALO, 0), south))
    return halos


def put_columns(tiles, east_ref, west_ref):
    lane = tile_iota(1)
    for t in range(3):
        east = jnp.zeros((8, 128), F32)
        west = jnp.zeros((8, 128), F32)
        for f, tile in enumerate(tiles):
            here = (lane >= HALO * f) & (lane < HALO * (f + 1))
            x = tile(t)
            first, last = x[:, 0:128], x[:, COLS - 128 : COLS]
            west = jnp.where(here, first if f == 0 else pltpu.roll(first, HALO * f, 1), west)
            east = jnp.where(here, pltpu.roll(last, (HALO * f + HALO) % 128, 1), east)
        east_ref[8 * t : 8 * t + 8, :] = east
        west_ref[8 * t : 8 * t + 8, :] = west


def side_column(f, from_west, from_east):
    lane = lax.broadcasted_iota(I32, (XR, 128), 1)
    east = pltpu.roll(from_east, lax.rem(128 - HALO * f, 128), 1)
    west = pltpu.roll(from_west, lax.rem(124 - HALO * f + 128, 128), 1)
    return jnp.where(lane < HALO, east, jnp.where(lane >= 128 - HALO, west, jnp.zeros_like(east)))


def extend(main, halo, side):
    return jnp.concatenate([jnp.concatenate([main, halo], axis=0), side], axis=1)


def to_east(x):
    return pltpu.roll(x, XC - 1, 1)


def to_west(x):
    return pltpu.roll(x, 1, 1)


def to_north(x):
    return pltpu.roll(x, XR - 1, 0)


def to_south(x):
    return pltpu.roll(x, 1, 0)


def sweep(f, c_east, c_north):
    c_west, c_south = to_west(c_east), to_south(c_north)
    for _ in range(NSTEP):
        change = c_east * (to_east(f) - f) + c_west * (to_west(f) - f)
        change = change + c_south * (to_south(f) - f)
        change = change + c_north * (to_north(f) - f)
        f = f + change
    return f


def first_pack(inc_ref, diff_ref, land_ref, head_ref, tail_ref, mirror_ref, mask_ref):
    ocean = lax.axis_index("comp") == 1
    mask = jnp.where(ocean, land_ref[...].astype(F32), jnp.ones((ROWS, COLS), F32))
    mask_ref[...] = mask
    heads = [inc_ref[l, 0:8, :] for l in range(LEV)] + [diff_ref[l, 0:8, :] for l in range(LEV)]
    tails = [inc_ref[l, 8:16, :] for l in range(LEV)] + [diff_ref[l, 8:16, :] for l in range(LEV)]
    heads += [mask[0:8], mask[0:8]]
    tails += [mask[8:16], mask[8:16]]
    pairs = [(heads[2 * p], tails[2 * p], heads[2 * p + 1], tails[2 * p + 1]) for p in range(LEV + 1)]
    put_edges(pairs, head_ref, tail_ref, mirror_ref)


def first_columns(
    inc_ref, diff_ref, mask_ref, from_south_ref, from_north_ref, from_fold_ref,
    halo_ref, east_ref, west_ref,
):
    halos = take_edges(2 * LEV + 1, from_south_ref, from_north_ref, from_fold_ref)
    for f, halo in enumerate(halos):
        halo_ref[f] = halo

    def field(f):
        def tile(t):
            if t == 2:
                return halo_ref[f]
            rows = slice(8 * t, 8 * t + 8)
            if f < LEV:
                return inc_ref[f, rows, :]
            if f < 2 * LEV:
                return diff_ref[f - LEV, rows, :]
            return mask_ref[rows, :]

        return tile

    put_columns([field(f) for f in range(2 * LEV + 1)], east_ref, west_ref)


def first_level(
    l, inc_ref, diff_ref, mask_ref, halo_ref, from_west, from_east, c_east_ref, c_north_ref, at
):
    mask = extend(mask_ref[...], halo_ref[2 * LEV], side_column(2 * LEV, from_west, from_east))
    diff = extend(diff_ref[l], halo_ref[LEV + l], side_column(LEV + l, from_west, from_east))
    c_east = mask * to_east(mask) * 0.5 * (diff + to_east(diff))
    c_north = mask * to_north(mask) * 0.5 * (diff + to_north(diff))
    c_east_ref[at] = c_east
    c_north_ref[at] = c_north
    f = extend(inc_ref[l], halo_ref[l], side_column(l, from_west, from_east))
    return sweep(f, c_east, c_north)[:ROWS, :COLS]


def first_surface(
    inc_ref, diff_ref, mask_ref, halo_ref, from_west_ref, from_east_ref,
    state_ref, surface_ref, c_east_ref, c_north_ref,
):
    f = first_level(
        0, inc_ref, diff_ref, mask_ref, halo_ref, from_west_ref[...], from_east_ref[...],
        c_east_ref, c_north_ref, 0,
    )
    state_ref[...] = f
    surface_ref[...] = mask_ref[...] * f


def first_rest(
    inc_ref, diff_ref, innov_ref, mask_ref, halo_ref, from_west_ref, from_east_ref,
    state_ref, adj_ref, c_east_ref, c_north_ref, head_ref, tail_ref, mirror_ref,
):
    from_west, from_east = from_west_ref[...], from_east_ref[...]

    def level(k, carry):
        f = first_level(
            k + 1, inc_ref, diff_ref, mask_ref, halo_ref, from_west, from_east,
            c_east_ref, c_north_ref, k,
        )
        state_ref[k + 1] = f
        adj_ref[k] = f - innov_ref[k + 1]
        return carry

    lax.fori_loop(0, LEV - 1, level, 0)
    state_ref[0] = jnp.zeros((ROWS, COLS), F32)
    put_edges(level_pairs(adj_ref, LEV - 1), head_ref, tail_ref, mirror_ref)


def level_pairs(ref, count):
    pairs = []
    for p in range((count + 1) // 2):
        a, b = 2 * p, min(2 * p + 1, count - 1)
        pairs.append((ref[a, 0:8], ref[a, 8:16], ref[b, 0:8], ref[b, 8:16]))
    return pairs


def row_of(ref):
    return lambda h: ref[h // 4 : h // 4 + 1, (h % 4) * 128 : (h % 4) * 128 + 128]


def gather_slots(table, cells):
    high, low = lax.shift_right_logical(cells, 7), cells & 127
    found = jnp.zeros((8, 128), F32)
    for h in range(64):
        row = jnp.broadcast_to(table(h), (8, 128))
        found = jnp.where(high == h, jnp.take_along_axis(row, low, axis=1), found)
    return found


GROUP = 8
SUMS = 4


def gather_all(cells_ref, table_ref, store):
    def group(g, carry):
        for n in range(GROUP):
            b = g * GROUP + n
            store(b, gather_slots(row_of(table_ref), cells_ref[b]))
        return carry

    lax.fori_loop(0, BANDS // GROUP, group, 0)


def gather_kernel(cells_ref, table_ref, out_ref):
    def store(b, found):
        out_ref[b] = found

    gather_all(cells_ref, table_ref, store)


def scatter_band(cells, values):
    high_iota = lax.broadcasted_iota(I32, (64, 128), 0)
    low_iota = lax.broadcasted_iota(I32, (128, 128), 0)
    high, low = lax.shift_right_logical(cells, 7), cells & 127
    coarse = values.astype(BF16).astype(F32)
    fine = values - coarse
    left, right = [], []
    for k in range(8):
        at = high_iota == high[k : k + 1]
        a = jnp.where(at, coarse[k : k + 1], 0.0).astype(BF16)
        b = jnp.where(at, fine[k : k + 1], 0.0).astype(BF16)
        left.append(jnp.concatenate([a, b], axis=0))
        right.append(jnp.where(low_iota == low[k : k + 1], 1.0, 0.0).astype(BF16))
    return lax.dot_general(
        jnp.concatenate(left, axis=1),
        jnp.concatenate(right, axis=1),
        (((1,), (1,)), ((), ())),
        preferred_element_type=F32,
    )


def as_block(sums):
    return jnp.concatenate([sums.reshape(ROWS, 4, 128)[:, k, :] for k in range(4)], axis=1)


def sum_slots(cells_of, values_of, acc_ref):
    acc_ref[...] = jnp.zeros_like(acc_ref)

    def step(g, carry):
        total = acc_ref[...]
        for n in range(SUMS):
            total = total + scatter_band(cells_of(SUMS * g + n), values_of(SUMS * g + n))
        acc_ref[...] = total
        return carry

    lax.fori_loop(0, BANDS // SUMS, step, 0)
    return as_block(acc_ref[0:64, :] + acc_ref[64:128, :])


def live_of(b, weight_ref, count_ref):
    slot = tile_iota(0) * 128 + tile_iota(1)
    return jnp.where(slot < count_ref[0, b], weight_ref[b], jnp.zeros((8, 128), F32))


def couple_kernel(
    count_ref, values_ref, cells_ref, weight_ref, mask_ref, state_ref, innov_ref,
    linear_ref, residual_ref, out_ref, acc_ref, table_ref,
):
    income = sum_slots(
        lambda b: cells_ref[b], lambda b: live_of(b, weight_ref, count_ref) * values_ref[b], acc_ref
    )
    mask = mask_ref[...]
    linear = state_ref[...] + mask * income
    residual = linear - innov_ref[...]
    linear_ref[...] = linear
    residual_ref[...] = residual
    table_ref[...] = mask * residual

    def store(b, found):
        out_ref[b] = live_of(b, weight_ref, count_ref) * found

    gather_all(cells_ref, table_ref, store)


def collect_kernel(values_ref, cells_ref, out_ref, acc_ref):
    out_ref[...] = sum_slots(lambda b: cells_ref[b], lambda b: values_ref[b], acc_ref)


def second_pack(residual_ref, mask_ref, returned_ref, adj_ref, head_ref, tail_ref, mirror_ref):
    adj_ref[0] = residual_ref[...] + mask_ref[...] * returned_ref[...]
    put_edges(level_pairs(adj_ref, 1), head_ref, tail_ref, mirror_ref)


def second_columns(
    adj_ref, from_south_ref, from_north_ref, from_fold_ref, halo_ref, east_ref, west_ref
):
    count = adj_ref.shape[0]
    halos = take_edges(count, from_south_ref, from_north_ref, from_fold_ref)
    for f, halo in enumerate(halos):
        halo_ref[f] = halo

    def field(f):
        return lambda t: halo_ref[f] if t == 2 else adj_ref[f, 8 * t : 8 * t + 8, :]

    put_columns([field(f) for f in range(count)], east_ref, west_ref)


def second_level(l, at, adj_ref, halo_ref, from_west, from_east, c_east_ref, c_north_ref, inc_ref):
    f = extend(adj_ref[at], halo_ref[at], side_column(at, from_west, from_east))
    return sweep(f, c_east_ref[at], c_north_ref[at])[:ROWS, :COLS] + inc_ref[l]


def second_rest(
    adj_ref, halo_ref, from_west_ref, from_east_ref, c_east_ref, c_north_ref, inc_ref, out_ref
):
    from_west, from_east = from_west_ref[...], from_east_ref[...]

    def level(k, carry):
        out_ref[k + 1] = second_level(
            k + 1, k, adj_ref, halo_ref, from_west, from_east, c_east_ref, c_north_ref, inc_ref
        )
        return carry

    lax.fori_loop(0, LEV - 1, level, 0)
    out_ref[0] = jnp.zeros((ROWS, COLS), F32)


def second_surface(
    adj_ref, halo_ref, from_west_ref, from_east_ref, c_east_ref, c_north_ref, inc_ref, rest_ref,
    out_ref,
):
    out_ref[...] = rest_ref[...]
    out_ref[0] = second_level(
        0, 0, adj_ref, halo_ref, from_west_ref[...], from_east_ref[...], c_east_ref, c_north_ref,
        inc_ref,
    )


def across(value):
    return lax.ppermute(value, "comp", [(0, 1), (1, 0)])


def along(head, tail, mirror):
    n, m = lax.axis_size("lat"), lax.axis_size("lon")
    return (
        lax.ppermute(tail, "lat", [(i, (i + 1) % n) for i in range(n)]),
        lax.ppermute(head, "lat", [((i + 1) % n, i) for i in range(n)]),
        lax.ppermute(mirror, "lon", [(i, m - 1 - i) for i in range(m)]),
    )


def around(east, west):
    n = lax.axis_size("lon")
    return (
        lax.ppermute(east, "lon", [(i, (i + 1) % n) for i in range(n)]),
        lax.ppermute(west, "lon", [((i + 1) % n, i) for i in range(n)]),
    )


def exchange(slots):
    return lax.all_to_all(slots, "lat", 0, 0, tiled=True)


def local(
    increment, diffusivity, innovation, land_mask, pull_cells, put_cells, pull_weight, pull_count
):
    inc, diff, innov = increment[0], diffusivity[0], innovation[0]
    pulled = exchange(pull_cells.reshape(BANDS, 8, 128))
    placed = put_cells.reshape(BANDS, 8, 128)
    weight = pull_weight.reshape(BANDS, 8, 128)
    count = pull_count.reshape(1, BANDS)

    edge = sds(LEV + 1, 8, COLS)
    packed = sds(XR, 128)
    plane = sds(ROWS, COLS)
    slots = sds(BANDS, 8, 128)
    *edges, mask = call(first_pack, (edge, edge, edge, plane), "first_pack")(inc, diff, land_mask)
    halo, east, west = call(
        first_columns, (sds(2 * LEV + 1, 8, COLS), packed, packed), "first_columns"
    )(inc, diff, mask, *along(*edges))
    from_west, from_east = around(east, west)
    wide = sds(1, XR, XC)
    state0, surface, c_east0, c_north0 = call(
        first_surface, (plane, plane, wide, wide), "first_surface"
    )(inc, diff, mask, halo, from_west, from_east)
    sent = call(gather_kernel, slots, "gather_slots")(pulled, across(surface))
    sent, halo, from_west, from_east = lax.optimization_barrier((sent, halo, from_west, from_east))
    values = exchange(sent)

    edge = sds(LEV // 2, 8, COLS)
    wide = sds(LEV - 1, XR, XC)
    state, adj, c_east, c_north, *edges = call(
        first_rest,
        (sds(LEV, ROWS, COLS), sds(LEV - 1, ROWS, COLS), wide, wide, edge, edge, edge),
        "first_rest",
        nbytes=12000000,
    )(inc, diff, innov, mask, halo, from_west, from_east)
    edges = along(*edges)

    acc = pltpu.VMEM((128, 128), F32)
    smem = pl.BlockSpec(memory_space=pltpu.SMEM)
    vmem = pl.BlockSpec(memory_space=pltpu.VMEM)
    linear, residual, outgoing = pl.pallas_call(
        couple_kernel,
        out_shape=(plane, plane, slots),
        in_specs=[smem] + [vmem] * 6,
        out_specs=(vmem,) * 3,
        scratch_shapes=[acc, pltpu.VMEM((ROWS, COLS), F32)],
        name="couple",
        compiler_params=pltpu.CompilerParams(vmem_limit_bytes=48 << 20),
    )(count, values, placed, weight, mask, state0, innov[0])

    outgoing, adj, *edges = lax.optimization_barrier((outgoing, adj, *edges))
    back = exchange(outgoing)
    halo, east, west = call(
        second_columns, (sds(LEV - 1, 8, COLS), packed, packed), "second_columns_rest"
    )(adj, *edges)
    from_west, from_east = around(east, west)
    rest = call(second_rest, sds(LEV, ROWS, COLS), "second_rest", nbytes=12000000)(
        adj, halo, from_west, from_east, c_east, c_north, inc
    )

    returned = across(call(collect_kernel, plane, "collect", [acc])(back, pulled))
    edge = sds(1, 8, COLS)
    adj, *edges = call(second_pack, (sds(1, ROWS, COLS), edge, edge, edge), "second_pack")(
        residual, mask, returned
    )
    halo, east, west = call(second_columns, (sds(1, 8, COLS), packed, packed), "second_columns")(
        adj, *along(*edges)
    )
    from_west, from_east = around(east, west)
    gradient = call(second_surface, sds(LEV, ROWS, COLS), "second_surface")(
        adj, halo, from_west, from_east, c_east0, c_north0, inc, rest
    )
    linear_state = lax.dynamic_update_slice(state, linear[None], (0, 0, 0))
    return (linear_state[None], gradient[None])


def solution(mesh):
    placed = (
        P("comp", None, "lat", "lon"),
        P("comp", None, "lat", "lon"),
        P("comp", None, "lat", "lon"),
        P("lat", "lon"),
        P("comp", "lat", "lon", None, None),
        P("comp", "lat", "lon", None, None),
        P("comp", "lat", "lon", None, None),
        P("comp", "lat", "lon", None),
    )
    return jax.shard_map(
        local,
        mesh=mesh,
        in_specs=placed,
        out_specs=(P("comp", None, "lat", "lon"), P("comp", None, "lat", "lon")),
        check_vma=False,
    )
```

time: 116 us -> 106 us (0.914)
  Pallas kernels: 32.1 us -> 16.2 us
  waiting for transfers between devices: 28.4 us -> 13.6 us
  starting transfers between devices: 35.1 us -> 46.2 us
  local copies, waits for them, and re-layouts: 4.01 us -> 11.3 us
  blocking collectives: 13.9 us -> 17.8 us
    pallas_call x9 -> x11, Pallas kernels: 32.1 us -> 16.2 us  [the longest x1 4.24 us: local(): call(first_rest, (sds(LEV, ROWS, COLS), sds(LEV - 1, ROWS, COLS), wide, w...]
    ppermute x4 -> x9, starting transfers between devices: 9.33 us -> 19.9 us  [the longest x3 11.3 us: along(): lax.ppermute(head, 'lat', [((i + 1) % n, i) for i in range(n)])]
    all_to_all x2, waiting for transfers between devices: 9.65 us -> 0.11 us  [exchange(): return lax.all_to_all(slots, 'lat', 0, 0, tiled=True)]
    pallas_call x0 -> x1, local copies, waits for them, and re-layouts: none -> 7.32 us  [local(): pl.pallas_call(couple_kernel, out_shape=(plane, plane, slots), in_specs=[...]
    ppermute x4 -> x9, waiting for transfers between devices: 10.6 us -> 5.89 us  [the longest x3 5.03 us: along(): lax.ppermute(tail, 'lat', [(i, (i + 1) % n) for i in range(n)])]
    all_to_all x1, blocking collectives: 13.9 us -> 17.8 us  [exchange(): return lax.all_to_all(slots, 'lat', 0, 0, tiled=True)]
    ppermute x2 -> x3, starting transfers between devices: 0.91 us -> 3.39 us  [around(): lax.ppermute(east, 'lon', [(i, (i + 1) % n) for i in range(n)])]
    all_to_all x2, starting transfers between devices: 21.4 us -> 19.2 us  [exchange(): return lax.all_to_all(slots, 'lat', 0, 0, tiled=True)]
  transfers between devices with their start and end apart: 12 -> 19, of which waited for: 11 -> 9; matrix products, arithmetic and copies ran while one was open for 1% -> 7% of each run, Pallas kernels for 4% -> 8%
where the time goes in v2:
time: 106 us
  starting transfers between devices  46.2 us (44%)
  blocking collectives  17.8 us (17%)
  Pallas kernels  16.2 us (15%)
  waiting for transfers between devices  13.6 us (13%)
  local copies, waits for them, and re-layouts  11.3 us (11%)
    all_to_all x2, starting transfers between devices, exchange(): return lax.all_to_all(slots, 'lat', 0, 0, tiled=True)  19.2 us
    all_to_all x1, blocking collectives, exchange(): return lax.all_to_all(slots, 'lat', 0, 0, tiled=True)  17.8 us
    ppermute x3, starting transfers between devices, along(): lax.ppermute(head, 'lat', [((i + 1) % n, i) for i in range(n)])  11.3 us
    pallas_call x1, local copies, waits for them, and re-layouts, local(): pl.pallas_call(couple_kernel, out_shape=(plane, plane, slots), in_specs=[...  7.32 us
    ppermute x3, waiting for transfers between devices, along(): lax.ppermute(tail, 'lat', [(i, (i + 1) % n) for i in range(n)])  5.03 us
    ppermute x3, starting transfers between devices, along(): lax.ppermute(tail, 'lat', [(i, (i + 1) % n) for i in range(n)])  4.88 us
    pallas_call x1, Pallas kernels, local(): call(first_rest, (sds(LEV, ROWS, COLS), sds(LEV - 1, ROWS, COLS), wide, w...  4.24 us
    unnamed x17, local copies, waits for them, and re-layouts  3.99 us
  transfers between devices with their start and end apart: 19, of which 9 were waited for; matrix products, arithmetic and copies ran while one was open for 7% of the time, Pallas kernels for 8%

profile of v2, /device:TPU:6, one launch (start us, length us, event | category | flops | bytes accessed | tf_op | source)
XLA Modules:
  0.0 105.9 jit_solution(2712462659046156961)
XLA Ops:
  0.6 1.6 %copy.10 = s32[4,8,8,128]{3,2,1,0:T(8,128)} copy(s32[4,8,8,128]{3,1,2,0:T(8,128)} %bitcast.36) | data formatting | bytes 262144
  2.3 11.5 %all-to-all-start = ((s32[32,8,128]{2,1,0:T(8,128)}), s32[32,8,128]{2,1,0:T(8,128)S(1)}, u32[]{:S(2)}, u32[]{:S(2)}) async-start(s32[32,8,128]{2,1,0:T(8,128)} %bitcast.11), calls=%async_computation | async-start | bytes 262144 | tf_op jit(solution)/shard_map/all_to_all | solution.py:393
  13.8 0.7 copy-done.3
  14.6 1.9 %collective-permute-start = (f32[9,8,512]{2,1,0:T(8,128)S(1)}, f32[9,8,512]{2,1,0:T(8,128)S(1)}, u32[]{:S(2)}, u32[]{:S(2)}) collective-permute-start(f32[9,8,512]{2,1,0:T(8,128)S(1)} %get-tuple-element.43), channel_id=1, source_target_pairs={{0,4},{4,8},{8,12},{12,16},{16,20},{20,24},{24,28},{28,32},{32,36}... | collective-permute-start | bytes 442376 | tf_op jit(solution)/shard_map/ppermute | solution.py:378
  16.5 3.6 %collective-permute-start.1 = (f32[9,8,512]{2,1,0:T(8,128)S(1)}, f32[9,8,512]{2,1,0:T(8,128)S(1)}, u32[]{:S(2)}, u32[]{:S(2)}) collective-permute-start(f32[9,8,512]{2,1,0:T(8,128)S(1)} %get-tuple-element.44), channel_id=1, source_target_pairs={{4,0},{8,4},{12,8},{16,12},{20,16},{24,20},{28,24},{32,28},{36,32}... | collective-permute-start | bytes 442376 | tf_op jit(solution)/shard_map/ppermute | solution.py:379
  20.5 5.0 %collective-permute-done.from_south_ref = f32[9,8,512]{2,1,0:T(8,128)S(1)} collective-permute-done((f32[9,8,512]{2,1,0:T(8,128)S(1)}, f32[9,8,512]{2,1,0:T(8,128)S(1)}, u32[]{:S(2)}, u32[]{:S(2)}) %collective-permute-start) | collective-permute-done | bytes 147488 | tf_op jit(solution)/shard_map/ppermute | solution.py:378
  25.5 0.8 collective-permute-done.2.from_fold_ref
  26.6 0.6 collective-permute-start.3
  27.1 1.5 %collective-permute-start.4 = (f32[24,128]{1,0:T(8,128)S(1)}, f32[24,128]{1,0:T(8,128)S(1)}, u32[]{:S(2)}, u32[]{:S(2)}) collective-permute-start(f32[24,128]{1,0:T(8,128)S(1)} %get-tuple-element.48), channel_id=1, source_target_pairs={{1,0},{2,1},{3,2},{0,3},{5,4},{6,5},{7,6},{4,7},{9,8},{10,9},{11,1... | collective-permute-start | bytes 36872 | tf_op jit(solution)/shard_map/ppermute | solution.py:388
  28.7 1.7 %collective-permute-done.3.from_west_ref = f32[24,128]{1,0:T(8,128)S(1)} collective-permute-done((f32[24,128]{1,0:T(8,128)S(1)}, f32[24,128]{1,0:T(8,128)S(1)}, u32[]{:S(2)}, u32[]{:S(2)}) %collective-permute-start.3) | collective-permute-done | bytes 12320 | tf_op jit(solution)/shard_map/ppermute | solution.py:387
  30.3 1.7 %collective-permute-done.4.from_east_ref = f32[24,128]{1,0:T(8,128)S(1)} collective-permute-done((f32[24,128]{1,0:T(8,128)S(1)}, f32[24,128]{1,0:T(8,128)S(1)}, u32[]{:S(2)}, u32[]{:S(2)}) %collective-permute-start.4) | collective-permute-done | bytes 12320 | tf_op jit(solution)/shard_map/ppermute | solution.py:388
  32.0 0.5 first_surface.1
  32.6 1.2 %collective-permute-done.5.table_ref = f32[16,512]{1,0:T(8,128)S(1)} collective-permute-done((f32[16,512]{1,0:T(8,128)S(1)}, f32[16,512]{1,0:T(8,128)S(1)}, u32[]{:S(2)}, u32[]{:S(2)}) %collective-permute-start.5) | collective-permute-done | bytes 32800 | tf_op jit(solution)/shard_map/ppermute | solution.py:372
  33.8 3.2 %gather_slots.1 = f32[32,8,128]{2,1,0:T(8,128)} custom-call(s32[32,8,128]{2,1,0:T(8,128)S(1)} %all-to-all-done.cells_ref, f32[16,512]{1,0:T(8,128)S(1)} %collective-permute-done.5.table_ref), custom_call_target="tpu_custom_call" | custom-call | flops 100000 | bytes 1000000 | tf_op jit(solution)/shard_map/gather_slots/pallas_call | solution.py:418
  37.0 7.7 %all-to-all-start.1 = ((f32[32,8,128]{2,1,0:T(8,128)}), f32[32,8,128]{2,1,0:T(8,128)S(1)}, u32[]{:S(2)}, u32[]{:S(2)}) async-start(f32[32,8,128]{2,1,0:T(8,128)} %gather_slots.1), calls=%async_computation.1 | async-start | bytes 262144 | tf_op jit(solution)/shard_map/all_to_all | solution.py:393
  44.7 4.2 %first_rest.1 = (f32[8,16,512]{2,1,0:T(8,128)}, f32[7,16,512]{2,1,0:T(8,128)S(1)}, f32[7,24,640]{2,1,0:T(8,128)S(1)}, f32[7,24,640]{2,1,0:T(8,128)S(1)}, f32[4,8...) custom-call(f32[8,16,512]{2,1,0:T(8,128)S(1)} %bitcast.25, f32[8,16,512]{2,1,0:T(8,128)S(1)} %bitcast.31, ...), custom_call_target="tpu_custom_call" | custom-call | flops 100000 | bytes 12000000 | tf_op jit(solution)/shard_map/first_rest/pallas_call | solution.py:424
  49.0 1.8 %collective-permute-start.6 = (f32[4,8,512]{2,1,0:T(8,128)S(1)}, f32[4,8,512]{2,1,0:T(8,128)S(1)}, u32[]{:S(2)}, u32[]{:S(2)}) collective-permute-start(f32[4,8,512]{2,1,0:T(8,128)S(1)} %get-tuple-element.60), channel_id=1, source_target_pairs={{0,4},{4,8},{8,12},{12,16},{16,20},{20,24},{24,28},{28,32},{32,36}... | collective-permute-start | bytes 196616 | tf_op jit(solution)/shard_map/ppermute | solution.py:378
  50.8 3.6 %collective-permute-start.7 = (f32[4,8,512]{2,1,0:T(8,128)S(1)}, f32[4,8,512]{2,1,0:T(8,128)S(1)}, u32[]{:S(2)}, u32[]{:S(2)}) collective-permute-start(f32[4,8,512]{2,1,0:T(8,128)S(1)} %get-tuple-element.61), channel_id=1, source_target_pairs={{4,0},{8,4},{12,8},{16,12},{20,16},{24,20},{28,24},{32,28},{36,32}... | collective-permute-start | bytes 196616 | tf_op jit(solution)/shard_map/ppermute | solution.py:379
  54.4 0.9 copy-done.5
  55.4 0.7 copy-done.6
  56.0 7.3 %couple.1 = (f32[1,8,16,512]{3,2,1,0:T(8,128)}, f32[16,512]{1,0:T(8,128)S(1)}, f32[32,8,128]{2,1,0:T(8,128)S(1)}) fusion(f32[1,8,16,512]{3,2,1,0:T(8,128)} %bitcast.40, s32[1,32]{1,0:T(1,128)S(1)} %bitcast.39, f32[32,8,128]{2,1,0:T(8,128)S(1)} %all-to-all-done.1, s32[32,8,128]{2,1,0:T(8,128)S(1)} %bitcast.33, f32[32,8,128]{2,1,0:T(8,128)S(1)} %bitcast.34, ...), kind=kCustom, calls=%fused_computation | custom fusion | bytes 688256 | tf_op jit(solution)/shard_map/couple/pallas_call | solution.py:435
  63.4 17.8 %all_to_all.15.values_ref = f32[32,8,128]{2,1,0:T(8,128)S(1)} all-to-all(f32[32,8,128]{2,1,0:T(8,128)S(1)} %get-tuple-element.63), channel_id=1, replica_groups=mesh['comp'=2,'lat'=32,'lon'=4] {'lat'}, dimensions={0} | all-to-all | bytes 262144 | tf_op jit(solution)/shard_map/all_to_all | solution.py:393
  81.1 3.7 %collect.1 = f32[16,512]{1,0:T(8,128)S(1)} custom-call(f32[32,8,128]{2,1,0:T(8,128)S(1)} %all_to_all.15.values_ref, s32[32,8,128]{2,1,0:T(8,128)S(1)} %all-to-all-done.cells_ref), custom_call_target="tpu_custom_call" | custom-call | flops 100000 | bytes 1000000 | tf_op jit(solution)/shard_map/collect/pallas_call | solution.py:455
  85.0 1.2 %collective-permute-done.9.returned_ref = f32[16,512]{1,0:T(8,128)S(1)} collective-permute-done((f32[16,512]{1,0:T(8,128)S(1)}, f32[16,512]{1,0:T(8,128)S(1)}, u32[]{:S(2)}, u32[]{:S(2)}) %collective-permute-start.9) | collective-permute-done | bytes 32800 | tf_op jit(solution)/shard_map/ppermute | solution.py:372
  86.2 1.2 %collective-permute-start.10 = (f32[1,8,512]{2,1,0:T(8,128)S(1)}, f32[1,8,512]{2,1,0:T(8,128)S(1)}, u32[]{:S(2)}, u32[]{:S(2)}) collective-permute-start(f32[1,8,512]{2,1,0:T(8,128)S(1)} %get-tuple-element.65), channel_id=1, source_target_pairs={{0,4},{4,8},{8,12},{12,16},{16,20},{20,24},{24,28},{28,32},{32,36}... | collective-permute-start | bytes 49160 | tf_op jit(solution)/shard_map/ppermute | solution.py:378
  87.4 4.2 %collective-permute-start.11 = (f32[1,8,512]{2,1,0:T(8,128)S(1)}, f32[1,8,512]{2,1,0:T(8,128)S(1)}, u32[]{:S(2)}, u32[]{:S(2)}) collective-permute-start(f32[1,8,512]{2,1,0:T(8,128)S(1)} %get-tuple-element.66), channel_id=1, source_target_pairs={{4,0},{8,4},{12,8},{16,12},{20,16},{24,20},{28,24},{32,28},{36,32}... | collective-permute-start | bytes 49160 | tf_op jit(solution)/shard_map/ppermute | solution.py:379
  91.6 3.2 %collective-permute-start.12 = (f32[1,8,512]{2,1,0:T(8,128)S(1)}, f32[1,8,512]{2,1,0:T(8,128)S(1)}, u32[]{:S(2)}, u32[]{:S(2)}) collective-permute-start(f32[1,8,512]{2,1,0:T(8,128)S(1)} %get-tuple-element.67), channel_id=1, source_target_pairs={{0,3},{1,2},{2,1},{3,0},{4,7},{5,6},{6,5},{7,4},{8,11},{9,10},{10,... | collective-permute-start | bytes 49160 | tf_op jit(solution)/shard_map/ppermute | solution.py:380
  95.1 2.0 %collective-permute-start.16 = (f32[24,128]{1,0:T(8,128)S(1)}, f32[24,128]{1,0:T(8,128)S(1)}, u32[]{:S(2)}, u32[]{:S(2)}) collective-permute-start(f32[24,128]{1,0:T(8,128)S(1)} %get-tuple-element.79), channel_id=1, source_target_pairs={{1,0},{2,1},{3,2},{0,3},{5,4},{6,5},{7,6},{4,7},{9,8},{10,9},{11,1... | collective-permute-start | bytes 36872 | tf_op jit(solution)/shard_map/ppermute | solution.py:388
  97.1 2.7 %collective-permute-start.13 = (f32[24,128]{1,0:T(8,128)S(1)}, f32[24,128]{1,0:T(8,128)S(1)}, u32[]{:S(2)}, u32[]{:S(2)}) collective-permute-start(f32[24,128]{1,0:T(8,128)S(1)} %get-tuple-element.69), channel_id=1, source_target_pairs={{0,1},{1,2},{2,3},{3,0},{4,5},{5,6},{6,7},{7,4},{8,9},{9,10},{10,1... | collective-permute-start | bytes 36872 | tf_op jit(solution)/shard_map/ppermute | solution.py:387
  100.0 3.0 %second_rest.1.rest_ref = f32[8,16,512]{2,1,0:T(8,128)S(1)} custom-call(f32[7,16,512]{2,1,0:T(8,128)S(1)} %get-tuple-element.73.adj_ref, f32[7,8,512]{2,1,0:T(8,128)S(1)} %get-tuple-element.77.halo_ref, f32[24,128]{1,0:T(8,128)S(1)} %collective-permute-done.15.from_west_ref, f32[24,128]{1,0:T(8,128)S(1)} %collective-permute-done.16.from_east_ref, ...), custom_call_target="tpu_custom_call" | custom-call | flops 100000 | bytes 12000000 | tf_op jit(solution)/shard_map/second_rest/pallas_call | solution.py:451
  103.0 1.7 %collective-permute-done.14.from_east_ref = f32[24,128]{1,0:T(8,128)S(1)} collective-permute-done((f32[24,128]{1,0:T(8,128)S(1)}, f32[24,128]{1,0:T(8,128)S(1)}, u32[]{:S(2)}, u32[]{:S(2)}) %collective-permute-start.14) | collective-permute-done | bytes 12320 | tf_op jit(solution)/shard_map/ppermute | solution.py:388
  104.8 1.1 %second_surface.1 = f32[8,16,512]{2,1,0:T(8,128)} custom-call(f32[1,16,512]{2,1,0:T(8,128)S(1)} %get-tuple-element.64.adj_ref, f32[1,8,512]{2,1,0:T(8,128)S(1)} %get-tuple-element.68.halo_ref, f32[24,128]{1,0:T(8,128)S(1)} %collective-permute-done.13.from_west_ref, f32[24,128]{1,0:T(8,128)S(1)} %collective-permute-done.14.from_east_ref, ...), custom_call_target="tpu_custom_call" | custom-call | flops 100000 | bytes 1000000 | tf_op jit(solution)/shard_map/second_surface/pallas_call | solution.py:464
  (37 shorter events, 1.6 us)
Async XLA Ops:
  0.6 13.2 %copy-start = (f32[1,8,16,512]{3,2,1,0:T(8,128)S(1)}, f32[1,8,16,512]{3,2,1,0:T(8,128)}, u32[]{:S(2)}) copy-start(f32[1,8,16,512]{3,2,1,0:T(8,128)} %param.8) | copy-start | bytes 786436
  0.6 13.2 %copy-start.1 = (f32[1,8,16,512]{3,2,1,0:T(8,128)S(1)}, f32[1,8,16,512]{3,2,1,0:T(8,128)}, u32[]{:S(2)}) copy-start(f32[1,8,16,512]{3,2,1,0:T(8,128)} %param.9) | copy-start | bytes 786436
  2.3 31.5 %all-to-all-start = ((s32[32,8,128]{2,1,0:T(8,128)}), s32[32,8,128]{2,1,0:T(8,128)S(1)}, u32[]{:S(2)}, u32[]{:S(2)}) async-start(s32[32,8,128]{2,1,0:T(8,128)} %bitcast.11), calls=%async_computation | async-start | bytes 262144 | tf_op jit(solution)/shard_map/all_to_all | solution.py:393
  13.8 0.8 copy-start.3
  14.6 10.9 %collective-permute-start = (f32[9,8,512]{2,1,0:T(8,128)S(1)}, f32[9,8,512]{2,1,0:T(8,128)S(1)}, u32[]{:S(2)}, u32[]{:S(2)}) collective-permute-start(f32[9,8,512]{2,1,0:T(8,128)S(1)} %get-tuple-element.43), channel_id=1, source_target_pairs={{0,4},{4,8},{8,12},{12,16},{16,20},{20,24},{24,28},{28,32},{32,36}... | collective-permute-start | bytes 442376 | tf_op jit(solution)/shard_map/ppermute | solution.py:378
  16.5 9.1 %collective-permute-start.1 = (f32[9,8,512]{2,1,0:T(8,128)S(1)}, f32[9,8,512]{2,1,0:T(8,128)S(1)}, u32[]{:S(2)}, u32[]{:S(2)}) collective-permute-start(f32[9,8,512]{2,1,0:T(8,128)S(1)} %get-tuple-element.44), channel_id=1, source_target_pairs={{4,0},{8,4},{12,8},{16,12},{20,16},{24,20},{28,24},{32,28},{36,32}... | collective-permute-start | bytes 442376 | tf_op jit(solution)/shard_map/ppermute | solution.py:379
  20.0 6.4 %collective-permute-start.2 = (f32[9,8,512]{2,1,0:T(8,128)S(1)}, f32[9,8,512]{2,1,0:T(8,128)S(1)}, u32[]{:S(2)}, u32[]{:S(2)}) collective-permute-start(f32[9,8,512]{2,1,0:T(8,128)S(1)} %get-tuple-element.45), channel_id=1, source_target_pairs={{0,3},{1,2},{2,1},{3,0},{4,7},{5,6},{6,5},{7,4},{8,11},{9,10},{10,... | collective-permute-start | bytes 442376 | tf_op jit(solution)/shard_map/ppermute | solution.py:380
  26.6 3.8 %collective-permute-start.3 = (f32[24,128]{1,0:T(8,128)S(1)}, f32[24,128]{1,0:T(8,128)S(1)}, u32[]{:S(2)}, u32[]{:S(2)}) collective-permute-start(f32[24,128]{1,0:T(8,128)S(1)} %get-tuple-element.47), channel_id=1, source_target_pairs={{0,1},{1,2},{2,3},{3,0},{4,5},{5,6},{6,7},{7,4},{8,9},{9,10},{10,1... | collective-permute-start | bytes 36872 | tf_op jit(solution)/shard_map/ppermute | solution.py:387
  27.1 4.9 %collective-permute-start.4 = (f32[24,128]{1,0:T(8,128)S(1)}, f32[24,128]{1,0:T(8,128)S(1)}, u32[]{:S(2)}, u32[]{:S(2)}) collective-permute-start(f32[24,128]{1,0:T(8,128)S(1)} %get-tuple-element.48), channel_id=1, source_target_pairs={{1,0},{2,1},{3,2},{0,3},{5,4},{6,5},{7,6},{4,7},{9,8},{10,9},{11,1... | collective-permute-start | bytes 36872 | tf_op jit(solution)/shard_map/ppermute | solution.py:388
  32.5 12.2 %copy-start.2 = (f32[1,8,16,512]{3,2,1,0:T(8,128)S(1)}, f32[1,8,16,512]{3,2,1,0:T(8,128)}, u32[]{:S(2)}) copy-start(f32[1,8,16,512]{3,2,1,0:T(8,128)} %param.10) | copy-start | bytes 786436
  32.5 1.3 %collective-permute-start.5 = (f32[16,512]{1,0:T(8,128)S(1)}, f32[16,512]{1,0:T(8,128)S(1)}, u32[]{:S(2)}, u32[]{:S(2)}) collective-permute-start(f32[16,512]{1,0:T(8,128)S(1)} %get-tuple-element.49), channel_id=1, source_target_pairs={{0,128},{128,0},{1,129},{129,1},{2,130},{130,2},{3,131},{131,3},{4... | collective-permute-start | bytes 98312 | tf_op jit(solution)/shard_map/ppermute | solution.py:372
  37.0 18.4 %all-to-all-start.1 = ((f32[32,8,128]{2,1,0:T(8,128)}), f32[32,8,128]{2,1,0:T(8,128)S(1)}, u32[]{:S(2)}, u32[]{:S(2)}) async-start(f32[32,8,128]{2,1,0:T(8,128)} %gather_slots.1), calls=%async_computation.1 | async-start | bytes 262144 | tf_op jit(solution)/shard_map/all_to_all | solution.py:393
  44.7 9.6 %copy-start.4 = (s32[1,1,1,32,1024]{4,3,2,1,0:T(8,128)S(1)}, s32[1,1,1,32,1024]{4,3,2,1,0:T(8,128)}, u32[]{:S(2)}) copy-start(s32[1,1,1,32,1024]{4,3,2,1,0:T(8,128)} %param.13) | copy-start | bytes 393220
  49.0 14.4 %collective-permute-start.6 = (f32[4,8,512]{2,1,0:T(8,128)S(1)}, f32[4,8,512]{2,1,0:T(8,128)S(1)}, u32[]{:S(2)}, u32[]{:S(2)}) collective-permute-start(f32[4,8,512]{2,1,0:T(8,128)S(1)} %get-tuple-element.60), channel_id=1, source_target_pairs={{0,4},{4,8},{8,12},{12,16},{16,20},{20,24},{24,28},{28,32},{32,36}... | collective-permute-start | bytes 196616 | tf_op jit(solution)/shard_map/ppermute | solution.py:378
  50.8 12.6 %collective-permute-start.7 = (f32[4,8,512]{2,1,0:T(8,128)S(1)}, f32[4,8,512]{2,1,0:T(8,128)S(1)}, u32[]{:S(2)}, u32[]{:S(2)}) collective-permute-start(f32[4,8,512]{2,1,0:T(8,128)S(1)} %get-tuple-element.61), channel_id=1, source_target_pairs={{4,0},{8,4},{12,8},{16,12},{20,16},{24,20},{28,24},{32,28},{36,32}... | collective-permute-start | bytes 196616 | tf_op jit(solution)/shard_map/ppermute | solution.py:379
  54.3 9.0 %collective-permute-start.8 = (f32[4,8,512]{2,1,0:T(8,128)S(1)}, f32[4,8,512]{2,1,0:T(8,128)S(1)}, u32[]{:S(2)}, u32[]{:S(2)}) collective-permute-start(f32[4,8,512]{2,1,0:T(8,128)S(1)} %get-tuple-element.62), channel_id=1, source_target_pairs={{0,3},{1,2},{2,1},{3,0},{4,7},{5,6},{6,5},{7,4},{8,11},{9,10},{10,... | collective-permute-start | bytes 196616 | tf_op jit(solution)/shard_map/ppermute | solution.py:380
  54.3 0.9 copy-start.5
  55.4 0.7 copy-start.6
  84.9 1.3 %collective-permute-start.9 = (f32[16,512]{1,0:T(8,128)S(1)}, f32[16,512]{1,0:T(8,128)S(1)}, u32[]{:S(2)}, u32[]{:S(2)}) collective-permute-start(f32[16,512]{1,0:T(8,128)S(1)} %collect.1), channel_id=1, source_target_pairs={{0,128},{128,0},{1,129},{129,1},{2,130},{130,2},{3,131},{131,3},{4... | collective-permute-start | bytes 98312 | tf_op jit(solution)/shard_map/ppermute | solution.py:372
  86.2 10.8 %collective-permute-start.10 = (f32[1,8,512]{2,1,0:T(8,128)S(1)}, f32[1,8,512]{2,1,0:T(8,128)S(1)}, u32[]{:S(2)}, u32[]{:S(2)}) collective-permute-start(f32[1,8,512]{2,1,0:T(8,128)S(1)} %get-tuple-element.65), channel_id=1, source_target_pairs={{0,4},{4,8},{8,12},{12,16},{16,20},{20,24},{24,28},{28,32},{32,36}... | collective-permute-start | bytes 49160 | tf_op jit(solution)/shard_map/ppermute | solution.py:378
  87.4 9.6 %collective-permute-start.11 = (f32[1,8,512]{2,1,0:T(8,128)S(1)}, f32[1,8,512]{2,1,0:T(8,128)S(1)}, u32[]{:S(2)}, u32[]{:S(2)}) collective-permute-start(f32[1,8,512]{2,1,0:T(8,128)S(1)} %get-tuple-element.66), channel_id=1, source_target_pairs={{4,0},{8,4},{12,8},{16,12},{20,16},{24,20},{28,24},{32,28},{36,32}... | collective-permute-start | bytes 49160 | tf_op jit(solution)/shard_map/ppermute | solution.py:379
  91.6 5.4 %collective-permute-start.12 = (f32[1,8,512]{2,1,0:T(8,128)S(1)}, f32[1,8,512]{2,1,0:T(8,128)S(1)}, u32[]{:S(2)}, u32[]{:S(2)}) collective-permute-start(f32[1,8,512]{2,1,0:T(8,128)S(1)} %get-tuple-element.67), channel_id=1, source_target_pairs={{0,3},{1,2},{2,1},{3,0},{4,7},{5,6},{6,5},{7,4},{8,11},{9,10},{10,... | collective-permute-start | bytes 49160 | tf_op jit(solution)/shard_map/ppermute | solution.py:380
  94.9 4.9 %collective-permute-start.15 = (f32[24,128]{1,0:T(8,128)S(1)}, f32[24,128]{1,0:T(8,128)S(1)}, u32[]{:S(2)}, u32[]{:S(2)}) collective-permute-start(f32[24,128]{1,0:T(8,128)S(1)} %get-tuple-element.78), channel_id=1, source_target_pairs={{0,1},{1,2},{2,3},{3,0},{4,5},{5,6},{6,7},{7,4},{8,9},{9,10},{10,1... | collective-permute-start | bytes 36872 | tf_op jit(solution)/shard_map/ppermute | solution.py:387
  95.1 5.0 %collective-permute-start.16 = (f32[24,128]{1,0:T(8,128)S(1)}, f32[24,128]{1,0:T(8,128)S(1)}, u32[]{:S(2)}, u32[]{:S(2)}) collective-permute-start(f32[24,128]{1,0:T(8,128)S(1)} %get-tuple-element.79), channel_id=1, source_target_pairs={{1,0},{2,1},{3,2},{0,3},{5,4},{6,5},{7,6},{4,7},{9,8},{10,9},{11,1... | collective-permute-start | bytes 36872 | tf_op jit(solution)/shard_map/ppermute | solution.py:388
  97.1 5.9 %collective-permute-start.13 = (f32[24,128]{1,0:T(8,128)S(1)}, f32[24,128]{1,0:T(8,128)S(1)}, u32[]{:S(2)}, u32[]{:S(2)}) collective-permute-start(f32[24,128]{1,0:T(8,128)S(1)} %get-tuple-element.69), channel_id=1, source_target_pairs={{0,1},{1,2},{2,3},{3,0},{4,5},{5,6},{6,7},{7,4},{8,9},{9,10},{10,1... | collective-permute-start | bytes 36872 | tf_op jit(solution)/shard_map/ppermute | solution.py:387
  99.9 4.9 %collective-permute-start.14 = (f32[24,128]{1,0:T(8,128)S(1)}, f32[24,128]{1,0:T(8,128)S(1)}, u32[]{:S(2)}, u32[]{:S(2)}) collective-permute-start(f32[24,128]{1,0:T(8,128)S(1)} %get-tuple-element.70), channel_id=1, source_target_pairs={{1,0},{2,1},{3,2},{0,3},{5,4},{6,5},{7,6},{4,7},{9,8},{10,9},{11,1... | collective-permute-start | bytes 36872 | tf_op jit(solution)/shard_map/ppermute | solution.py:388

commit v3 on v2

v3 whole, which is shorter than its diff:
```python
import jax
import jax.numpy as jnp
from jax import lax
from jax.experimental import pallas as pl
from jax.experimental.pallas import tpu as pltpu
from jax.sharding import PartitionSpec as P

NSTEP = 4
HALO, WIDE = 4, 8
ROWS, COLS, LEV = 16, 512, 8
XR, XC = 24, 640
FIELDS = 2 * LEV + 1
EDGES = FIELDS + LEV // 2
SPLIT = 4
BANDS = 32
F32, BF16, I32 = jnp.float32, jnp.bfloat16, jnp.int32


def sds(*shape):
    return jax.ShapeDtypeStruct(shape, F32)


def call(kernel, out_shape, name, scratch=(), flops=100000, nbytes=1000000):
    return pl.pallas_call(
        kernel,
        out_shape=out_shape,
        scratch_shapes=list(scratch),
        name=name,
        cost_estimate=pl.CostEstimate(flops=flops, bytes_accessed=nbytes, transcendentals=0),
        compiler_params=pltpu.CompilerParams(vmem_limit_bytes=48 << 20),
    )


def tile_iota(dim):
    return lax.broadcasted_iota(I32, (8, 128), dim)


def wide_iota(width, dim):
    return lax.broadcasted_iota(I32, (8, width), dim)


def pair_edges(first, second):
    low = wide_iota(COLS, 0) < HALO
    head = jnp.where(low, first[0], pltpu.roll(second[0], HALO, 0))
    tail = jnp.where(low, pltpu.roll(first[1], HALO, 0), second[1])
    return head, tail


def put_edges(whole, paired, head_ref, tail_ref, mirror_ref):
    sub, lane = tile_iota(0), tile_iota(1)
    tiles = whole + [pair_edges(*two) for two in paired]
    for p, (head, tail) in enumerate(tiles):
        head_ref[p] = head
        tail_ref[p] = tail

    @pl.when((lax.axis_index("comp") == 1) & (lax.axis_index("lat") == BANDS - 1))
    def _():
        for p in range(len(tiles)):
            for k in range(4):
                x = tail_ref[p, :, (3 - k) * 128 : (4 - k) * 128]
                for bit in (1, 2, 4) if p < len(whole) else (1, 2):
                    x = jnp.where((sub & bit) == bit, pltpu.roll(x, bit, 0), pltpu.roll(x, 8 - bit, 0))
                mirror_ref[p, :, k * 128 : (k + 1) * 128] = jnp.take_along_axis(
                    x, 127 - lane, axis=1
                )


def taker(from_south_ref, from_north_ref, from_fold_ref):
    ocean = lax.axis_index("comp") == 1
    band = lax.axis_index("lat")
    first, last = band == 0, band == BANDS - 1
    zero = jnp.zeros((8, COLS), F32)

    def take(p):
        north = jnp.where(last, jnp.where(ocean, from_fold_ref[p], zero), from_north_ref[p])
        return north, jnp.where(first, zero, from_south_ref[p])

    return take


def split_pair(north, south):
    low = wide_iota(COLS, 0) < HALO
    return (
        jnp.where(low, north, pltpu.roll(south, HALO, 0)),
        jnp.where(low, pltpu.roll(north, HALO, 0), south),
    )


def put_columns(tiles, tile_rows, width, east_ref, west_ref, base=0):
    lane = tile_iota(1)
    for t in range(tile_rows):
        east = jnp.zeros((8, 128), F32)
        west = jnp.zeros((8, 128), F32)
        for f, tile in enumerate(tiles):
            here = (lane >= width * f) & (lane < width * (f + 1))
            x = tile(t)
            if x is None:
                continue
            first, last = x[:, 0:128], x[:, COLS - 128 : COLS]
            west = jnp.where(here, first if f == 0 else pltpu.roll(first, width * f, 1), west)
            shift = (width * f + width) % 128
            east = jnp.where(here, pltpu.roll(last, shift, 1) if shift else last, east)
        east_ref[8 * t : 8 * t + 8, base : base + 128] = east
        west_ref[8 * t : 8 * t + 8, base : base + 128] = west


def side_column(f, width, from_west, from_east):
    lane = lax.broadcasted_iota(I32, from_west.shape, 1)
    east = pltpu.roll(from_east, lax.rem(128 - width * f, 128), 1)
    west = pltpu.roll(from_west, lax.rem(256 - width - width * f, 128), 1)
    return jnp.where(lane < width, east, jnp.where(lane >= 128 - width, west, jnp.zeros_like(east)))


def narrow(x):
    low = lax.broadcasted_iota(I32, (8, x.shape[1]), 0) < HALO
    return jnp.concatenate([x[0:16], jnp.where(low, x[16:24], x[24:32])], axis=0)


def extend(main, halo, side):
    return jnp.concatenate([jnp.concatenate([main, halo], axis=0), side], axis=1)


def to_east(x):
    return pltpu.roll(x, XC - 1, 1)


def to_west(x):
    return pltpu.roll(x, 1, 1)


def to_north(x):
    return pltpu.roll(x, x.shape[0] - 1, 0)


def to_south(x):
    return pltpu.roll(x, 1, 0)


def sweep(f, c_east, c_north):
    c_west, c_south = to_west(c_east), to_south(c_north)
    for _ in range(NSTEP):
        change = c_east * (to_east(f) - f) + c_west * (to_west(f) - f)
        change = change + c_south * (to_south(f) - f)
        change = change + c_north * (to_north(f) - f)
        f = f + change
    return f


def first_pack(inc_ref, diff_ref, innov_ref, land_ref, head_ref, tail_ref, mirror_ref, mask_ref):
    ocean = lax.axis_index("comp") == 1
    mask = jnp.where(ocean, land_ref[...].astype(F32), jnp.ones((ROWS, COLS), F32))
    mask_ref[...] = mask

    def rows(ref, l):
        return ref[l, 0:8, :], ref[l, 8:16, :]

    whole = [rows(inc_ref, l) for l in range(LEV)] + [rows(diff_ref, l) for l in range(LEV)]
    whole.append((mask[0:8], mask[8:16]))
    paired = [
        (rows(innov_ref, l), rows(innov_ref, min(l + 1, LEV - 1))) for l in range(1, LEV, 2)
    ]
    put_edges(whole, paired, head_ref, tail_ref, mirror_ref)


def first_columns(
    inc_ref, diff_ref, innov_ref, mask_ref, from_south_ref, from_north_ref, from_fold_ref,
    halo_ref, innov_halo_ref, east_ref, west_ref,
):
    take = taker(from_south_ref, from_north_ref, from_fold_ref)
    for f in range(FIELDS):
        north, south = take(f)
        halo_ref[f, 0:8, :] = north
        halo_ref[f, 8:16, :] = south
    for p in range(LEV // 2):
        one, two = split_pair(*take(FIELDS + p))
        innov_halo_ref[2 * p] = one
        innov_halo_ref[2 * p + 1] = two

    def field(f):
        def tile(t):
            if t >= 2:
                return halo_ref[f, 8 * t - 16 : 8 * t - 8, :]
            rows = slice(8 * t, 8 * t + 8)
            if f < LEV:
                return inc_ref[f, rows, :]
            if f < 2 * LEV:
                return diff_ref[f - LEV, rows, :]
            return mask_ref[rows, :]

        return tile

    def innov(l):
        def tile(t):
            if t >= 2:
                return innov_halo_ref[l - 1] if t == 2 else None
            return innov_ref[l, 8 * t : 8 * t + 8, :]

        return tile

    put_columns([field(f) for f in range(16)], 4, WIDE, east_ref, west_ref)
    put_columns(
        [field(16)] + [innov(l) for l in range(1, LEV)], 4, WIDE, east_ref, west_ref, 128
    )


def start_level(l, inc_ref, diff_ref, mask_ref, halo_ref, from_west_ref, from_east_ref, shape):
    sides = from_west_ref[:, 0:128], from_east_ref[:, 0:128]
    other = from_west_ref[:, 128:256], from_east_ref[:, 128:256]
    mask = shape(extend(mask_ref[...], halo_ref[2 * LEV], side_column(0, WIDE, *other)))
    diff = shape(extend(diff_ref[l], halo_ref[LEV + l], side_column(LEV + l, WIDE, *sides)))
    f = shape(extend(inc_ref[l], halo_ref[l], side_column(l, WIDE, *sides)))
    c_east = mask * to_east(mask) * 0.5 * (diff + to_east(diff))
    c_north = mask * to_north(mask) * 0.5 * (diff + to_north(diff))
    return f, c_east, c_north


def first_surface(
    inc_ref, diff_ref, mask_ref, halo_ref, from_west_ref, from_east_ref,
    state_ref, surface_ref, c_east_ref, c_north_ref,
):
    f, c_east, c_north = start_level(
        0, inc_ref, diff_ref, mask_ref, halo_ref, from_west_ref, from_east_ref, narrow
    )
    c_east_ref[...] = c_east
    c_north_ref[...] = c_north
    f = sweep(f, c_east, c_north)[:ROWS, :COLS]
    state_ref[...] = f
    surface_ref[...] = mask_ref[...] * f


def rest_levels(low, high):
    def kernel(
        inc_ref, diff_ref, innov_ref, mask_ref, halo_ref, innov_halo_ref, from_west_ref,
        from_east_ref, *refs,
    ):
        state_ref, gradient_ref = refs[-2:]
        other = from_west_ref[0:XR, 128:256], from_east_ref[0:XR, 128:256]

        def level(l, carry):
            f, c_east, c_north = start_level(
                l, inc_ref, diff_ref, mask_ref, halo_ref, from_west_ref, from_east_ref, lambda x: x
            )
            f = narrow(sweep(f, c_east, c_north))
            state_ref[l] = f[:ROWS, :COLS]
            innov = extend(innov_ref[l], innov_halo_ref[l - 1], side_column(l, WIDE, *other))
            f = sweep(f - innov, narrow(c_east), narrow(c_north))
            gradient_ref[l] = f[:ROWS, :COLS] + inc_ref[l]
            return carry

        lax.fori_loop(low, high, level, 0)
        if len(refs) == 4:
            old_state_ref, old_gradient_ref = refs[:2]
            state_ref[1:low] = old_state_ref[1:low]
            gradient_ref[1:low] = old_gradient_ref[1:low]

    return kernel


def row_of(ref):
    return lambda h: ref[h // 4 : h // 4 + 1, (h % 4) * 128 : (h % 4) * 128 + 128]


def gather_slots(table, cells):
    high, low = lax.shift_right_logical(cells, 7), cells & 127
    found = jnp.zeros((8, 128), F32)
    for h in range(64):
        row = jnp.broadcast_to(table(h), (8, 128))
        found = jnp.where(high == h, jnp.take_along_axis(row, low, axis=1), found)
    return found


GROUP = 8
SUMS = 4


def gather_all(cells_ref, table_ref, store):
    def group(g, carry):
        for n in range(GROUP):
            b = g * GROUP + n
            store(b, gather_slots(row_of(table_ref), cells_ref[b]))
        return carry

    lax.fori_loop(0, BANDS // GROUP, group, 0)


def gather_kernel(cells_ref, table_ref, out_ref):
    def store(b, found):
        out_ref[b] = found

    gather_all(cells_ref, table_ref, store)


def scatter_band(cells, values):
    high_iota = lax.broadcasted_iota(I32, (64, 128), 0)
    low_iota = lax.broadcasted_iota(I32, (128, 128), 0)
    high, low = lax.shift_right_logical(cells, 7), cells & 127
    coarse = values.astype(BF16).astype(F32)
    fine = values - coarse
    left, right = [], []
    for k in range(8):
        at = high_iota == high[k : k + 1]
        a = jnp.where(at, coarse[k : k + 1], 0.0).astype(BF16)
        b = jnp.where(at, fine[k : k + 1], 0.0).astype(BF16)
        left.append(jnp.concatenate([a, b], axis=0))
        right.append(jnp.where(low_iota == low[k : k + 1], 1.0, 0.0).astype(BF16))
    return lax.dot_general(
        jnp.concatenate(left, axis=1),
        jnp.concatenate(right, axis=1),
        (((1,), (1,)), ((), ())),
        preferred_element_type=F32,
    )


def as_block(sums):
    return jnp.concatenate([sums.reshape(ROWS, 4, 128)[:, k, :] for k in range(4)], axis=1)


def sum_slots(cells_of, values_of, acc_ref):
    acc_ref[...] = jnp.zeros_like(acc_ref)

    def step(g, carry):
        total = acc_ref[...]
        for n in range(SUMS):
            total = total + scatter_band(cells_of(SUMS * g + n), values_of(SUMS * g + n))
        acc_ref[...] = total
        return carry

    lax.fori_loop(0, BANDS // SUMS, step, 0)
    return as_block(acc_ref[0:64, :] + acc_ref[64:128, :])


def live_of(b, weight_ref, count_ref):
    slot = tile_iota(0) * 128 + tile_iota(1)
    return jnp.where(slot < count_ref[0, b], weight_ref[b], jnp.zeros((8, 128), F32))


def couple_kernel(
    count_ref, values_ref, cells_ref, weight_ref, mask_ref, state_ref, innov_ref,
    linear_ref, residual_ref, out_ref, acc_ref, table_ref,
):
    income = sum_slots(
        lambda b: cells_ref[b], lambda b: live_of(b, weight_ref, count_ref) * values_ref[b], acc_ref
    )
    mask = mask_ref[...]
    linear = state_ref[...] + mask * income
    residual = linear - innov_ref[...]
    linear_ref[...] = linear
    residual_ref[...] = residual
    table_ref[...] = mask * residual

    def store(b, found):
        out_ref[b] = live_of(b, weight_ref, count_ref) * found

    gather_all(cells_ref, table_ref, store)


def collect_kernel(values_ref, cells_ref, out_ref, acc_ref):
    out_ref[...] = sum_slots(lambda b: cells_ref[b], lambda b: values_ref[b], acc_ref)


def second_pack(residual_ref, mask_ref, returned_ref, adj_ref, head_ref, tail_ref, mirror_ref):
    adj = residual_ref[...] + mask_ref[...] * returned_ref[...]
    adj_ref[...] = adj
    edges = adj[0:8], adj[8:16]
    put_edges([], [(edges, edges)], head_ref, tail_ref, mirror_ref)


def second_columns(
    adj_ref, from_south_ref, from_north_ref, from_fold_ref, halo_ref, east_ref, west_ref
):
    halo, _ = split_pair(*taker(from_south_ref, from_north_ref, from_fold_ref)(0))
    halo_ref[...] = halo
    put_columns(
        [lambda t: halo if t == 2 else adj_ref[8 * t : 8 * t + 8, :]], 3, HALO, east_ref, west_ref
    )


def second_surface(
    adj_ref, halo_ref, from_west_ref, from_east_ref, c_east_ref, c_north_ref, inc_ref, linear_ref,
    state_any, gradient_any, state_ref, gradient_ref,
):
    side = side_column(0, HALO, from_west_ref[...], from_east_ref[...])
    f = sweep(extend(adj_ref[...], halo_ref[...], side), c_east_ref[...], c_north_ref[...])
    gradient_ref[0] = f[:ROWS, :COLS] + inc_ref[...]
    state_ref[0] = linear_ref[...]


def across(value):
    return lax.ppermute(value, "comp", [(0, 1), (1, 0)])


def along(head, tail, mirror):
    n, m = lax.axis_size("lat"), lax.axis_size("lon")
    return (
        lax.ppermute(tail, "lat", [(i, (i + 1) % n) for i in range(n)]),
        lax.ppermute(head, "lat", [((i + 1) % n, i) for i in range(n)]),
        lax.ppermute(mirror, "lon", [(i, m - 1 - i) for i in range(m)]),
    )


def around(east, west):
    n = lax.axis_size("lon")
    return (
        lax.ppermute(east, "lon", [(i, (i + 1) % n) for i in range(n)]),
        lax.ppermute(west, "lon", [((i + 1) % n, i) for i in range(n)]),
    )


def exchange(slots):
    return lax.all_to_all(slots, "lat", 0, 0, tiled=True)


def local(
    increment, diffusivity, innovation, land_mask, pull_cells, put_cells, pull_weight, pull_count
):
    inc, diff, innov = increment[0], diffusivity[0], innovation[0]
    placed = put_cells.reshape(BANDS, 8, 128)
    weight = pull_weight.reshape(BANDS, 8, 128)
    count = pull_count.reshape(1, BANDS)
    plane = sds(ROWS, COLS)
    field = sds(LEV, ROWS, COLS)
    slots = sds(BANDS, 8, 128)
    smem = pl.BlockSpec(memory_space=pltpu.SMEM)
    vmem = pl.BlockSpec(memory_space=pltpu.VMEM)
    params = pltpu.CompilerParams(vmem_limit_bytes=48 << 20)

    edge = sds(EDGES, 8, COLS)
    *edges, mask = call(first_pack, (edge, edge, edge, plane), "first_pack")(
        inc, diff, innov, land_mask
    )
    cells, *edges = lax.optimization_barrier((pull_cells.reshape(BANDS, 8, 128), *edges))
    pulled = exchange(cells)
    packed = sds(32, 256)
    halo, innov_halo, east, west = call(
        first_columns, (sds(FIELDS, 16, COLS), sds(LEV, 8, COLS), packed, packed), "first_columns"
    )(inc, diff, innov, mask, *along(*edges))
    from_west, from_east = around(east, west)
    wide = sds(XR, XC)
    state0, surface, c_east, c_north = call(
        first_surface, (plane, plane, wide, wide), "first_surface"
    )(inc, diff, mask, halo, from_west, from_east)
    sent = call(gather_kernel, slots, "gather_slots")(pulled, across(surface))

    sent, halo = lax.optimization_barrier((sent, halo))
    values = exchange(sent)
    shared = (inc, diff, innov, mask)
    rest = call(rest_levels(1, SPLIT), (field, field), "rest_one", nbytes=10000000)(
        *shared, halo, innov_halo, from_west, from_east
    )

    values, *rest = lax.optimization_barrier((values, *rest))
    acc = pltpu.VMEM((128, 128), F32)
    linear, residual, outgoing = pl.pallas_call(
        couple_kernel,
        out_shape=(plane, plane, slots),
        in_specs=[smem] + [vmem] * 6,
        out_specs=(vmem,) * 3,
        scratch_shapes=[acc, pltpu.VMEM((ROWS, COLS), F32)],
        name="couple",
        compiler_params=params,
    )(count, values, placed, weight, mask, state0, innov[0])

    outgoing, *rest = lax.optimization_barrier((outgoing, *rest))
    back = exchange(outgoing)
    rest = pl.pallas_call(
        rest_levels(SPLIT, LEV),
        out_shape=(field, field),
        in_specs=[vmem] * 10,
        out_specs=(vmem,) * 2,
        input_output_aliases={8: 0, 9: 1},
        name="rest_two",
        cost_estimate=pl.CostEstimate(flops=100000, bytes_accessed=14000000, transcendentals=0),
        compiler_params=params,
    )(*shared, halo, innov_halo, from_west, from_east, *rest)

    back, *rest = lax.optimization_barrier((back, *rest))
    returned = across(call(collect_kernel, plane, "collect", [acc])(back, pulled))
    edge = sds(1, 8, COLS)
    adj, *edges = call(second_pack, (plane, edge, edge, edge), "second_pack")(
        residual, mask, returned
    )
    packed = sds(XR, 128)
    halo, east, west = call(second_columns, (sds(8, COLS), packed, packed), "second_columns")(
        adj, *along(*edges)
    )
    from_west, from_east = around(east, west)
    top = pl.BlockSpec((1, ROWS, COLS), lambda i: (0, 0, 0))
    whole = pl.BlockSpec(memory_space=pl.ANY)

    def full(*shape):
        return pl.BlockSpec(shape, lambda i: (0,) * len(shape))

    state, gradient = pl.pallas_call(
        second_surface,
        out_shape=(field, field),
        grid=(1,),
        in_specs=[
            full(ROWS, COLS), full(8, COLS), full(XR, 128), full(XR, 128), full(XR, XC),
            full(XR, XC), full(ROWS, COLS), full(ROWS, COLS), whole, whole,
        ],
        out_specs=(top, top),
        input_output_aliases={8: 0, 9: 1},
        name="second_surface",
        compiler_params=params,
    )(adj, halo, from_west, from_east, c_east, c_north, inc[0], linear, *rest)
    return (state[None], gradient[None])


def solution(mesh):
    placed = (
        P("comp", None, "lat", "lon"),
        P("comp", None, "lat", "lon"),
        P("comp", None, "lat", "lon"),
        P("lat", "lon"),
        P("comp", "lat", "lon", None, None),
        P("comp", "lat", "lon", None, None),
        P("comp", "lat", "lon", None, None),
        P("comp", "lat", "lon", None),
    )
    return jax.shard_map(
        local,
        mesh=mesh,
        in_specs=placed,
        out_specs=(P("comp", None, "lat", "lon"), P("comp", None, "lat", "lon")),
        check_vma=False,
    )
```

time: 106 us -> 98.5 us (0.929)
  blocking collectives: 17.8 us -> 0 us
  waiting for transfers between devices: 13.6 us -> 29 us
  Pallas kernels: 16.2 us -> 25.3 us
  starting transfers between devices: 46.2 us -> 37.1 us
  local copies, waits for them, and re-layouts: 11.3 us -> 5.88 us
    all_to_all x1 -> x0, blocking collectives: 17.8 us -> none  [exchange(): return lax.all_to_all(slots, 'lat', 0, 0, tiled=True)]
    all_to_all x2 -> x3, waiting for transfers between devices: 0.11 us -> 11.1 us  [exchange(): return lax.all_to_all(slots, 'lat', 0, 0, tiled=True)]
    pallas_call x7, Pallas kernels: 8.76 us -> 17.8 us  [the longest x1 7.5 us: local(): pl.pallas_call(couple_kernel, out_shape=(plane, plane, slots), in_specs=[...]
    pallas_call x1 -> x0, local copies, waits for them, and re-layouts: 7.32 us -> none  [local(): pl.pallas_call(couple_kernel, out_shape=(plane, plane, slots), in_specs=[...]
    ppermute x3 -> x2, waiting for transfers between devices: 0.85 us -> 5.38 us  [along(): lax.ppermute(mirror, 'lon', [(i, m - 1 - i) for i in range(m)])]
    ppermute x3 -> x2, starting transfers between devices: 3.68 us -> 0.48 us  [along(): lax.ppermute(mirror, 'lon', [(i, m - 1 - i) for i in range(m)])]
    ppermute x3 -> x2, starting transfers between devices: 3.39 us -> 0.58 us  [around(): lax.ppermute(east, 'lon', [(i, (i + 1) % n) for i in range(n)])]
    ppermute x3 -> x2, waiting for transfers between devices: 5.03 us -> 3.02 us  [along(): lax.ppermute(tail, 'lat', [(i, (i + 1) % n) for i in range(n)])]
  transfers between devices with their start and end apart: 19 -> 15, of which waited for: 9 -> 13; matrix products, arithmetic and copies ran while one was open for 7% -> 0% of each run, Pallas kernels for 8% -> 10%
where the time goes in v3:
time: 98.5 us; the launch traced here: 98.1 us
  starting transfers between devices  37.1 us (38%)
  waiting for transfers between devices  29 us (29%)
  Pallas kernels  25.3 us (26%)
  local copies, waits for them, and re-layouts  5.88 us (6%)
    all_to_all x3, starting transfers between devices, exchange(): return lax.all_to_all(slots, 'lat', 0, 0, tiled=True)  18.4 us
    all_to_all x3, waiting for transfers between devices, exchange(): return lax.all_to_all(slots, 'lat', 0, 0, tiled=True)  11.1 us
    ppermute x2, starting transfers between devices, along(): lax.ppermute(head, 'lat', [((i + 1) % n, i) for i in range(n)])  10.7 us
    pallas_call x1, Pallas kernels, local(): pl.pallas_call(couple_kernel, out_shape=(plane, plane, slots), in_specs=[...  7.5 us
    unnamed x21, local copies, waits for them, and re-layouts  5.87 us
    pallas_call x1, Pallas kernels, local(): pl.pallas_call(rest_levels(SPLIT, LEV), out_shape=(field, field), in_spec...  5.5 us
    ppermute x2, waiting for transfers between devices, along(): lax.ppermute(mirror, 'lon', [(i, m - 1 - i) for i in range(m)])  5.38 us
    pallas_call x1, Pallas kernels, local(): call(collect_kernel, plane, 'collect', [acc])(back, pulled)  3.73 us
  transfers between devices with their start and end apart: 15, of which 13 were waited for; matrix products, arithmetic and copies ran while one was open for 0% of the time, Pallas kernels for 10%

profile of v3, /device:TPU:6, one launch (start us, length us, event | category | flops | bytes accessed | tf_op | source)
XLA Modules:
  0.0 98.1 jit_solution(14672707081752117022)
XLA Ops:
  0.6 1.6 %copy.14 = s32[4,8,8,128]{3,2,1,0:T(8,128)} copy(s32[4,8,8,128]{3,1,2,0:T(8,128)} %bitcast.41) | data formatting | bytes 262144
  2.3 0.9 copy-done.1
  3.2 0.9 copy-done.3
  4.2 0.8 copy-done.5
  5.0 2.0 %collective-permute-start = (f32[21,8,512]{2,1,0:T(8,128)S(1)}, f32[21,8,512]{2,1,0:T(8,128)S(1)}, u32[]{:S(2)}, u32[]{:S(2)}) collective-permute-start(f32[21,8,512]{2,1,0:T(8,128)S(1)} %get-tuple-element.50), channel_id=1, source_target_pairs={{0,4},{4,8},{8,12},{12,16},{16,20},{20,24},{24,28},{28,32},{32,36}... | collective-permute-start | bytes 1032200 | tf_op jit(solution)/shard_map/ppermute | solution.py:395
  7.0 6.5 %collective-permute-start.1 = (f32[21,8,512]{2,1,0:T(8,128)S(1)}, f32[21,8,512]{2,1,0:T(8,128)S(1)}, u32[]{:S(2)}, u32[]{:S(2)}) collective-permute-start(f32[21,8,512]{2,1,0:T(8,128)S(1)} %get-tuple-element.51), channel_id=1, source_target_pairs={{4,0},{8,4},{12,8},{16,12},{20,16},{24,20},{28,24},{32,28},{36,32}... | collective-permute-start | bytes 1032200 | tf_op jit(solution)/shard_map/ppermute | solution.py:396
  14.0 6.3 %all-to-all-start = ((s32[32,8,128]{2,1,0:T(8,128)}), s32[32,8,128]{2,1,0:T(8,128)S(1)}, u32[]{:S(2)}, u32[]{:S(2)}) async-start(s32[32,8,128]{2,1,0:T(8,128)} %bitcast.11), calls=%async_computation | async-start | bytes 262144 | tf_op jit(solution)/shard_map/all_to_all | solution.py:410
  20.3 1.3 %collective-permute-done.from_south_ref = f32[21,8,512]{2,1,0:T(8,128)S(1)} collective-permute-done((f32[21,8,512]{2,1,0:T(8,128)S(1)}, f32[21,8,512]{2,1,0:T(8,128)S(1)}, u32[]{:S(2)}, u32[]{:S(2)}) %collective-permute-start) | collective-permute-done | bytes 344096 | tf_op jit(solution)/shard_map/ppermute | solution.py:395
  22.2 2.1 %collective-permute-done.2.from_fold_ref = f32[21,8,512]{2,1,0:T(8,128)S(1)} collective-permute-done((f32[21,8,512]{2,1,0:T(8,128)S(1)}, f32[21,8,512]{2,1,0:T(8,128)S(1)}, u32[]{:S(2)}, u32[]{:S(2)}) %collective-permute-start.2) | collective-permute-done | bytes 344096 | tf_op jit(solution)/shard_map/ppermute | solution.py:397
  25.2 1.5 %collective-permute-start.4 = (f32[32,256]{1,0:T(8,128)S(1)}, f32[32,256]{1,0:T(8,128)S(1)}, u32[]{:S(2)}, u32[]{:S(2)}) collective-permute-start(f32[32,256]{1,0:T(8,128)S(1)} %get-tuple-element.55), channel_id=1, source_target_pairs={{1,0},{2,1},{3,2},{0,3},{5,4},{6,5},{7,6},{4,7},{9,8},{10,9},{11,1... | collective-permute-start | bytes 98312 | tf_op jit(solution)/shard_map/ppermute | solution.py:405
  26.7 1.9 %collective-permute-done.3.from_west_ref = f32[32,256]{1,0:T(8,128)S(1)} collective-permute-done((f32[32,256]{1,0:T(8,128)S(1)}, f32[32,256]{1,0:T(8,128)S(1)}, u32[]{:S(2)}, u32[]{:S(2)}) %collective-permute-start.3) | collective-permute-done | bytes 32800 | tf_op jit(solution)/shard_map/ppermute | solution.py:404
  28.6 1.7 %collective-permute-done.4.from_east_ref = f32[32,256]{1,0:T(8,128)S(1)} collective-permute-done((f32[32,256]{1,0:T(8,128)S(1)}, f32[32,256]{1,0:T(8,128)S(1)}, u32[]{:S(2)}, u32[]{:S(2)}) %collective-permute-start.4) | collective-permute-done | bytes 32800 | tf_op jit(solution)/shard_map/ppermute | solution.py:405
  30.9 1.2 %collective-permute-done.5.table_ref = f32[16,512]{1,0:T(8,128)S(1)} collective-permute-done((f32[16,512]{1,0:T(8,128)S(1)}, f32[16,512]{1,0:T(8,128)S(1)}, u32[]{:S(2)}, u32[]{:S(2)}) %collective-permute-start.5) | collective-permute-done | bytes 32800 | tf_op jit(solution)/shard_map/ppermute | solution.py:389
  32.1 3.2 %gather_slots.1 = f32[32,8,128]{2,1,0:T(8,128)} custom-call(s32[32,8,128]{2,1,0:T(8,128)S(1)} %all-to-all-done.cells_ref, f32[16,512]{1,0:T(8,128)S(1)} %collective-permute-done.5.table_ref), custom_call_target="tpu_custom_call" | custom-call | flops 100000 | bytes 1000000 | tf_op jit(solution)/shard_map/gather_slots/pallas_call | solution.py:442
  35.3 8.2 %all-to-all-start.1 = ((f32[32,8,128]{2,1,0:T(8,128)}), f32[32,8,128]{2,1,0:T(8,128)S(1)}, u32[]{:S(2)}, u32[]{:S(2)}) async-start(f32[32,8,128]{2,1,0:T(8,128)} %gather_slots.1), calls=%async_computation.1 | async-start | bytes 262144 | tf_op jit(solution)/shard_map/all_to_all | solution.py:410
  43.5 0.9 copy-done.8
  44.4 3.5 %rest_one.1 = (f32[8,16,512]{2,1,0:T(8,128)}, f32[8,16,512]{2,1,0:T(8,128)}) custom-call(f32[8,16,512]{2,1,0:T(8,128)S(1)} %bitcast.25, f32[8,16,512]{2,1,0:T(8,128)S(1)} %bitcast.30, f32[8,16,512]{2,1,0:T(8,128)S(1)} %bitcast.34, f32[16,512]{1,0:T(8,128)S(1)} %get-tuple-element.49.mask_ref, f32[17,16,512]{2,1,0:T(8,128)S(1)} %get-tuple-element.58.halo_ref, ...), custom_call_target="tpu_custom_call" | custom-call | flops 100000 | bytes 10000000 | tf_op jit(solution)/shard_map/rest_one/pallas_call | solution.py:447
  47.9 6.2 %all-to-all-done.1.values_ref = f32[32,8,128]{2,1,0:T(8,128)S(1)} async-done(((f32[32,8,128]{2,1,0:T(8,128)}), f32[32,8,128]{2,1,0:T(8,128)S(1)}, u32[]{:S(2)}, u32[]{:S(2)}) %all-to-all-start.1) | async-done | bytes 131104 | tf_op jit(solution)/shard_map/all_to_all | solution.py:410
  54.7 7.5 %couple.1 = (f32[16,512]{1,0:T(8,128)S(1)}, f32[16,512]{1,0:T(8,128)S(1)}, f32[32,8,128]{2,1,0:T(8,128)}) custom-call(s32[1,32]{1,0:T(1,128)S(1)} %bitcast.38, f32[32,8,128]{2,1,0:T(8,128)S(1)} %all-to-all-done.1.values_ref, s32[32,8,128]{2,1,0:T(8,128)S(1)} %bitcast.36, f32[32,8,128]{2,1,0:T(8,128)S(1)} %bitcast.37, ...), custom_call_target="tpu_custom_call" | custom-call | tf_op jit(solution)/shard_map/couple/pallas_call | solution.py:453
  62.2 3.9 %all-to-all-start.2 = ((f32[32,8,128]{2,1,0:T(8,128)}), f32[32,8,128]{2,1,0:T(8,128)S(1)}, u32[]{:S(2)}, u32[]{:S(2)}) async-start(f32[32,8,128]{2,1,0:T(8,128)} %get-tuple-element.68), calls=%async_computation.2 | async-start | bytes 262144 | tf_op jit(solution)/shard_map/all_to_all | solution.py:410
  66.1 5.5 %rest_two.1 = (f32[8,16,512]{2,1,0:T(8,128)}, f32[8,16,512]{2,1,0:T(8,128)}) custom-call(f32[8,16,512]{2,1,0:T(8,128)S(1)} %bitcast.26, f32[8,16,512]{2,1,0:T(8,128)S(1)} %bitcast.31, f32[8,16,512]{2,1,0:T(8,128)S(1)} %bitcast.35, f32[16,512]{1,0:T(8,128)S(1)} %get-tuple-element.49.mask_ref, ...), custom_call_target="tpu_custom_call", output_to_operand_aliasing={{0}: (8, {}), {1}: (9, {})} | custom-call | flops 100000 | bytes 14000000 | tf_op jit(solution)/shard_map/rest_two/pallas_call | solution.py:465
  71.6 4.9 %all-to-all-done.2.values_ref = f32[32,8,128]{2,1,0:T(8,128)S(1)} async-done(((f32[32,8,128]{2,1,0:T(8,128)}), f32[32,8,128]{2,1,0:T(8,128)S(1)}, u32[]{:S(2)}, u32[]{:S(2)}) %all-to-all-start.2) | async-done | bytes 131104 | tf_op jit(solution)/shard_map/all_to_all | solution.py:410
  76.5 3.7 %collect.1 = f32[16,512]{1,0:T(8,128)S(1)} custom-call(f32[32,8,128]{2,1,0:T(8,128)S(1)} %all-to-all-done.2.values_ref, s32[32,8,128]{2,1,0:T(8,128)S(1)} %all-to-all-done.cells_ref), custom_call_target="tpu_custom_call" | custom-call | flops 100000 | bytes 1000000 | tf_op jit(solution)/shard_map/collect/pallas_call | solution.py:477
  80.3 1.2 %collective-permute-done.6.returned_ref = f32[16,512]{1,0:T(8,128)S(1)} collective-permute-done((f32[16,512]{1,0:T(8,128)S(1)}, f32[16,512]{1,0:T(8,128)S(1)}, u32[]{:S(2)}, u32[]{:S(2)}) %collective-permute-start.6) | collective-permute-done | bytes 32800 | tf_op jit(solution)/shard_map/ppermute | solution.py:389
  81.6 1.2 %collective-permute-start.7 = (f32[1,8,512]{2,1,0:T(8,128)S(1)}, f32[1,8,512]{2,1,0:T(8,128)S(1)}, u32[]{:S(2)}, u32[]{:S(2)}) collective-permute-start(f32[1,8,512]{2,1,0:T(8,128)S(1)} %get-tuple-element.75), channel_id=1, source_target_pairs={{0,4},{4,8},{8,12},{12,16},{16,20},{20,24},{24,28},{28,32},{32,36}... | collective-permute-start | bytes 49160 | tf_op jit(solution)/shard_map/ppermute | solution.py:395
  82.8 4.2 %collective-permute-start.8 = (f32[1,8,512]{2,1,0:T(8,128)S(1)}, f32[1,8,512]{2,1,0:T(8,128)S(1)}, u32[]{:S(2)}, u32[]{:S(2)}) collective-permute-start(f32[1,8,512]{2,1,0:T(8,128)S(1)} %get-tuple-element.76), channel_id=1, source_target_pairs={{4,0},{8,4},{12,8},{16,12},{20,16},{24,20},{28,24},{32,28},{36,32}... | collective-permute-start | bytes 49160 | tf_op jit(solution)/shard_map/ppermute | solution.py:396
  87.0 1.7 %collective-permute-done.7.from_south_ref = f32[1,8,512]{2,1,0:T(8,128)S(1)} collective-permute-done((f32[1,8,512]{2,1,0:T(8,128)S(1)}, f32[1,8,512]{2,1,0:T(8,128)S(1)}, u32[]{:S(2)}, u32[]{:S(2)}) %collective-permute-start.7) | collective-permute-done | bytes 16416 | tf_op jit(solution)/shard_map/ppermute | solution.py:395
  88.7 3.2 %collective-permute-done.9.from_fold_ref = f32[1,8,512]{2,1,0:T(8,128)S(1)} collective-permute-done((f32[1,8,512]{2,1,0:T(8,128)S(1)}, f32[1,8,512]{2,1,0:T(8,128)S(1)}, u32[]{:S(2)}, u32[]{:S(2)}) %collective-permute-start.9) | collective-permute-done | bytes 16416 | tf_op jit(solution)/shard_map/ppermute | solution.py:397
  92.0 2.0 %collective-permute-start.11 = (f32[24,128]{1,0:T(8,128)S(1)}, f32[24,128]{1,0:T(8,128)S(1)}, u32[]{:S(2)}, u32[]{:S(2)}) collective-permute-start(f32[24,128]{1,0:T(8,128)S(1)} %get-tuple-element.80), channel_id=1, source_target_pairs={{1,0},{2,1},{3,2},{0,3},{5,4},{6,5},{7,6},{4,7},{9,8},{10,9},{11,1... | collective-permute-start | bytes 36872 | tf_op jit(solution)/shard_map/ppermute | solution.py:405
  94.1 1.7 %collective-permute-done.10.from_west_ref = f32[24,128]{1,0:T(8,128)S(1)} collective-permute-done((f32[24,128]{1,0:T(8,128)S(1)}, f32[24,128]{1,0:T(8,128)S(1)}, u32[]{:S(2)}, u32[]{:S(2)}) %collective-permute-start.10) | collective-permute-done | bytes 12320 | tf_op jit(solution)/shard_map/ppermute | solution.py:404
  95.7 1.3 %collective-permute-done.11.from_east_ref = f32[24,128]{1,0:T(8,128)S(1)} collective-permute-done((f32[24,128]{1,0:T(8,128)S(1)}, f32[24,128]{1,0:T(8,128)S(1)}, u32[]{:S(2)}, u32[]{:S(2)}) %collective-permute-start.11) | collective-permute-done | bytes 12320 | tf_op jit(solution)/shard_map/ppermute | solution.py:405
  97.0 1.0 %second_surface.1 = (f32[8,16,512]{2,1,0:T(8,128)}, f32[8,16,512]{2,1,0:T(8,128)}) custom-call(f32[16,512]{1,0:T(8,128)S(1)} %get-tuple-element.74.adj_ref, f32[8,512]{1,0:T(8,128)S(1)} %get-tuple-element.78.halo_ref, f32[24,128]{1,0:T(8,128)S(1)} %collective-permute-done.10.from_west_ref, ...), custom_call_target="tpu_custom_call", output_to_operand_aliasing={{0}: (8, {}), {1}: (9, {})} | custom-call | tf_op jit(solution)/shard_map/second_surface/pallas_call | solution.py:493
  (32 shorter events, 3.5 us)
Async XLA Ops:
  0.6 1.6 %copy-start = (f32[1,8,16,512]{3,2,1,0:T(8,128)S(1)}, f32[1,8,16,512]{3,2,1,0:T(8,128)}, u32[]{:S(2)}) copy-start(f32[1,8,16,512]{3,2,1,0:T(8,128)} %param.8) | copy-start | bytes 786436
  2.3 1.0 copy-start.1
  3.2 0.9 copy-start.3
  4.2 0.8 copy-start.5
  4.9 19.4 %copy-start.4 = (f32[1,8,16,512]{3,2,1,0:T(8,128)S(1)}, f32[1,8,16,512]{3,2,1,0:T(8,128)}, u32[]{:S(2)}) copy-start(f32[1,8,16,512]{3,2,1,0:T(8,128)} %param.10) | copy-start | bytes 786436
  5.0 19.4 %copy-start.2 = (f32[1,8,16,512]{3,2,1,0:T(8,128)S(1)}, f32[1,8,16,512]{3,2,1,0:T(8,128)}, u32[]{:S(2)}) copy-start(f32[1,8,16,512]{3,2,1,0:T(8,128)} %param.9) | copy-start | bytes 786436
  5.0 16.6 %collective-permute-start = (f32[21,8,512]{2,1,0:T(8,128)S(1)}, f32[21,8,512]{2,1,0:T(8,128)S(1)}, u32[]{:S(2)}, u32[]{:S(2)}) collective-permute-start(f32[21,8,512]{2,1,0:T(8,128)S(1)} %get-tuple-element.50), channel_id=1, source_target_pairs={{0,4},{4,8},{8,12},{12,16},{16,20},{20,24},{24,28},{28,32},{32,36}... | collective-permute-start | bytes 1032200 | tf_op jit(solution)/shard_map/ppermute | solution.py:395
  7.0 15.2 %collective-permute-start.1 = (f32[21,8,512]{2,1,0:T(8,128)S(1)}, f32[21,8,512]{2,1,0:T(8,128)S(1)}, u32[]{:S(2)}, u32[]{:S(2)}) collective-permute-start(f32[21,8,512]{2,1,0:T(8,128)S(1)} %get-tuple-element.51), channel_id=1, source_target_pairs={{4,0},{8,4},{12,8},{16,12},{20,16},{24,20},{28,24},{32,28},{36,32}... | collective-permute-start | bytes 1032200 | tf_op jit(solution)/shard_map/ppermute | solution.py:396
  13.5 10.9 %collective-permute-start.2 = (f32[21,8,512]{2,1,0:T(8,128)S(1)}, f32[21,8,512]{2,1,0:T(8,128)S(1)}, u32[]{:S(2)}, u32[]{:S(2)}) collective-permute-start(f32[21,8,512]{2,1,0:T(8,128)S(1)} %get-tuple-element.52), channel_id=1, source_target_pairs={{0,3},{1,2},{2,1},{3,0},{4,7},{5,6},{6,5},{7,4},{8,11},{9,10},{10,... | collective-permute-start | bytes 1032200 | tf_op jit(solution)/shard_map/ppermute | solution.py:397
  14.0 16.9 %all-to-all-start = ((s32[32,8,128]{2,1,0:T(8,128)}), s32[32,8,128]{2,1,0:T(8,128)S(1)}, u32[]{:S(2)}, u32[]{:S(2)}) async-start(s32[32,8,128]{2,1,0:T(8,128)} %bitcast.11), calls=%async_computation | async-start | bytes 262144 | tf_op jit(solution)/shard_map/all_to_all | solution.py:410
  24.6 4.0 %collective-permute-start.3 = (f32[32,256]{1,0:T(8,128)S(1)}, f32[32,256]{1,0:T(8,128)S(1)}, u32[]{:S(2)}, u32[]{:S(2)}) collective-permute-start(f32[32,256]{1,0:T(8,128)S(1)} %get-tuple-element.54), channel_id=1, source_target_pairs={{0,1},{1,2},{2,3},{3,0},{4,5},{5,6},{6,7},{7,4},{8,9},{9,10},{10,1... | collective-permute-start | bytes 98312 | tf_op jit(solution)/shard_map/ppermute | solution.py:404
  25.2 5.1 %collective-permute-start.4 = (f32[32,256]{1,0:T(8,128)S(1)}, f32[32,256]{1,0:T(8,128)S(1)}, u32[]{:S(2)}, u32[]{:S(2)}) collective-permute-start(f32[32,256]{1,0:T(8,128)S(1)} %get-tuple-element.55), channel_id=1, source_target_pairs={{1,0},{2,1},{3,2},{0,3},{5,4},{6,5},{7,6},{4,7},{9,8},{10,9},{11,1... | collective-permute-start | bytes 98312 | tf_op jit(solution)/shard_map/ppermute | solution.py:405
  30.8 1.3 %collective-permute-start.5 = (f32[16,512]{1,0:T(8,128)S(1)}, f32[16,512]{1,0:T(8,128)S(1)}, u32[]{:S(2)}, u32[]{:S(2)}) collective-permute-start(f32[16,512]{1,0:T(8,128)S(1)} %get-tuple-element.56), channel_id=1, source_target_pairs={{0,128},{128,0},{1,129},{129,1},{2,130},{130,2},{3,131},{131,3},{4... | collective-permute-start | bytes 98312 | tf_op jit(solution)/shard_map/ppermute | solution.py:389
  35.3 8.2 %copy-start.7 = (s32[1,1,1,32,1024]{4,3,2,1,0:T(8,128)S(1)}, s32[1,1,1,32,1024]{4,3,2,1,0:T(8,128)}, u32[]{:S(2)}) copy-start(s32[1,1,1,32,1024]{4,3,2,1,0:T(8,128)} %param.13) | copy-start | bytes 393220
  35.3 18.8 %all-to-all-start.1 = ((f32[32,8,128]{2,1,0:T(8,128)}), f32[32,8,128]{2,1,0:T(8,128)S(1)}, u32[]{:S(2)}, u32[]{:S(2)}) async-start(f32[32,8,128]{2,1,0:T(8,128)} %gather_slots.1), calls=%async_computation.1 | async-start | bytes 262144 | tf_op jit(solution)/shard_map/all_to_all | solution.py:410
  43.5 0.9 copy-start.8
  54.1 0.7 copy-start.6
  62.2 14.3 %all-to-all-start.2 = ((f32[32,8,128]{2,1,0:T(8,128)}), f32[32,8,128]{2,1,0:T(8,128)S(1)}, u32[]{:S(2)}, u32[]{:S(2)}) async-start(f32[32,8,128]{2,1,0:T(8,128)} %get-tuple-element.68), calls=%async_computation.2 | async-start | bytes 262144 | tf_op jit(solution)/shard_map/all_to_all | solution.py:410
  80.2 1.3 %collective-permute-start.6 = (f32[16,512]{1,0:T(8,128)S(1)}, f32[16,512]{1,0:T(8,128)S(1)}, u32[]{:S(2)}, u32[]{:S(2)}) collective-permute-start(f32[16,512]{1,0:T(8,128)S(1)} %collect.1), channel_id=1, source_target_pairs={{0,128},{128,0},{1,129},{129,1},{2,130},{130,2},{3,131},{131,3},{4... | collective-permute-start | bytes 98312 | tf_op jit(solution)/shard_map/ppermute | solution.py:389
  81.6 7.1 %collective-permute-start.7 = (f32[1,8,512]{2,1,0:T(8,128)S(1)}, f32[1,8,512]{2,1,0:T(8,128)S(1)}, u32[]{:S(2)}, u32[]{:S(2)}) collective-permute-start(f32[1,8,512]{2,1,0:T(8,128)S(1)} %get-tuple-element.75), channel_id=1, source_target_pairs={{0,4},{4,8},{8,12},{12,16},{16,20},{20,24},{24,28},{28,32},{32,36}... | collective-permute-start | bytes 49160 | tf_op jit(solution)/shard_map/ppermute | solution.py:395
  82.8 5.9 %collective-permute-start.8 = (f32[1,8,512]{2,1,0:T(8,128)S(1)}, f32[1,8,512]{2,1,0:T(8,128)S(1)}, u32[]{:S(2)}, u32[]{:S(2)}) collective-permute-start(f32[1,8,512]{2,1,0:T(8,128)S(1)} %get-tuple-element.76), channel_id=1, source_target_pairs={{4,0},{8,4},{12,8},{16,12},{20,16},{24,20},{28,24},{32,28},{36,32}... | collective-permute-start | bytes 49160 | tf_op jit(solution)/shard_map/ppermute | solution.py:396
  87.0 4.9 %collective-permute-start.9 = (f32[1,8,512]{2,1,0:T(8,128)S(1)}, f32[1,8,512]{2,1,0:T(8,128)S(1)}, u32[]{:S(2)}, u32[]{:S(2)}) collective-permute-start(f32[1,8,512]{2,1,0:T(8,128)S(1)} %get-tuple-element.77), channel_id=1, source_target_pairs={{0,3},{1,2},{2,1},{3,0},{4,7},{5,6},{6,5},{7,4},{8,11},{9,10},{10,... | collective-permute-start | bytes 49160 | tf_op jit(solution)/shard_map/ppermute | solution.py:397
  92.0 3.7 %collective-permute-start.10 = (f32[24,128]{1,0:T(8,128)S(1)}, f32[24,128]{1,0:T(8,128)S(1)}, u32[]{:S(2)}, u32[]{:S(2)}) collective-permute-start(f32[24,128]{1,0:T(8,128)S(1)} %get-tuple-element.79), channel_id=1, source_target_pairs={{0,1},{1,2},{2,3},{3,0},{4,5},{5,6},{6,7},{7,4},{8,9},{9,10},{10,1... | collective-permute-start | bytes 36872 | tf_op jit(solution)/shard_map/ppermute | solution.py:404
  92.0 5.0 %collective-permute-start.11 = (f32[24,128]{1,0:T(8,128)S(1)}, f32[24,128]{1,0:T(8,128)S(1)}, u32[]{:S(2)}, u32[]{:S(2)}) collective-permute-start(f32[24,128]{1,0:T(8,128)S(1)} %get-tuple-element.80), channel_id=1, source_target_pairs={{1,0},{2,1},{3,2},{0,3},{5,4},{6,5},{7,6},{4,7},{9,8},{10,9},{11,1... | collective-permute-start | bytes 36872 | tf_op jit(solution)/shard_map/ppermute | solution.py:405

commit v4 on v3

--- a/solution.py
+++ b/solution.py
@@ -12,7 +12,7 @@
 FIELDS = 2 * LEV + 1
 EDGES = FIELDS + LEV // 2
 SPLIT = 4
-BANDS = 32
+BANDS, CAP = 32, 1024
 F32, BF16, I32 = jnp.float32, jnp.bfloat16, jnp.int32
 
 
@@ -46,19 +46,15 @@
     return head, tail
 
 
-def put_edges(whole, paired, head_ref, tail_ref, mirror_ref):
+def mirror_edges(whole, tiles, tail_ref, mirror_ref):
     sub, lane = tile_iota(0), tile_iota(1)
-    tiles = whole + [pair_edges(*two) for two in paired]
-    for p, (head, tail) in enumerate(tiles):
-        head_ref[p] = head
-        tail_ref[p] = tail
 
     @pl.when((lax.axis_index("comp") == 1) & (lax.axis_index("lat") == BANDS - 1))
     def _():
-        for p in range(len(tiles)):
+        for p in range(tiles):
             for k in range(4):
                 x = tail_ref[p, :, (3 - k) * 128 : (4 - k) * 128]
-                for bit in (1, 2, 4) if p < len(whole) else (1, 2):
+                for bit in (1, 2, 4) if p < whole else (1, 2):
                     x = jnp.where((sub & bit) == bit, pltpu.roll(x, bit, 0), pltpu.roll(x, 8 - bit, 0))
                 mirror_ref[p, :, k * 128 : (k + 1) * 128] = jnp.take_along_axis(
                     x, 127 - lane, axis=1
@@ -146,20 +142,60 @@
     return f
 
 
-def first_pack(inc_ref, diff_ref, innov_ref, land_ref, head_ref, tail_ref, mirror_ref, mask_ref):
+def first_pack(
+    inc_hbm, diff_hbm, innov_hbm, land_hbm, head_ref, tail_ref, mirror_ref, mask_ref,
+    other_mask_ref, innov_ref, land_ref, sem,
+):
+    copies = []
+
+    def fetch(source, target):
+        copies.append(pltpu.make_async_copy(source, target, sem.at[len(copies)]))
+        copies[-1].start()
+
+    for base, source in ((0, inc_hbm), (LEV, diff_hbm)):
+        fetch(source.at[:, 0:8, :], head_ref.at[base : base + LEV])
+        fetch(source.at[:, 8:16, :], tail_ref.at[base : base + LEV])
+    fetch(innov_hbm.at[0:4], innov_ref.at[0:4])
+    fetch(innov_hbm.at[4:8], innov_ref.at[4:8])
+    fetch(land_hbm, land_ref)
+    for copy in copies:
+        copy.wait()
+
     ocean = lax.axis_index("comp") == 1
-    mask = jnp.where(ocean, land_ref[...].astype(F32), jnp.ones((ROWS, COLS), F32))
+    land = land_ref[...].astype(F32)
+    ones = jnp.ones((ROWS, COLS), F32)
+    mask = jnp.where(ocean, land, ones)
     mask_ref[...] = mask
-
-    def rows(ref, l):
-        return ref[l, 0:8, :], ref[l, 8:16, :]
-
-    whole = [rows(inc_ref, l) for l in range(LEV)] + [rows(diff_ref, l) for l in range(LEV)]
-    whole.append((mask[0:8], mask[8:16]))
-    paired = [
-        (rows(innov_ref, l), rows(innov_ref, min(l + 1, LEV - 1))) for l in range(1, LEV, 2)
-    ]
-    put_edges(whole, paired, head_ref, tail_ref, mirror_ref)
+    other_mask_ref[...] = jnp.where(ocean, ones, land)
+    head_ref[2 * LEV] = mask[0:8]
+    tail_ref[2 * LEV] = mask[8:16]
+    for p in range(LEV // 2):
+        one, two = 2 * p + 1, min(2 * p + 2, LEV - 1)
+        head, tail = pair_edges(
+            (innov_ref[one, 0:8], innov_ref[one, 8:16]), (innov_ref[two, 0:8], innov_ref[two, 8:16])
+        )
+        head_ref[FIELDS + p] = head
+        tail_ref[FIELDS + p] = tail
+    mirror_edges(FIELDS, EDGES, tail_ref, mirror_ref)
+
+
+def regroup(x):
+    return x.reshape(8, 8, 128)
+
+
+def regroup_kernel(cells_ref, out_ref):
+    for g in range(BANDS // 8):
+        out_ref[8 * g : 8 * g + 8] = regroup(cells_ref[8 * g : 8 * g + 8, :])
+
+
+def receive_kernel(count_ref, cells_ref, weight_ref, out_ref):
+    for g in range(BANDS // 8):
+        rows = slice(8 * g, 8 * g + 8)
+        out_ref[0, rows] = regroup(weight_ref[rows, :])
+        out_ref[1, rows] = regroup(cells_ref[rows, :].astype(F32))
+    slot = tile_iota(0) * 128 + tile_iota(1)
+    for b in range(BANDS):
+        out_ref[0, b] = jnp.where(slot < count_ref[0, b], out_ref[0, b], 0.0)
 
 
 def first_columns(
@@ -215,7 +251,7 @@
 
 
 def first_surface(
-    inc_ref, diff_ref, mask_ref, halo_ref, from_west_ref, from_east_ref,
+    inc_ref, diff_ref, innov_ref, mask_ref, halo_ref, from_west_ref, from_east_ref,
     state_ref, surface_ref, c_east_ref, c_north_ref,
 ):
     f, c_east, c_north = start_level(
@@ -224,7 +260,8 @@
     c_east_ref[...] = c_east
     c_north_ref[...] = c_north
     f = sweep(f, c_east, c_north)[:ROWS, :COLS]
-    state_ref[...] = f
+    state_ref[0] = f
+    state_ref[1] = innov_ref[0]
     surface_ref[...] = mask_ref[...] * f
 
 
@@ -270,14 +307,14 @@
 
 
 GROUP = 8
-SUMS = 4
-
-
-def gather_all(cells_ref, table_ref, store):
+SUMS = 8
+
+
+def gather_all(cells_of, table_ref, store):
     def group(g, carry):
         for n in range(GROUP):
             b = g * GROUP + n
-            store(b, gather_slots(row_of(table_ref), cells_ref[b]))
+            store(b, gather_slots(row_of(table_ref), cells_of(b)))
         return carry
 
     lax.fori_loop(0, BANDS // GROUP, group, 0)
@@ -287,22 +324,26 @@
     def store(b, found):
         out_ref[b] = found
 
-    gather_all(cells_ref, table_ref, store)
+    gather_all(lambda b: cells_ref[b], table_ref, store)
 
 
 def scatter_band(cells, values):
-    high_iota = lax.broadcasted_iota(I32, (64, 128), 0)
-    low_iota = lax.broadcasted_iota(I32, (128, 128), 0)
-    high, low = lax.shift_right_logical(cells, 7), cells & 127
+    high_iota = lax.broadcasted_iota(I32, (64, 128), 0).astype(F32).astype(BF16)
+    low_iota = lax.broadcasted_iota(I32, (128, 128), 0).astype(F32).astype(BF16)
+    high, low = lax.shift_right_logical(cells, 7).astype(F32), (cells & 127).astype(F32)
     coarse = values.astype(BF16).astype(F32)
     fine = values - coarse
+    zero, one = jnp.zeros((16, 128), BF16), jnp.ones((16, 128), BF16)
     left, right = [], []
     for k in range(8):
-        at = high_iota == high[k : k + 1]
-        a = jnp.where(at, coarse[k : k + 1], 0.0).astype(BF16)
-        b = jnp.where(at, fine[k : k + 1], 0.0).astype(BF16)
-        left.append(jnp.concatenate([a, b], axis=0))
-        right.append(jnp.where(low_iota == low[k : k + 1], 1.0, 0.0).astype(BF16))
+        h, l, a, b = (
+            jnp.broadcast_to(x[k : k + 1], (16, 128)).astype(BF16) for x in (high, low, coarse, fine)
+        )
+        at = [high_iota[t : t + 16] == h for t in range(0, 64, 16)]
+        parts = [jnp.where(here, x, zero) for x in (a, b) for here in at]
+        left.append(jnp.concatenate(parts, axis=0))
+        parts = [jnp.where(low_iota[t : t + 16] == l, one, zero) for t in range(0, 128, 16)]
+        right.append(jnp.concatenate(parts, axis=0))
     return lax.dot_general(
         jnp.concatenate(left, axis=1),
         jnp.concatenate(right, axis=1),
@@ -329,40 +370,37 @@
     return as_block(acc_ref[0:64, :] + acc_ref[64:128, :])
 
 
-def live_of(b, weight_ref, count_ref):
-    slot = tile_iota(0) * 128 + tile_iota(1)
-    return jnp.where(slot < count_ref[0, b], weight_ref[b], jnp.zeros((8, 128), F32))
-
-
 def couple_kernel(
-    count_ref, values_ref, cells_ref, weight_ref, mask_ref, state_ref, innov_ref,
-    linear_ref, residual_ref, out_ref, acc_ref, table_ref,
-):
-    income = sum_slots(
-        lambda b: cells_ref[b], lambda b: live_of(b, weight_ref, count_ref) * values_ref[b], acc_ref
-    )
+    values_ref, slots_ref, mask_ref, state_ref, linear_ref, out_ref, acc_ref, table_ref
+):
+    def cells(b):
+        return slots_ref[1, b].astype(I32)
+
+    income = sum_slots(cells, lambda b: slots_ref[0, b] * values_ref[b], acc_ref)
     mask = mask_ref[...]
-    linear = state_ref[...] + mask * income
-    residual = linear - innov_ref[...]
-    linear_ref[...] = linear
-    residual_ref[...] = residual
+    linear = state_ref[0] + mask * income
+    residual = linear - state_ref[1]
+    linear_ref[0] = linear
+    linear_ref[1] = residual
     table_ref[...] = mask * residual
 
     def store(b, found):
-        out_ref[b] = live_of(b, weight_ref, count_ref) * found
-
-    gather_all(cells_ref, table_ref, store)
+        out_ref[b] = slots_ref[0, b] * found
+
+    gather_all(cells, table_ref, store)
 
 
 def collect_kernel(values_ref, cells_ref, out_ref, acc_ref):
     out_ref[...] = sum_slots(lambda b: cells_ref[b], lambda b: values_ref[b], acc_ref)
 
 
-def second_pack(residual_ref, mask_ref, returned_ref, adj_ref, head_ref, tail_ref, mirror_ref):
-    adj = residual_ref[...] + mask_ref[...] * returned_ref[...]
+def second_pack(linear_ref, mask_ref, returned_ref, adj_ref, head_ref, tail_ref, mirror_ref):
+    adj = linear_ref[1] + mask_ref[...] * returned_ref[...]
     adj_ref[...] = adj
-    edges = adj[0:8], adj[8:16]
-    put_edges([], [(edges, edges)], head_ref, tail_ref, mirror_ref)
+    head, tail = pair_edges((adj[0:8], adj[8:16]), (adj[0:8], adj[8:16]))
+    head_ref[0] = head
+    tail_ref[0] = tail
+    mirror_edges(0, 1, tail_ref, mirror_ref)
 
 
 def second_columns(
@@ -381,8 +419,8 @@
 ):
     side = side_column(0, HALO, from_west_ref[...], from_east_ref[...])
     f = sweep(extend(adj_ref[...], halo_ref[...], side), c_east_ref[...], c_north_ref[...])
-    gradient_ref[0] = f[:ROWS, :COLS] + inc_ref[...]
-    state_ref[0] = linear_ref[...]
+    gradient_ref[0] = f[:ROWS, :COLS] + inc_ref[0]
+    state_ref[0] = linear_ref[0]
 
 
 def across(value):
@@ -414,54 +452,77 @@
     increment, diffusivity, innovation, land_mask, pull_cells, put_cells, pull_weight, pull_count
 ):
     inc, diff, innov = increment[0], diffusivity[0], innovation[0]
-    placed = put_cells.reshape(BANDS, 8, 128)
-    weight = pull_weight.reshape(BANDS, 8, 128)
-    count = pull_count.reshape(1, BANDS)
     plane = sds(ROWS, COLS)
+    pair = sds(2, ROWS, COLS)
     field = sds(LEV, ROWS, COLS)
     slots = sds(BANDS, 8, 128)
     smem = pl.BlockSpec(memory_space=pltpu.SMEM)
     vmem = pl.BlockSpec(memory_space=pltpu.VMEM)
+    whole = pl.BlockSpec(memory_space=pl.ANY)
     params = pltpu.CompilerParams(vmem_limit_bytes=48 << 20)
+    barrier = lax.optimization_barrier
 
     edge = sds(EDGES, 8, COLS)
-    *edges, mask = call(first_pack, (edge, edge, edge, plane), "first_pack")(
-        inc, diff, innov, land_mask
-    )
-    cells, *edges = lax.optimization_barrier((pull_cells.reshape(BANDS, 8, 128), *edges))
+    *edges, mask, other_mask = pl.pallas_call(
+        first_pack,
+        out_shape=(edge, edge, edge, plane, plane),
+        in_specs=[pl.BlockSpec(memory_space=pltpu.HBM)] * 4,
+        out_specs=(vmem,) * 5,
+        scratch_shapes=[
+            pltpu.VMEM((LEV, ROWS, COLS), F32),
+            pltpu.VMEM((ROWS, COLS), I32),
+            pltpu.SemaphoreType.DMA((7,)),
+        ],
+        name="first_pack",
+        compiler_params=params,
+    )(*(pltpu.with_memory_space_constraint(x, pltpu.HBM) for x in (inc, diff, innov, land_mask)))
+    cells, _ = barrier((across(pull_cells.reshape(BANDS, CAP)), edges[0]))
+    cells = pl.pallas_call(
+        regroup_kernel, out_shape=jax.ShapeDtypeStruct(slots.shape, I32), name="regroup"
+    )(cells)
     pulled = exchange(cells)
     packed = sds(32, 256)
     halo, innov_halo, east, west = call(
         first_columns, (sds(FIELDS, 16, COLS), sds(LEV, 8, COLS), packed, packed), "first_columns"
     )(inc, diff, innov, mask, *along(*edges))
+
+    put, weight, east, west = barrier(
+        (put_cells.reshape(BANDS, CAP), pull_weight.reshape(BANDS, CAP), east, west)
+    )
+    received = across(
+        pl.pallas_call(
+            receive_kernel,
+            out_shape=sds(2, BANDS, 8, 128),
+            in_specs=[smem, vmem, vmem],
+            out_specs=vmem,
+            name="receive",
+            compiler_params=params,
+        )(pull_count.reshape(1, BANDS), put, weight)
+    )
     from_west, from_east = around(east, west)
     wide = sds(XR, XC)
-    state0, surface, c_east, c_north = call(
-        first_surface, (plane, plane, wide, wide), "first_surface"
-    )(inc, diff, mask, halo, from_west, from_east)
-    sent = call(gather_kernel, slots, "gather_slots")(pulled, across(surface))
-
-    sent, halo = lax.optimization_barrier((sent, halo))
+    state, surface, c_east, c_north = call(
+        first_surface, (pair, plane, wide, wide), "first_surface"
+    )(inc, diff, innov, mask, halo, from_west, from_east)
+    sent = call(gather_kernel, slots, "gather_slots")(pulled, surface)
+
+    sent, halo, state = barrier((sent, halo, state))
     values = exchange(sent)
+    state = across(state)
     shared = (inc, diff, innov, mask)
     rest = call(rest_levels(1, SPLIT), (field, field), "rest_one", nbytes=10000000)(
         *shared, halo, innov_halo, from_west, from_east
     )
 
-    values, *rest = lax.optimization_barrier((values, *rest))
+    values, *rest = barrier((values, *rest))
     acc = pltpu.VMEM((128, 128), F32)
-    linear, residual, outgoing = pl.pallas_call(
-        couple_kernel,
-        out_shape=(plane, plane, slots),
-        in_specs=[smem] + [vmem] * 6,
-        out_specs=(vmem,) * 3,
-        scratch_shapes=[acc, pltpu.VMEM((ROWS, COLS), F32)],
-        name="couple",
-        compiler_params=params,
-    )(count, values, placed, weight, mask, state0, innov[0])
-
-    outgoing, *rest = lax.optimization_barrier((outgoing, *rest))
+    linear, outgoing = call(
+        couple_kernel, (pair, slots), "couple", [acc, pltpu.VMEM((ROWS, COLS), F32)]
+    )(values, received, other_mask, state)
+
+    outgoing, linear, *rest = barrier((outgoing, linear, *rest))
     back = exchange(outgoing)
+    linear = across(linear)
     rest = pl.pallas_call(
         rest_levels(SPLIT, LEV),
         out_shape=(field, field),
@@ -473,11 +534,11 @@
         compiler_params=params,
     )(*shared, halo, innov_halo, from_west, from_east, *rest)
 
-    back, *rest = lax.optimization_barrier((back, *rest))
-    returned = across(call(collect_kernel, plane, "collect", [acc])(back, pulled))
+    back, *rest = barrier((back, *rest))
+    returned = call(collect_kernel, plane, "collect", [acc])(back, pulled)
     edge = sds(1, 8, COLS)
     adj, *edges = call(second_pack, (plane, edge, edge, edge), "second_pack")(
-        residual, mask, returned
+        linear, mask, returned
     )
     packed = sds(XR, 128)
     halo, east, west = call(second_columns, (sds(8, COLS), packed, packed), "second_columns")(
@@ -485,7 +546,6 @@
     )
     from_west, from_east = around(east, west)
     top = pl.BlockSpec((1, ROWS, COLS), lambda i: (0, 0, 0))
-    whole = pl.BlockSpec(memory_space=pl.ANY)
 
     def full(*shape):
         return pl.BlockSpec(shape, lambda i: (0,) * len(shape))
@@ -496,13 +556,13 @@
         grid=(1,),
         in_specs=[
             full(ROWS, COLS), full(8, COLS), full(XR, 128), full(XR, 128), full(XR, XC),
-            full(XR, XC), full(ROWS, COLS), full(ROWS, COLS), whole, whole,
+            full(XR, XC), top, top, whole, whole,
         ],
         out_specs=(top, top),
         input_output_aliases={8: 0, 9: 1},
         name="second_surface",
         compiler_params=params,
-    )(adj, halo, from_west, from_east, c_east, c_north, inc[0], linear, *rest)
+    )(adj, halo, from_west, from_east, c_east, c_north, inc, linear, *rest)
     return (state[None], gradient[None])
 
 

time: 98.5 us -> 91.9 us (0.933)
  local copies, waits for them, and re-layouts: 5.88 us -> 0.69 us
  waiting for transfers between devices: 29 us -> 25.1 us
  starting transfers between devices: 37.1 us -> 38.4 us
  Pallas kernels: 25.3 us -> 26.5 us
    unnamed x21 -> x14, local copies, waits for them, and re-layouts: 5.87 us -> 0.69 us
    ppermute x2, starting transfers between devices: 0.58 us -> 2.95 us  [around(): lax.ppermute(east, 'lon', [(i, (i + 1) % n) for i in range(n)])]
    ppermute x2 -> x4, waiting for transfers between devices: 2.38 us -> 0.01 us  [across(): return lax.ppermute(value, 'comp', [(0, 1), (1, 0)])]
    ppermute x2, waiting for transfers between devices: 5.38 us -> 3.24 us  [along(): lax.ppermute(mirror, 'lon', [(i, m - 1 - i) for i in range(m)])]
    ppermute x2, waiting for transfers between devices: 2.99 us -> 4.83 us  [around(): lax.ppermute(west, 'lon', [((i + 1) % n, i) for i in range(n)])]
    all_to_all x3, waiting for transfers between devices: 11.1 us -> 12.9 us  [exchange(): return lax.all_to_all(slots, 'lat', 0, 0, tiled=True)]
    ppermute x2, starting transfers between devices: 3.56 us -> 1.93 us  [around(): lax.ppermute(west, 'lon', [((i + 1) % n, i) for i in range(n)])]
    ppermute x2, waiting for transfers between devices: 3.02 us -> 1.62 us  [along(): lax.ppermute(tail, 'lat', [(i, (i + 1) % n) for i in range(n)])]
  transfers between devices with their start and end apart: 15 -> 17, of which waited for: 13 -> 9; matrix products, arithmetic and copies ran while one was open for 0% -> 0% of each run, Pallas kernels for 10% -> 21%
where the time goes in v4:
time: 91.9 us; the launch traced here: 91.6 us
  starting transfers between devices  38.4 us (42%)
  Pallas kernels  26.5 us (29%)
  waiting for transfers between devices  25.1 us (27%)
    all_to_all x3, starting transfers between devices, exchange(): return lax.all_to_all(slots, 'lat', 0, 0, tiled=True)  18.5 us
    all_to_all x3, waiting for transfers between devices, exchange(): return lax.all_to_all(slots, 'lat', 0, 0, tiled=True)  12.9 us
    ppermute x2, starting transfers between devices, along(): lax.ppermute(head, 'lat', [((i + 1) % n, i) for i in range(n)])  10.6 us
    pallas_call x1, Pallas kernels, local(): call(couple_kernel, (pair, slots), 'couple', [acc, pltpu.VMEM((ROWS, COLS...  6.09 us
    pallas_call x1, Pallas kernels, local(): pl.pallas_call(rest_levels(SPLIT, LEV), out_shape=(field, field), in_spec...  5.51 us
    ppermute x2, waiting for transfers between devices, around(): lax.ppermute(west, 'lon', [((i + 1) % n, i) for i in range(n)])  4.83 us
    ppermute x2, starting transfers between devices, along(): lax.ppermute(tail, 'lat', [(i, (i + 1) % n) for i in range(n)])  3.48 us
    pallas_call x1, Pallas kernels, local(): call(rest_levels(1, SPLIT), (field, field), 'rest_one', nbytes=10000000)  3.48 us
  transfers between devices with their start and end apart: 17, of which 9 were waited for; matrix products, arithmetic and copies ran while one was open for 0% of the time, Pallas kernels for 21%

profile of v4, /device:TPU:6, one launch (start us, length us, event | category | flops | bytes accessed | tf_op | source)
XLA Modules:
  0.0 91.6 jit_solution(13813552854069161742)
XLA Ops:
  0.7 1.3 %first_pack.1 = (f32[21,8,512]{2,1,0:T(8,128)S(1)}, f32[21,8,512]{2,1,0:T(8,128)S(1)}, f32[21,8,512]{2,1,0:T(8,128)S(1)}, f32[16,512]{1,0:T(8,128)S(1)}, f32[16,512]{1,0:T(8,128)S(1)}) custom-call(f32[8,16,512]{2,1,0:T(8,128)} %bitcast.9, f32[8,16,512]{2,1,0:T(8,128)} %bitcast.15, f32[8,16,512]{2,1,0:T(8,128)} %bitcast.20, s32[16,512]{1,0:T(8,128)} %land_hbm.1), custom_call_target="tpu_custom_call" | custom-call | tf_op jit(solution)/shard_map/first_pack/pallas_call | solution.py:466
  2.1 2.0 %collective-permute-start.1 = (f32[21,8,512]{2,1,0:T(8,128)S(1)}, f32[21,8,512]{2,1,0:T(8,128)S(1)}, u32[]{:S(2)}, u32[]{:S(2)}) collective-permute-start(f32[21,8,512]{2,1,0:T(8,128)S(1)} %get-tuple-element.51), channel_id=1, source_target_pairs={{0,4},{4,8},{8,12},{12,16},{16,20},{20,24},{24,28},{28,32},{32,36}... | collective-permute-start | bytes 1032200 | tf_op jit(solution)/shard_map/ppermute | solution.py:433
  4.1 0.5 collective-permute-start.3
  4.6 6.5 %collective-permute-start.2 = (f32[21,8,512]{2,1,0:T(8,128)S(1)}, f32[21,8,512]{2,1,0:T(8,128)S(1)}, u32[]{:S(2)}, u32[]{:S(2)}) collective-permute-start(f32[21,8,512]{2,1,0:T(8,128)S(1)} %get-tuple-element.48), channel_id=1, source_target_pairs={{4,0},{8,4},{12,8},{16,12},{20,16},{24,20},{28,24},{32,28},{36,32}... | collective-permute-start | bytes 1032200 | tf_op jit(solution)/shard_map/ppermute | solution.py:434
  11.1 0.7 copy-done.6
  11.7 1.6 %regroup.1 = s32[32,8,128]{2,1,0:T(8,128)} custom-call(s32[32,1024]{1,0:T(8,128)} %copy-done.6), custom_call_target="tpu_custom_call" | custom-call | tf_op jit(solution)/shard_map/regroup/pallas_call | solution.py:480
  13.3 6.3 %all-to-all-start = ((s32[32,8,128]{2,1,0:T(8,128)}), s32[32,8,128]{2,1,0:T(8,128)S(1)}, u32[]{:S(2)}, u32[]{:S(2)}) async-start(s32[32,8,128]{2,1,0:T(8,128)} %regroup.1), calls=%async_computation | async-start | bytes 262144 | tf_op jit(solution)/shard_map/all_to_all | solution.py:448
  19.7 0.2 first_columns.1
  19.9 2.8 %collective-permute-start.4 = (f32[32,256]{1,0:T(8,128)S(1)}, f32[32,256]{1,0:T(8,128)S(1)}, u32[]{:S(2)}, u32[]{:S(2)}) collective-permute-start(f32[32,256]{1,0:T(8,128)S(1)} %get-tuple-element.56), channel_id=1, source_target_pairs={{0,1},{1,2},{2,3},{3,0},{4,5},{5,6},{6,7},{7,4},{8,9},{9,10},{10,1... | collective-permute-start | bytes 98312 | tf_op jit(solution)/shard_map/ppermute | solution.py:442
  22.8 0.6 receive.1
  23.5 0.9 collective-permute-done.4.from_west_ref
  24.4 3.5 %collective-permute-done.5.from_east_ref = f32[32,256]{1,0:T(8,128)S(1)} collective-permute-done((f32[32,256]{1,0:T(8,128)S(1)}, f32[32,256]{1,0:T(8,128)S(1)}, u32[]{:S(2)}, u32[]{:S(2)}) %collective-permute-start.5) | collective-permute-done | bytes 32800 | tf_op jit(solution)/shard_map/ppermute | solution.py:443
  27.9 0.5 first_surface.1
  28.4 1.5 %all-to-all-done.cells_ref = s32[32,8,128]{2,1,0:T(8,128)S(1)} async-done(((s32[32,8,128]{2,1,0:T(8,128)}), s32[32,8,128]{2,1,0:T(8,128)S(1)}, u32[]{:S(2)}, u32[]{:S(2)}) %all-to-all-start) | async-done | bytes 131104 | tf_op jit(solution)/shard_map/all_to_all | solution.py:448
  29.9 3.2 %gather_slots.1 = f32[32,8,128]{2,1,0:T(8,128)} custom-call(s32[32,8,128]{2,1,0:T(8,128)S(1)} %all-to-all-done.cells_ref, f32[16,512]{1,0:T(8,128)S(1)} %get-tuple-element.58.table_ref), custom_call_target="tpu_custom_call" | custom-call | flops 100000 | bytes 1000000 | tf_op jit(solution)/shard_map/gather_slots/pallas_call | solution.py:507
  33.0 8.3 %all-to-all-start.1 = ((f32[32,8,128]{2,1,0:T(8,128)}), f32[32,8,128]{2,1,0:T(8,128)S(1)}, u32[]{:S(2)}, u32[]{:S(2)}) async-start(f32[32,8,128]{2,1,0:T(8,128)} %gather_slots.1), calls=%async_computation.1 | async-start | bytes 262144 | tf_op jit(solution)/shard_map/all_to_all | solution.py:448
  41.5 3.5 %rest_one.1 = (f32[8,16,512]{2,1,0:T(8,128)}, f32[8,16,512]{2,1,0:T(8,128)}) custom-call(f32[8,16,512]{2,1,0:T(8,128)S(1)} %bitcast.12, f32[8,16,512]{2,1,0:T(8,128)S(1)} %bitcast.18, f32[8,16,512]{2,1,0:T(8,128)S(1)} %bitcast.23, f32[16,512]{1,0:T(8,128)S(1)} %get-tuple-element.50.mask_ref, f32[17,16,512]{2,1,0:T(8,128)S(1)} %get-tuple-element.61.halo_ref, ...), custom_call_target="tpu_custom_call" | custom-call | flops 100000 | bytes 10000000 | tf_op jit(solution)/shard_map/rest_one/pallas_call | solution.py:513
  45.0 6.7 %all-to-all-done.1.values_ref = f32[32,8,128]{2,1,0:T(8,128)S(1)} async-done(((f32[32,8,128]{2,1,0:T(8,128)}), f32[32,8,128]{2,1,0:T(8,128)S(1)}, u32[]{:S(2)}, u32[]{:S(2)}) %all-to-all-start.1) | async-done | bytes 131104 | tf_op jit(solution)/shard_map/all_to_all | solution.py:448
  51.7 6.1 %couple.1 = (f32[2,16,512]{2,1,0:T(8,128)S(1)}, f32[32,8,128]{2,1,0:T(8,128)}) custom-call(f32[32,8,128]{2,1,0:T(8,128)S(1)} %all-to-all-done.1.values_ref, f32[2,32,8,128]{3,2,1,0:T(8,128)S(1)} %collective-permute-done.6.slots_ref, f32[16,512]{1,0:T(8,128)S(1)} %get-tuple-element.68.mask_ref, f32[2,16,512]{2,1,0:T(8,128)S(1)} %collective-permute-done.7.state_ref), custom_call_target="tpu_custom_call" | custom-call | flops 100000 | bytes 1000000 | tf_op jit(solution)/shard_map/couple/pallas_call | solution.py:519
  57.8 3.9 %all-to-all-start.2 = ((f32[32,8,128]{2,1,0:T(8,128)}), f32[32,8,128]{2,1,0:T(8,128)S(1)}, u32[]{:S(2)}, u32[]{:S(2)}) async-start(f32[32,8,128]{2,1,0:T(8,128)} %get-tuple-element.75), calls=%async_computation.2 | async-start | bytes 262144 | tf_op jit(solution)/shard_map/all_to_all | solution.py:448
  61.8 5.5 %rest_two.1 = (f32[8,16,512]{2,1,0:T(8,128)}, f32[8,16,512]{2,1,0:T(8,128)}) custom-call(f32[8,16,512]{2,1,0:T(8,128)S(1)} %bitcast.13, f32[8,16,512]{2,1,0:T(8,128)S(1)} %bitcast.19, f32[8,16,512]{2,1,0:T(8,128)S(1)} %bitcast.24, f32[16,512]{1,0:T(8,128)S(1)} %get-tuple-element.50.mask_ref, ...), custom_call_target="tpu_custom_call", output_to_operand_aliasing={{0}: (8, {}), {1}: (9, {})} | custom-call | flops 100000 | bytes 14000000 | tf_op jit(solution)/shard_map/rest_two/pallas_call | solution.py:526
  67.3 4.7 %all-to-all-done.2.values_ref = f32[32,8,128]{2,1,0:T(8,128)S(1)} async-done(((f32[32,8,128]{2,1,0:T(8,128)}), f32[32,8,128]{2,1,0:T(8,128)S(1)}, u32[]{:S(2)}, u32[]{:S(2)}) %all-to-all-start.2) | async-done | bytes 131104 | tf_op jit(solution)/shard_map/all_to_all | solution.py:448
  71.9 2.9 %collect.1.returned_ref = f32[16,512]{1,0:T(8,128)S(1)} custom-call(f32[32,8,128]{2,1,0:T(8,128)S(1)} %all-to-all-done.2.values_ref, s32[32,8,128]{2,1,0:T(8,128)S(1)} %all-to-all-done.cells_ref), custom_call_target="tpu_custom_call" | custom-call | flops 100000 | bytes 1000000 | tf_op jit(solution)/shard_map/collect/pallas_call | solution.py:538
  74.9 1.5 %collective-permute-start.9 = (f32[1,8,512]{2,1,0:T(8,128)S(1)}, f32[1,8,512]{2,1,0:T(8,128)S(1)}, u32[]{:S(2)}, u32[]{:S(2)}) collective-permute-start(f32[1,8,512]{2,1,0:T(8,128)S(1)} %get-tuple-element.82), channel_id=1, source_target_pairs={{0,4},{4,8},{8,12},{12,16},{16,20},{20,24},{24,28},{28,32},{32,36}... | collective-permute-start | bytes 49160 | tf_op jit(solution)/shard_map/ppermute | solution.py:433
  76.3 4.1 %collective-permute-start.10 = (f32[1,8,512]{2,1,0:T(8,128)S(1)}, f32[1,8,512]{2,1,0:T(8,128)S(1)}, u32[]{:S(2)}, u32[]{:S(2)}) collective-permute-start(f32[1,8,512]{2,1,0:T(8,128)S(1)} %get-tuple-element.83), channel_id=1, source_target_pairs={{4,0},{8,4},{12,8},{16,12},{20,16},{24,20},{28,24},{32,28},{36,32}... | collective-permute-start | bytes 49160 | tf_op jit(solution)/shard_map/ppermute | solution.py:434
  80.6 1.6 %collective-permute-done.9.from_south_ref = f32[1,8,512]{2,1,0:T(8,128)S(1)} collective-permute-done((f32[1,8,512]{2,1,0:T(8,128)S(1)}, f32[1,8,512]{2,1,0:T(8,128)S(1)}, u32[]{:S(2)}, u32[]{:S(2)}) %collective-permute-start.9) | collective-permute-done | bytes 16416 | tf_op jit(solution)/shard_map/ppermute | solution.py:433
  82.2 3.2 %collective-permute-done.11.from_fold_ref = f32[1,8,512]{2,1,0:T(8,128)S(1)} collective-permute-done((f32[1,8,512]{2,1,0:T(8,128)S(1)}, f32[1,8,512]{2,1,0:T(8,128)S(1)}, u32[]{:S(2)}, u32[]{:S(2)}) %collective-permute-start.11) | collective-permute-done | bytes 16416 | tf_op jit(solution)/shard_map/ppermute | solution.py:435
  85.5 0.1 collective-permute-start.12
  85.6 1.9 %collective-permute-start.13 = (f32[24,128]{1,0:T(8,128)S(1)}, f32[24,128]{1,0:T(8,128)S(1)}, u32[]{:S(2)}, u32[]{:S(2)}) collective-permute-start(f32[24,128]{1,0:T(8,128)S(1)} %get-tuple-element.87), channel_id=1, source_target_pairs={{1,0},{2,1},{3,2},{0,3},{5,4},{6,5},{7,6},{4,7},{9,8},{10,9},{11,1... | collective-permute-start | bytes 36872 | tf_op jit(solution)/shard_map/ppermute | solution.py:443
  87.5 1.7 %collective-permute-done.12.from_west_ref = f32[24,128]{1,0:T(8,128)S(1)} collective-permute-done((f32[24,128]{1,0:T(8,128)S(1)}, f32[24,128]{1,0:T(8,128)S(1)}, u32[]{:S(2)}, u32[]{:S(2)}) %collective-permute-start.12) | collective-permute-done | bytes 12320 | tf_op jit(solution)/shard_map/ppermute | solution.py:442
  89.2 1.3 %collective-permute-done.13.from_east_ref = f32[24,128]{1,0:T(8,128)S(1)} collective-permute-done((f32[24,128]{1,0:T(8,128)S(1)}, f32[24,128]{1,0:T(8,128)S(1)}, u32[]{:S(2)}, u32[]{:S(2)}) %collective-permute-start.13) | collective-permute-done | bytes 12320 | tf_op jit(solution)/shard_map/ppermute | solution.py:443
  90.5 1.0 %second_surface.1 = (f32[8,16,512]{2,1,0:T(8,128)}, f32[8,16,512]{2,1,0:T(8,128)}) custom-call(f32[16,512]{1,0:T(8,128)S(1)} %get-tuple-element.81.adj_ref, f32[8,512]{1,0:T(8,128)S(1)} %get-tuple-element.85.halo_ref, f32[24,128]{1,0:T(8,128)S(1)} %collective-permute-done.12.from_west_ref, ...), custom_call_target="tpu_custom_call", output_to_operand_aliasing={{0}: (8, {}), {1}: (9, {})} | custom-call | tf_op jit(solution)/shard_map/second_surface/pallas_call | solution.py:553
  (29 shorter events, 0.6 us)
Async XLA Ops:
  0.6 10.4 %collective-permute-start = (s32[32,1024]{1,0:T(8,128)}, s32[32,1024]{1,0:T(8,128)S(1)}, u32[]{:S(2)}, u32[]{:S(2)}) collective-permute-start(s32[32,1024]{1,0:T(8,128)} %bitcast.30), channel_id=1, source_target_pairs={{0,128},{128,0},{1,129},{129,1},{2,130},{130,2},{3,131},{131,3},{4... | collective-permute-start | bytes 393224 | tf_op jit(solution)/shard_map/ppermute | solution.py:427
  0.7 18.9 %copy-start.2 = (f32[1,8,16,512]{3,2,1,0:T(8,128)S(1)}, f32[1,8,16,512]{3,2,1,0:T(8,128)}, u32[]{:S(2)}) copy-start(f32[1,8,16,512]{3,2,1,0:T(8,128)} %param.10) | copy-start | bytes 786436
  2.1 17.5 %collective-permute-start.1 = (f32[21,8,512]{2,1,0:T(8,128)S(1)}, f32[21,8,512]{2,1,0:T(8,128)S(1)}, u32[]{:S(2)}, u32[]{:S(2)}) collective-permute-start(f32[21,8,512]{2,1,0:T(8,128)S(1)} %get-tuple-element.51), channel_id=1, source_target_pairs={{0,4},{4,8},{8,12},{12,16},{16,20},{20,24},{24,28},{28,32},{32,36}... | collective-permute-start | bytes 1032200 | tf_op jit(solution)/shard_map/ppermute | solution.py:433
  4.1 15.5 %collective-permute-start.3 = (f32[21,8,512]{2,1,0:T(8,128)S(1)}, f32[21,8,512]{2,1,0:T(8,128)S(1)}, u32[]{:S(2)}, u32[]{:S(2)}) collective-permute-start(f32[21,8,512]{2,1,0:T(8,128)S(1)} %get-tuple-element.52), channel_id=1, source_target_pairs={{0,3},{1,2},{2,1},{3,0},{4,7},{5,6},{6,5},{7,4},{8,11},{9,10},{10,... | collective-permute-start | bytes 1032200 | tf_op jit(solution)/shard_map/ppermute | solution.py:435
  4.5 15.1 %copy-start = (f32[1,8,16,512]{3,2,1,0:T(8,128)S(1)}, f32[1,8,16,512]{3,2,1,0:T(8,128)}, u32[]{:S(2)}) copy-start(f32[1,8,16,512]{3,2,1,0:T(8,128)} %param.8) | copy-start | bytes 786436
  4.5 15.1 %copy-start.1 = (f32[1,8,16,512]{3,2,1,0:T(8,128)S(1)}, f32[1,8,16,512]{3,2,1,0:T(8,128)}, u32[]{:S(2)}) copy-start(f32[1,8,16,512]{3,2,1,0:T(8,128)} %param.9) | copy-start | bytes 786436
  4.6 15.1 %collective-permute-start.2 = (f32[21,8,512]{2,1,0:T(8,128)S(1)}, f32[21,8,512]{2,1,0:T(8,128)S(1)}, u32[]{:S(2)}, u32[]{:S(2)}) collective-permute-start(f32[21,8,512]{2,1,0:T(8,128)S(1)} %get-tuple-element.48), channel_id=1, source_target_pairs={{4,0},{8,4},{12,8},{16,12},{20,16},{24,20},{28,24},{32,28},{36,32}... | collective-permute-start | bytes 1032200 | tf_op jit(solution)/shard_map/ppermute | solution.py:434
  11.1 0.7 copy-start.6
  13.3 16.6 %all-to-all-start = ((s32[32,8,128]{2,1,0:T(8,128)}), s32[32,8,128]{2,1,0:T(8,128)S(1)}, u32[]{:S(2)}, u32[]{:S(2)}) async-start(s32[32,8,128]{2,1,0:T(8,128)} %regroup.1), calls=%async_computation | async-start | bytes 262144 | tf_op jit(solution)/shard_map/all_to_all | solution.py:448
  19.7 3.1 %copy-start.3 = (s32[1,1,1,32,1024]{4,3,2,1,0:T(8,128)S(1)}, s32[1,1,1,32,1024]{4,3,2,1,0:T(8,128)}, u32[]{:S(2)}) copy-start(s32[1,1,1,32,1024]{4,3,2,1,0:T(8,128)} %param.13) | copy-start | bytes 393220
  19.7 3.1 %copy-start.4 = (f32[1,1,1,32,1024]{4,3,2,1,0:T(8,128)S(1)}, f32[1,1,1,32,1024]{4,3,2,1,0:T(8,128)}, u32[]{:S(2)}) copy-start(f32[1,1,1,32,1024]{4,3,2,1,0:T(8,128)} %param.14) | copy-start | bytes 393220
  19.9 2.9 %copy-start.5 = (s32[1,1,1,32]{3,2,1,0:T(1,128)S(1)}, s32[1,1,1,32]{3,2,1,0:T(1,128)}, u32[]{:S(2)}) copy-start(s32[1,1,1,32]{3,2,1,0:T(1,128)} %param.15) | copy-start | bytes 388
  19.9 4.4 %collective-permute-start.4 = (f32[32,256]{1,0:T(8,128)S(1)}, f32[32,256]{1,0:T(8,128)S(1)}, u32[]{:S(2)}, u32[]{:S(2)}) collective-permute-start(f32[32,256]{1,0:T(8,128)S(1)} %get-tuple-element.56), channel_id=1, source_target_pairs={{0,1},{1,2},{2,3},{3,0},{4,5},{5,6},{6,7},{7,4},{8,9},{9,10},{10,1... | collective-permute-start | bytes 98312 | tf_op jit(solution)/shard_map/ppermute | solution.py:442
  22.8 5.1 %collective-permute-start.5 = (f32[32,256]{1,0:T(8,128)S(1)}, f32[32,256]{1,0:T(8,128)S(1)}, u32[]{:S(2)}, u32[]{:S(2)}) collective-permute-start(f32[32,256]{1,0:T(8,128)S(1)} %get-tuple-element.57), channel_id=1, source_target_pairs={{1,0},{2,1},{3,2},{0,3},{5,4},{6,5},{7,6},{4,7},{9,8},{10,9},{11,1... | collective-permute-start | bytes 98312 | tf_op jit(solution)/shard_map/ppermute | solution.py:443
  23.4 28.3 %collective-permute-start.6 = (f32[2,32,8,128]{3,2,1,0:T(8,128)S(1)}, f32[2,32,8,128]{3,2,1,0:T(8,128)S(1)}, u32[]{:S(2)}, u32[]{:S(2)}) collective-permute-start(f32[2,32,8,128]{3,2,1,0:T(8,128)S(1)} %receive.1), channel_id=1, source_target_pairs={{0,128},{128,0},{1,129},{129,1},{2,130},{130,2},{3,131},{131,3},{4... | collective-permute-start | bytes 786440 | tf_op jit(solution)/shard_map/ppermute | solution.py:427
  33.0 18.7 %all-to-all-start.1 = ((f32[32,8,128]{2,1,0:T(8,128)}), f32[32,8,128]{2,1,0:T(8,128)S(1)}, u32[]{:S(2)}, u32[]{:S(2)}) async-start(f32[32,8,128]{2,1,0:T(8,128)} %gather_slots.1), calls=%async_computation.1 | async-start | bytes 262144 | tf_op jit(solution)/shard_map/all_to_all | solution.py:448
  41.4 10.3 %collective-permute-start.7 = (f32[2,16,512]{2,1,0:T(8,128)S(1)}, f32[2,16,512]{2,1,0:T(8,128)S(1)}, u32[]{:S(2)}, u32[]{:S(2)}) collective-permute-start(f32[2,16,512]{2,1,0:T(8,128)S(1)} %get-tuple-element.69), channel_id=1, source_target_pairs={{0,128},{128,0},{1,129},{129,1},{2,130},{130,2},{3,131},{131,3},{4... | collective-permute-start | bytes 196616 | tf_op jit(solution)/shard_map/ppermute | solution.py:427
  57.8 14.1 %all-to-all-start.2 = ((f32[32,8,128]{2,1,0:T(8,128)}), f32[32,8,128]{2,1,0:T(8,128)S(1)}, u32[]{:S(2)}, u32[]{:S(2)}) async-start(f32[32,8,128]{2,1,0:T(8,128)} %get-tuple-element.75), calls=%async_computation.2 | async-start | bytes 262144 | tf_op jit(solution)/shard_map/all_to_all | solution.py:448
  61.7 13.2 %collective-permute-start.8 = (f32[2,16,512]{2,1,0:T(8,128)S(1)}, f32[2,16,512]{2,1,0:T(8,128)S(1)}, u32[]{:S(2)}, u32[]{:S(2)}) collective-permute-start(f32[2,16,512]{2,1,0:T(8,128)S(1)} %get-tuple-element.74), channel_id=1, source_target_pairs={{0,128},{128,0},{1,129},{129,1},{2,130},{130,2},{3,131},{131,3},{4... | collective-permute-start | bytes 196616 | tf_op jit(solution)/shard_map/ppermute | solution.py:427
  74.9 7.3 %collective-permute-start.9 = (f32[1,8,512]{2,1,0:T(8,128)S(1)}, f32[1,8,512]{2,1,0:T(8,128)S(1)}, u32[]{:S(2)}, u32[]{:S(2)}) collective-permute-start(f32[1,8,512]{2,1,0:T(8,128)S(1)} %get-tuple-element.82), channel_id=1, source_target_pairs={{0,4},{4,8},{8,12},{12,16},{16,20},{20,24},{24,28},{28,32},{32,36}... | collective-permute-start | bytes 49160 | tf_op jit(solution)/shard_map/ppermute | solution.py:433
  76.3 5.8 %collective-permute-start.10 = (f32[1,8,512]{2,1,0:T(8,128)S(1)}, f32[1,8,512]{2,1,0:T(8,128)S(1)}, u32[]{:S(2)}, u32[]{:S(2)}) collective-permute-start(f32[1,8,512]{2,1,0:T(8,128)S(1)} %get-tuple-element.83), channel_id=1, source_target_pairs={{4,0},{8,4},{12,8},{16,12},{20,16},{24,20},{28,24},{32,28},{36,32}... | collective-permute-start | bytes 49160 | tf_op jit(solution)/shard_map/ppermute | solution.py:434
  80.5 4.9 %collective-permute-start.11 = (f32[1,8,512]{2,1,0:T(8,128)S(1)}, f32[1,8,512]{2,1,0:T(8,128)S(1)}, u32[]{:S(2)}, u32[]{:S(2)}) collective-permute-start(f32[1,8,512]{2,1,0:T(8,128)S(1)} %get-tuple-element.84), channel_id=1, source_target_pairs={{0,3},{1,2},{2,1},{3,0},{4,7},{5,6},{6,5},{7,4},{8,11},{9,10},{10,... | collective-permute-start | bytes 49160 | tf_op jit(solution)/shard_map/ppermute | solution.py:435
  85.5 3.7 %collective-permute-start.12 = (f32[24,128]{1,0:T(8,128)S(1)}, f32[24,128]{1,0:T(8,128)S(1)}, u32[]{:S(2)}, u32[]{:S(2)}) collective-permute-start(f32[24,128]{1,0:T(8,128)S(1)} %get-tuple-element.86), channel_id=1, source_target_pairs={{0,1},{1,2},{2,3},{3,0},{4,5},{5,6},{6,7},{7,4},{8,9},{9,10},{10,1... | collective-permute-start | bytes 36872 | tf_op jit(solution)/shard_map/ppermute | solution.py:442
  85.6 4.9 %collective-permute-start.13 = (f32[24,128]{1,0:T(8,128)S(1)}, f32[24,128]{1,0:T(8,128)S(1)}, u32[]{:S(2)}, u32[]{:S(2)}) collective-permute-start(f32[24,128]{1,0:T(8,128)S(1)} %get-tuple-element.87), channel_id=1, source_target_pairs={{1,0},{2,1},{3,2},{0,3},{5,4},{6,5},{7,6},{4,7},{9,8},{10,9},{11,1... | collective-permute-start | bytes 36872 | tf_op jit(solution)/shard_map/ppermute | solution.py:443

commit v5 on v4

--- a/solution.py
+++ b/solution.py
@@ -11,7 +11,7 @@
 XR, XC = 24, 640
 FIELDS = 2 * LEV + 1
 EDGES = FIELDS + LEV // 2
-SPLIT = 4
+SPLITS = 4, 8
 BANDS, CAP = 32, 1024
 F32, BF16, I32 = jnp.float32, jnp.bfloat16, jnp.int32
 
@@ -143,8 +143,8 @@
 
 
 def first_pack(
-    inc_hbm, diff_hbm, innov_hbm, land_hbm, head_ref, tail_ref, mirror_ref, mask_ref,
-    other_mask_ref, innov_ref, land_ref, sem,
+    inc_hbm, diff_hbm, innov_hbm, land_hbm, cells_hbm, head_ref, tail_ref, mirror_ref, mask_ref,
+    other_mask_ref, slots_ref, innov_ref, land_ref, cells_ref, sem,
 ):
     copies = []
 
@@ -152,13 +152,17 @@
         copies.append(pltpu.make_async_copy(source, target, sem.at[len(copies)]))
         copies[-1].start()
 
+    fetch(cells_hbm, cells_ref)
     for base, source in ((0, inc_hbm), (LEV, diff_hbm)):
         fetch(source.at[:, 0:8, :], head_ref.at[base : base + LEV])
         fetch(source.at[:, 8:16, :], tail_ref.at[base : base + LEV])
     fetch(innov_hbm.at[0:4], innov_ref.at[0:4])
     fetch(innov_hbm.at[4:8], innov_ref.at[4:8])
     fetch(land_hbm, land_ref)
-    for copy in copies:
+    copies[0].wait()
+    for g in range(BANDS // 8):
+        slots_ref[8 * g : 8 * g + 8] = regroup(cells_ref[8 * g : 8 * g + 8, :])
+    for copy in copies[1:]:
         copy.wait()
 
     ocean = lax.axis_index("comp") == 1
@@ -181,11 +185,6 @@
 
 def regroup(x):
     return x.reshape(8, 8, 128)
-
-
-def regroup_kernel(cells_ref, out_ref):
-    for g in range(BANDS // 8):
-        out_ref[8 * g : 8 * g + 8] = regroup(cells_ref[8 * g : 8 * g + 8, :])
 
 
 def receive_kernel(count_ref, cells_ref, weight_ref, out_ref):
@@ -463,24 +462,27 @@
     barrier = lax.optimization_barrier
 
     edge = sds(EDGES, 8, COLS)
-    *edges, mask, other_mask = pl.pallas_call(
+    cells = jax.ShapeDtypeStruct(slots.shape, I32)
+    *edges, mask, other_mask, cells = pl.pallas_call(
         first_pack,
-        out_shape=(edge, edge, edge, plane, plane),
-        in_specs=[pl.BlockSpec(memory_space=pltpu.HBM)] * 4,
-        out_specs=(vmem,) * 5,
+        out_shape=(edge, edge, edge, plane, plane, cells),
+        in_specs=[pl.BlockSpec(memory_space=pltpu.HBM)] * 5,
+        out_specs=(vmem,) * 6,
         scratch_shapes=[
             pltpu.VMEM((LEV, ROWS, COLS), F32),
             pltpu.VMEM((ROWS, COLS), I32),
-            pltpu.SemaphoreType.DMA((7,)),
+            pltpu.VMEM((BANDS, CAP), I32),
+            pltpu.SemaphoreType.DMA((8,)),
         ],
         name="first_pack",
         compiler_params=params,
-    )(*(pltpu.with_memory_space_constraint(x, pltpu.HBM) for x in (inc, diff, innov, land_mask)))
-    cells, _ = barrier((across(pull_cells.reshape(BANDS, CAP)), edges[0]))
-    cells = pl.pallas_call(
-        regroup_kernel, out_shape=jax.ShapeDtypeStruct(slots.shape, I32), name="regroup"
-    )(cells)
-    pulled = exchange(cells)
+    )(
+        *(
+            pltpu.with_memory_space_constraint(x, pltpu.HBM)
+            for x in (inc, diff, innov, land_mask, pull_cells.reshape(BANDS, CAP))
+        )
+    )
+    pulled = exchange(across(cells))
     packed = sds(32, 256)
     halo, innov_halo, east, west = call(
         first_columns, (sds(FIELDS, 16, COLS), sds(LEV, 8, COLS), packed, packed), "first_columns"
@@ -510,7 +512,7 @@
     values = exchange(sent)
     state = across(state)
     shared = (inc, diff, innov, mask)
-    rest = call(rest_levels(1, SPLIT), (field, field), "rest_one", nbytes=10000000)(
+    rest = call(rest_levels(1, SPLITS[0]), (field, field), "rest_one", nbytes=10000000)(
         *shared, halo, innov_halo, from_west, from_east
     )
 
@@ -523,16 +525,21 @@
     outgoing, linear, *rest = barrier((outgoing, linear, *rest))
     back = exchange(outgoing)
     linear = across(linear)
-    rest = pl.pallas_call(
-        rest_levels(SPLIT, LEV),
-        out_shape=(field, field),
-        in_specs=[vmem] * 10,
-        out_specs=(vmem,) * 2,
-        input_output_aliases={8: 0, 9: 1},
-        name="rest_two",
-        cost_estimate=pl.CostEstimate(flops=100000, bytes_accessed=14000000, transcendentals=0),
-        compiler_params=params,
-    )(*shared, halo, innov_halo, from_west, from_east, *rest)
+
+    def more(low, high, name, rest):
+        return pl.pallas_call(
+            rest_levels(low, high),
+            out_shape=(field, field),
+            in_specs=[vmem] * 10,
+            out_specs=(vmem,) * 2,
+            input_output_aliases={8: 0, 9: 1},
+            name=name,
+            cost_estimate=pl.CostEstimate(flops=100000, bytes_accessed=9000000, transcendentals=0),
+            compiler_params=params,
+        )(inc, diff, innov, mask, halo8, innov_halo, west8, east8, *rest)
+
+    halo8, west8, east8 = halo, from_west, from_east
+    rest = more(SPLITS[0], SPLITS[1], "rest_two", rest)
 
     back, *rest = barrier((back, *rest))
     returned = call(collect_kernel, plane, "collect", [acc])(back, pulled)

time: 91.9 us -> 89.7 us (0.976)
  Pallas kernels: 26.5 us -> 25 us
  starting transfers between devices: 38.4 us -> 37 us
  waiting for transfers between devices: 25.1 us -> 26.5 us
    ppermute x2, waiting for transfers between devices: 3.24 us -> 5.64 us  [along(): lax.ppermute(mirror, 'lon', [(i, m - 1 - i) for i in range(m)])]
    ppermute x2, starting transfers between devices: 2.95 us -> 0.66 us  [around(): lax.ppermute(east, 'lon', [(i, (i + 1) % n) for i in range(n)])]
    ppermute x2, waiting for transfers between devices: 4.83 us -> 2.99 us  [around(): lax.ppermute(west, 'lon', [((i + 1) % n, i) for i in range(n)])]
    ppermute x2, waiting for transfers between devices: 1.62 us -> 3.36 us  [along(): lax.ppermute(tail, 'lat', [(i, (i + 1) % n) for i in range(n)])]
    ppermute x2, starting transfers between devices: 1.93 us -> 3.48 us  [around(): lax.ppermute(west, 'lon', [((i + 1) % n, i) for i in range(n)])]
    pallas_call x4 -> x3, Pallas kernels: 11.9 us -> 10.4 us  [the longest x1 5.5 us: more(): pl.pallas_call(rest_levels(low, high), out_shape=(field, field), in_specs...]
    all_to_all x3, waiting for transfers between devices: 12.9 us -> 11.4 us  [exchange(): return lax.all_to_all(slots, 'lat', 0, 0, tiled=True)]
  transfers between devices with their start and end apart: 17 -> 17, of which waited for: 9 -> 11; matrix products, arithmetic and copies ran while one was open for 0% -> 0% of each run, Pallas kernels for 21% -> 18%
where the time goes in v5:
time: 89.7 us; the launch traced here: 89.4 us
  starting transfers between devices  37 us (41%)
  waiting for transfers between devices  26.5 us (30%)
  Pallas kernels  25 us (28%)
    all_to_all x3, starting transfers between devices, exchange(): return lax.all_to_all(slots, 'lat', 0, 0, tiled=True)  17.9 us
    all_to_all x3, waiting for transfers between devices, exchange(): return lax.all_to_all(slots, 'lat', 0, 0, tiled=True)  11.4 us
    ppermute x2, starting transfers between devices, along(): lax.ppermute(head, 'lat', [((i + 1) % n, i) for i in range(n)])  10.6 us
    pallas_call x1, Pallas kernels, local(): call(couple_kernel, (pair, slots), 'couple', [acc, pltpu.VMEM((ROWS, COLS...  6.09 us
    ppermute x2, waiting for transfers between devices, along(): lax.ppermute(mirror, 'lon', [(i, m - 1 - i) for i in range(m)])  5.64 us
    pallas_call x1, Pallas kernels, more(): pl.pallas_call(rest_levels(low, high), out_shape=(field, field), in_specs...  5.5 us
    ppermute x2, starting transfers between devices, around(): lax.ppermute(west, 'lon', [((i + 1) % n, i) for i in range(n)])  3.48 us
    ppermute x2, starting transfers between devices, along(): lax.ppermute(tail, 'lat', [(i, (i + 1) % n) for i in range(n)])  3.48 us
  transfers between devices with their start and end apart: 17, of which 11 were waited for; matrix products, arithmetic and copies ran while one was open for 0% of the time, Pallas kernels for 18%

profile of v5, /device:TPU:6, one launch (start us, length us, event | category | flops | bytes accessed | tf_op | source)
XLA Modules:
  0.0 89.4 jit_solution(5735329084801997532)
XLA Ops:
  0.7 1.4 %first_pack.1 = (f32[21,8,512]{2,1,0:T(8,128)S(1)}, f32[21,8,512]{2,1,0:T(8,128)S(1)}, f32[21,8,512]{2,1,0:T(8,128)S(1)}, f32[16,512]{1,0:T(8,128)S(1)}, f32[16,...) custom-call(f32[8,16,512]{2,1,0:T(8,128)} %bitcast.9, f32[8,16,512]{2,1,0:T(8,128)} %bitcast.15, f32[8,16,512]{2,1,0:T(8,128)} %bitcast.20, ...), custom_call_target="tpu_custom_call" | custom-call | tf_op jit(solution)/shard_map/first_pack/pallas_call | solution.py:466
  2.2 2.0 %collective-permute-start.1 = (f32[21,8,512]{2,1,0:T(8,128)S(1)}, f32[21,8,512]{2,1,0:T(8,128)S(1)}, u32[]{:S(2)}, u32[]{:S(2)}) collective-permute-start(f32[21,8,512]{2,1,0:T(8,128)S(1)} %get-tuple-element.50), channel_id=1, source_target_pairs={{0,4},{4,8},{8,12},{12,16},{16,20},{20,24},{24,28},{28,32},{32,36}... | collective-permute-start | bytes 1032200 | tf_op jit(solution)/shard_map/ppermute | solution.py:432
  4.2 6.5 %collective-permute-start.2 = (f32[21,8,512]{2,1,0:T(8,128)S(1)}, f32[21,8,512]{2,1,0:T(8,128)S(1)}, u32[]{:S(2)}, u32[]{:S(2)}) collective-permute-start(f32[21,8,512]{2,1,0:T(8,128)S(1)} %get-tuple-element.51), channel_id=1, source_target_pairs={{4,0},{8,4},{12,8},{16,12},{20,16},{24,20},{28,24},{32,28},{36,32}... | collective-permute-start | bytes 1032200 | tf_op jit(solution)/shard_map/ppermute | solution.py:433
  10.6 0.5 collective-permute-start.3
  11.1 6.3 %all-to-all-start = ((s32[32,8,128]{2,1,0:T(8,128)}), s32[32,8,128]{2,1,0:T(8,128)S(1)}, u32[]{:S(2)}, u32[]{:S(2)}) async-start(s32[32,8,128]{2,1,0:T(8,128)} %collective-permute-done), calls=%async_computation | async-start | bytes 262144 | tf_op jit(solution)/shard_map/all_to_all | solution.py:447
  17.4 1.7 %collective-permute-done.1.from_south_ref = f32[21,8,512]{2,1,0:T(8,128)S(1)} collective-permute-done((f32[21,8,512]{2,1,0:T(8,128)S(1)}, f32[21,8,512]{2,1,0:T(8,128)S(1)}, u32[]{:S(2)}, u32[]{:S(2)}) %collective-permute-start.1) | collective-permute-done | bytes 344096 | tf_op jit(solution)/shard_map/ppermute | solution.py:432
  19.2 0.3 collective-permute-done.2.from_north_ref
  19.5 2.4 %collective-permute-done.3.from_fold_ref = f32[21,8,512]{2,1,0:T(8,128)S(1)} collective-permute-done((f32[21,8,512]{2,1,0:T(8,128)S(1)}, f32[21,8,512]{2,1,0:T(8,128)S(1)}, u32[]{:S(2)}, u32[]{:S(2)}) %collective-permute-start.3) | collective-permute-done | bytes 344096 | tf_op jit(solution)/shard_map/ppermute | solution.py:434
  21.9 0.2 first_columns.1
  22.2 0.6 collective-permute-start.4
  22.7 1.5 %collective-permute-start.5 = (f32[32,256]{1,0:T(8,128)S(1)}, f32[32,256]{1,0:T(8,128)S(1)}, u32[]{:S(2)}, u32[]{:S(2)}) collective-permute-start(f32[32,256]{1,0:T(8,128)S(1)} %get-tuple-element.57), channel_id=1, source_target_pairs={{1,0},{2,1},{3,2},{0,3},{5,4},{6,5},{7,6},{4,7},{9,8},{10,9},{11,1... | collective-permute-start | bytes 98312 | tf_op jit(solution)/shard_map/ppermute | solution.py:442
  24.3 0.6 receive.1
  25.0 1.2 %collective-permute-done.4.from_west_ref = f32[32,256]{1,0:T(8,128)S(1)} collective-permute-done((f32[32,256]{1,0:T(8,128)S(1)}, f32[32,256]{1,0:T(8,128)S(1)}, u32[]{:S(2)}, u32[]{:S(2)}) %collective-permute-start.4) | collective-permute-done | bytes 32800 | tf_op jit(solution)/shard_map/ppermute | solution.py:441
  26.1 1.7 %collective-permute-done.5.from_east_ref = f32[32,256]{1,0:T(8,128)S(1)} collective-permute-done((f32[32,256]{1,0:T(8,128)S(1)}, f32[32,256]{1,0:T(8,128)S(1)}, u32[]{:S(2)}, u32[]{:S(2)}) %collective-permute-start.5) | collective-permute-done | bytes 32800 | tf_op jit(solution)/shard_map/ppermute | solution.py:442
  27.8 0.5 first_surface.1
  28.3 3.2 %gather_slots.1 = f32[32,8,128]{2,1,0:T(8,128)} custom-call(s32[32,8,128]{2,1,0:T(8,128)S(1)} %all-to-all-done.cells_ref, f32[16,512]{1,0:T(8,128)S(1)} %get-tuple-element.58.table_ref), custom_call_target="tpu_custom_call" | custom-call | flops 100000 | bytes 1000000 | tf_op jit(solution)/shard_map/gather_slots/pallas_call | solution.py:509
  31.5 7.7 %all-to-all-start.1 = ((f32[32,8,128]{2,1,0:T(8,128)}), f32[32,8,128]{2,1,0:T(8,128)S(1)}, u32[]{:S(2)}, u32[]{:S(2)}) async-start(f32[32,8,128]{2,1,0:T(8,128)} %gather_slots.1), calls=%async_computation.1 | async-start | bytes 262144 | tf_op jit(solution)/shard_map/all_to_all | solution.py:447
  39.3 3.5 %rest_one.1 = (f32[8,16,512]{2,1,0:T(8,128)}, f32[8,16,512]{2,1,0:T(8,128)}) custom-call(f32[8,16,512]{2,1,0:T(8,128)S(1)} %bitcast.12, f32[8,16,512]{2,1,0:T(8,128)S(1)} %bitcast.18, f32[8,16,512]{2,1,0:T(8,128)S(1)} %bitcast.23, f32[16,512]{1,0:T(8,128)S(1)} %get-tuple-element.49.mask_ref, f32[17,16,512]{2,1,0:T(8,128)S(1)} %get-tuple-element.61.halo_ref, ...), custom_call_target="tpu_custom_call" | custom-call | flops 100000 | bytes 10000000 | tf_op jit(solution)/shard_map/rest_one/pallas_call | solution.py:515
  42.8 6.7 %all-to-all-done.1.values_ref = f32[32,8,128]{2,1,0:T(8,128)S(1)} async-done(((f32[32,8,128]{2,1,0:T(8,128)}), f32[32,8,128]{2,1,0:T(8,128)S(1)}, u32[]{:S(2)}, u32[]{:S(2)}) %all-to-all-start.1) | async-done | bytes 131104 | tf_op jit(solution)/shard_map/all_to_all | solution.py:447
  49.6 6.1 %couple.1 = (f32[2,16,512]{2,1,0:T(8,128)S(1)}, f32[32,8,128]{2,1,0:T(8,128)}) custom-call(f32[32,8,128]{2,1,0:T(8,128)S(1)} %all-to-all-done.1.values_ref, f32[2,32,8,128]{3,2,1,0:T(8,128)S(1)} %collective-permute-done.6.slots_ref, f32[16,512]{1,0:T(8,128)S(1)} %get-tuple-element.68.mask_ref, f32[2,16,512]{2,1,0:T(8,128)S(1)} %collective-permute-done.7.state_ref), custom_call_target="tpu_custom_call" | custom-call | flops 100000 | bytes 1000000 | tf_op jit(solution)/shard_map/couple/pallas_call | solution.py:521
  55.6 3.8 %all-to-all-start.2 = ((f32[32,8,128]{2,1,0:T(8,128)}), f32[32,8,128]{2,1,0:T(8,128)S(1)}, u32[]{:S(2)}, u32[]{:S(2)}) async-start(f32[32,8,128]{2,1,0:T(8,128)} %get-tuple-element.75), calls=%async_computation.2 | async-start | bytes 262144 | tf_op jit(solution)/shard_map/all_to_all | solution.py:447
  59.6 5.5 %rest_two.1 = (f32[8,16,512]{2,1,0:T(8,128)}, f32[8,16,512]{2,1,0:T(8,128)}) custom-call(f32[8,16,512]{2,1,0:T(8,128)S(1)} %bitcast.13, f32[8,16,512]{2,1,0:T(8,128)S(1)} %bitcast.19, f32[8,16,512]{2,1,0:T(8,128)S(1)} %bitcast.24, f32[16,512]{1,0:T(8,128)S(1)} %get-tuple-element.49.mask_ref, ...), custom_call_target="tpu_custom_call", output_to_operand_aliasing={{0}: (8, {}), {1}: (9, {})} | custom-call | flops 100000 | bytes 9000000 | tf_op jit(solution)/shard_map/rest_two/pallas_call | solution.py:530
  65.1 4.7 %all-to-all-done.2.values_ref = f32[32,8,128]{2,1,0:T(8,128)S(1)} async-done(((f32[32,8,128]{2,1,0:T(8,128)}), f32[32,8,128]{2,1,0:T(8,128)S(1)}, u32[]{:S(2)}, u32[]{:S(2)}) %all-to-all-start.2) | async-done | bytes 131104 | tf_op jit(solution)/shard_map/all_to_all | solution.py:447
  69.8 2.9 %collect.1.returned_ref = f32[16,512]{1,0:T(8,128)S(1)} custom-call(f32[32,8,128]{2,1,0:T(8,128)S(1)} %all-to-all-done.2.values_ref, s32[32,8,128]{2,1,0:T(8,128)S(1)} %all-to-all-done.cells_ref), custom_call_target="tpu_custom_call" | custom-call | flops 100000 | bytes 1000000 | tf_op jit(solution)/shard_map/collect/pallas_call | solution.py:545
  72.7 1.5 %collective-permute-start.9 = (f32[1,8,512]{2,1,0:T(8,128)S(1)}, f32[1,8,512]{2,1,0:T(8,128)S(1)}, u32[]{:S(2)}, u32[]{:S(2)}) collective-permute-start(f32[1,8,512]{2,1,0:T(8,128)S(1)} %get-tuple-element.82), channel_id=1, source_target_pairs={{0,4},{4,8},{8,12},{12,16},{16,20},{20,24},{24,28},{28,32},{32,36}... | collective-permute-start | bytes 49160 | tf_op jit(solution)/shard_map/ppermute | solution.py:432
  74.2 4.1 %collective-permute-start.10 = (f32[1,8,512]{2,1,0:T(8,128)S(1)}, f32[1,8,512]{2,1,0:T(8,128)S(1)}, u32[]{:S(2)}, u32[]{:S(2)}) collective-permute-start(f32[1,8,512]{2,1,0:T(8,128)S(1)} %get-tuple-element.83), channel_id=1, source_target_pairs={{4,0},{8,4},{12,8},{16,12},{20,16},{24,20},{28,24},{32,28},{36,32}... | collective-permute-start | bytes 49160 | tf_op jit(solution)/shard_map/ppermute | solution.py:433
  78.4 1.6 %collective-permute-done.9.from_south_ref = f32[1,8,512]{2,1,0:T(8,128)S(1)} collective-permute-done((f32[1,8,512]{2,1,0:T(8,128)S(1)}, f32[1,8,512]{2,1,0:T(8,128)S(1)}, u32[]{:S(2)}, u32[]{:S(2)}) %collective-permute-start.9) | collective-permute-done | bytes 16416 | tf_op jit(solution)/shard_map/ppermute | solution.py:432
  80.0 3.2 %collective-permute-done.11.from_fold_ref = f32[1,8,512]{2,1,0:T(8,128)S(1)} collective-permute-done((f32[1,8,512]{2,1,0:T(8,128)S(1)}, f32[1,8,512]{2,1,0:T(8,128)S(1)}, u32[]{:S(2)}, u32[]{:S(2)}) %collective-permute-start.11) | collective-permute-done | bytes 16416 | tf_op jit(solution)/shard_map/ppermute | solution.py:434
  83.4 1.9 %collective-permute-start.13 = (f32[24,128]{1,0:T(8,128)S(1)}, f32[24,128]{1,0:T(8,128)S(1)}, u32[]{:S(2)}, u32[]{:S(2)}) collective-permute-start(f32[24,128]{1,0:T(8,128)S(1)} %get-tuple-element.87), channel_id=1, source_target_pairs={{1,0},{2,1},{3,2},{0,3},{5,4},{6,5},{7,6},{4,7},{9,8},{10,9},{11,1... | collective-permute-start | bytes 36872 | tf_op jit(solution)/shard_map/ppermute | solution.py:442
  85.4 1.7 %collective-permute-done.12.from_west_ref = f32[24,128]{1,0:T(8,128)S(1)} collective-permute-done((f32[24,128]{1,0:T(8,128)S(1)}, f32[24,128]{1,0:T(8,128)S(1)}, u32[]{:S(2)}, u32[]{:S(2)}) %collective-permute-start.12) | collective-permute-done | bytes 12320 | tf_op jit(solution)/shard_map/ppermute | solution.py:441
  87.0 1.3 %collective-permute-done.13.from_east_ref = f32[24,128]{1,0:T(8,128)S(1)} collective-permute-done((f32[24,128]{1,0:T(8,128)S(1)}, f32[24,128]{1,0:T(8,128)S(1)}, u32[]{:S(2)}, u32[]{:S(2)}) %collective-permute-start.13) | collective-permute-done | bytes 12320 | tf_op jit(solution)/shard_map/ppermute | solution.py:442
  88.4 1.0 %second_surface.1 = (f32[8,16,512]{2,1,0:T(8,128)}, f32[8,16,512]{2,1,0:T(8,128)}) custom-call(f32[16,512]{1,0:T(8,128)S(1)} %get-tuple-element.81.adj_ref, f32[8,512]{1,0:T(8,128)S(1)} %get-tuple-element.85.halo_ref, f32[24,128]{1,0:T(8,128)S(1)} %collective-permute-done.12.from_west_ref, ...), custom_call_target="tpu_custom_call", output_to_operand_aliasing={{0}: (8, {}), {1}: (9, {})} | custom-call | tf_op jit(solution)/shard_map/second_surface/pallas_call | solution.py:560
  (26 shorter events, 0.7 us)
Async XLA Ops:
  0.6 21.2 %copy-start.1 = (f32[1,8,16,512]{3,2,1,0:T(8,128)S(1)}, f32[1,8,16,512]{3,2,1,0:T(8,128)}, u32[]{:S(2)}) copy-start(f32[1,8,16,512]{3,2,1,0:T(8,128)} %param.9) | copy-start | bytes 786436
  0.6 21.2 %copy-start.2 = (f32[1,8,16,512]{3,2,1,0:T(8,128)S(1)}, f32[1,8,16,512]{3,2,1,0:T(8,128)}, u32[]{:S(2)}) copy-start(f32[1,8,16,512]{3,2,1,0:T(8,128)} %param.10) | copy-start | bytes 786436
  2.0 19.8 %copy-start = (f32[1,8,16,512]{3,2,1,0:T(8,128)S(1)}, f32[1,8,16,512]{3,2,1,0:T(8,128)}, u32[]{:S(2)}) copy-start(f32[1,8,16,512]{3,2,1,0:T(8,128)} %param.8) | copy-start | bytes 786436
  2.1 9.1 %collective-permute-start = (s32[32,8,128]{2,1,0:T(8,128)S(1)}, s32[32,8,128]{2,1,0:T(8,128)}, u32[]{:S(2)}, u32[]{:S(2)}) collective-permute-start(s32[32,8,128]{2,1,0:T(8,128)S(1)} %get-tuple-element.48), channel_id=1, source_target_pairs={{0,128},{128,0},{1,129},{129,1},{2,130},{130,2},{3,131},{131,3},{4... | collective-permute-start | bytes 393224 | tf_op jit(solution)/shard_map/ppermute | solution.py:426
  2.2 17.0 %collective-permute-start.1 = (f32[21,8,512]{2,1,0:T(8,128)S(1)}, f32[21,8,512]{2,1,0:T(8,128)S(1)}, u32[]{:S(2)}, u32[]{:S(2)}) collective-permute-start(f32[21,8,512]{2,1,0:T(8,128)S(1)} %get-tuple-element.50), channel_id=1, source_target_pairs={{0,4},{4,8},{8,12},{12,16},{16,20},{20,24},{24,28},{28,32},{32,36}... | collective-permute-start | bytes 1032200 | tf_op jit(solution)/shard_map/ppermute | solution.py:432
  4.2 15.3 %collective-permute-start.2 = (f32[21,8,512]{2,1,0:T(8,128)S(1)}, f32[21,8,512]{2,1,0:T(8,128)S(1)}, u32[]{:S(2)}, u32[]{:S(2)}) collective-permute-start(f32[21,8,512]{2,1,0:T(8,128)S(1)} %get-tuple-element.51), channel_id=1, source_target_pairs={{4,0},{8,4},{12,8},{16,12},{20,16},{24,20},{28,24},{32,28},{36,32}... | collective-permute-start | bytes 1032200 | tf_op jit(solution)/shard_map/ppermute | solution.py:433
  10.6 11.2 %collective-permute-start.3 = (f32[21,8,512]{2,1,0:T(8,128)S(1)}, f32[21,8,512]{2,1,0:T(8,128)S(1)}, u32[]{:S(2)}, u32[]{:S(2)}) collective-permute-start(f32[21,8,512]{2,1,0:T(8,128)S(1)} %get-tuple-element.52), channel_id=1, source_target_pairs={{0,3},{1,2},{2,1},{3,0},{4,7},{5,6},{6,5},{7,4},{8,11},{9,10},{10,... | collective-permute-start | bytes 1032200 | tf_op jit(solution)/shard_map/ppermute | solution.py:434
  11.1 17.2 %all-to-all-start = ((s32[32,8,128]{2,1,0:T(8,128)}), s32[32,8,128]{2,1,0:T(8,128)S(1)}, u32[]{:S(2)}, u32[]{:S(2)}) async-start(s32[32,8,128]{2,1,0:T(8,128)} %collective-permute-done), calls=%async_computation | async-start | bytes 262144 | tf_op jit(solution)/shard_map/all_to_all | solution.py:447
  21.9 2.4 %copy-start.3 = (s32[1,1,1,32,1024]{4,3,2,1,0:T(8,128)S(1)}, s32[1,1,1,32,1024]{4,3,2,1,0:T(8,128)}, u32[]{:S(2)}) copy-start(s32[1,1,1,32,1024]{4,3,2,1,0:T(8,128)} %param.13) | copy-start | bytes 393220
  21.9 2.4 %copy-start.4 = (f32[1,1,1,32,1024]{4,3,2,1,0:T(8,128)S(1)}, f32[1,1,1,32,1024]{4,3,2,1,0:T(8,128)}, u32[]{:S(2)}) copy-start(f32[1,1,1,32,1024]{4,3,2,1,0:T(8,128)} %param.14) | copy-start | bytes 393220
  22.1 2.1 %copy-start.5 = (s32[1,1,1,32]{3,2,1,0:T(1,128)S(1)}, s32[1,1,1,32]{3,2,1,0:T(1,128)}, u32[]{:S(2)}) copy-start(s32[1,1,1,32]{3,2,1,0:T(1,128)} %param.15) | copy-start | bytes 388
  22.2 4.0 %collective-permute-start.4 = (f32[32,256]{1,0:T(8,128)S(1)}, f32[32,256]{1,0:T(8,128)S(1)}, u32[]{:S(2)}, u32[]{:S(2)}) collective-permute-start(f32[32,256]{1,0:T(8,128)S(1)} %get-tuple-element.56), channel_id=1, source_target_pairs={{0,1},{1,2},{2,3},{3,0},{4,5},{5,6},{6,7},{7,4},{8,9},{9,10},{10,1... | collective-permute-start | bytes 98312 | tf_op jit(solution)/shard_map/ppermute | solution.py:441
  22.7 5.1 %collective-permute-start.5 = (f32[32,256]{1,0:T(8,128)S(1)}, f32[32,256]{1,0:T(8,128)S(1)}, u32[]{:S(2)}, u32[]{:S(2)}) collective-permute-start(f32[32,256]{1,0:T(8,128)S(1)} %get-tuple-element.57), channel_id=1, source_target_pairs={{1,0},{2,1},{3,2},{0,3},{5,4},{6,5},{7,6},{4,7},{9,8},{10,9},{11,1... | collective-permute-start | bytes 98312 | tf_op jit(solution)/shard_map/ppermute | solution.py:442
  24.9 24.7 %collective-permute-start.6 = (f32[2,32,8,128]{3,2,1,0:T(8,128)S(1)}, f32[2,32,8,128]{3,2,1,0:T(8,128)S(1)}, u32[]{:S(2)}, u32[]{:S(2)}) collective-permute-start(f32[2,32,8,128]{3,2,1,0:T(8,128)S(1)} %receive.1), channel_id=1, source_target_pairs={{0,128},{128,0},{1,129},{129,1},{2,130},{130,2},{3,131},{131,3},{4... | collective-permute-start | bytes 786440 | tf_op jit(solution)/shard_map/ppermute | solution.py:426
  31.5 18.0 %all-to-all-start.1 = ((f32[32,8,128]{2,1,0:T(8,128)}), f32[32,8,128]{2,1,0:T(8,128)S(1)}, u32[]{:S(2)}, u32[]{:S(2)}) async-start(f32[32,8,128]{2,1,0:T(8,128)} %gather_slots.1), calls=%async_computation.1 | async-start | bytes 262144 | tf_op jit(solution)/shard_map/all_to_all | solution.py:447
  39.2 10.3 %collective-permute-start.7 = (f32[2,16,512]{2,1,0:T(8,128)S(1)}, f32[2,16,512]{2,1,0:T(8,128)S(1)}, u32[]{:S(2)}, u32[]{:S(2)}) collective-permute-start(f32[2,16,512]{2,1,0:T(8,128)S(1)} %get-tuple-element.69), channel_id=1, source_target_pairs={{0,128},{128,0},{1,129},{129,1},{2,130},{130,2},{3,131},{131,3},{4... | collective-permute-start | bytes 196616 | tf_op jit(solution)/shard_map/ppermute | solution.py:426
  55.6 14.1 %all-to-all-start.2 = ((f32[32,8,128]{2,1,0:T(8,128)}), f32[32,8,128]{2,1,0:T(8,128)S(1)}, u32[]{:S(2)}, u32[]{:S(2)}) async-start(f32[32,8,128]{2,1,0:T(8,128)} %get-tuple-element.75), calls=%async_computation.2 | async-start | bytes 262144 | tf_op jit(solution)/shard_map/all_to_all | solution.py:447
  59.5 13.2 %collective-permute-start.8 = (f32[2,16,512]{2,1,0:T(8,128)S(1)}, f32[2,16,512]{2,1,0:T(8,128)S(1)}, u32[]{:S(2)}, u32[]{:S(2)}) collective-permute-start(f32[2,16,512]{2,1,0:T(8,128)S(1)} %get-tuple-element.74), channel_id=1, source_target_pairs={{0,128},{128,0},{1,129},{129,1},{2,130},{130,2},{3,131},{131,3},{4... | collective-permute-start | bytes 196616 | tf_op jit(solution)/shard_map/ppermute | solution.py:426
  72.7 7.3 %collective-permute-start.9 = (f32[1,8,512]{2,1,0:T(8,128)S(1)}, f32[1,8,512]{2,1,0:T(8,128)S(1)}, u32[]{:S(2)}, u32[]{:S(2)}) collective-permute-start(f32[1,8,512]{2,1,0:T(8,128)S(1)} %get-tuple-element.82), channel_id=1, source_target_pairs={{0,4},{4,8},{8,12},{12,16},{16,20},{20,24},{24,28},{28,32},{32,36}... | collective-permute-start | bytes 49160 | tf_op jit(solution)/shard_map/ppermute | solution.py:432
  74.2 5.8 %collective-permute-start.10 = (f32[1,8,512]{2,1,0:T(8,128)S(1)}, f32[1,8,512]{2,1,0:T(8,128)S(1)}, u32[]{:S(2)}, u32[]{:S(2)}) collective-permute-start(f32[1,8,512]{2,1,0:T(8,128)S(1)} %get-tuple-element.83), channel_id=1, source_target_pairs={{4,0},{8,4},{12,8},{16,12},{20,16},{24,20},{28,24},{32,28},{36,32}... | collective-permute-start | bytes 49160 | tf_op jit(solution)/shard_map/ppermute | solution.py:433
  78.3 4.9 %collective-permute-start.11 = (f32[1,8,512]{2,1,0:T(8,128)S(1)}, f32[1,8,512]{2,1,0:T(8,128)S(1)}, u32[]{:S(2)}, u32[]{:S(2)}) collective-permute-start(f32[1,8,512]{2,1,0:T(8,128)S(1)} %get-tuple-element.84), channel_id=1, source_target_pairs={{0,3},{1,2},{2,1},{3,0},{4,7},{5,6},{6,5},{7,4},{8,11},{9,10},{10,... | collective-permute-start | bytes 49160 | tf_op jit(solution)/shard_map/ppermute | solution.py:434
  83.3 3.7 %collective-permute-start.12 = (f32[24,128]{1,0:T(8,128)S(1)}, f32[24,128]{1,0:T(8,128)S(1)}, u32[]{:S(2)}, u32[]{:S(2)}) collective-permute-start(f32[24,128]{1,0:T(8,128)S(1)} %get-tuple-element.86), channel_id=1, source_target_pairs={{0,1},{1,2},{2,3},{3,0},{4,5},{5,6},{6,7},{7,4},{8,9},{9,10},{10,1... | collective-permute-start | bytes 36872 | tf_op jit(solution)/shard_map/ppermute | solution.py:441
  83.4 4.9 %collective-permute-start.13 = (f32[24,128]{1,0:T(8,128)S(1)}, f32[24,128]{1,0:T(8,128)S(1)}, u32[]{:S(2)}, u32[]{:S(2)}) collective-permute-start(f32[24,128]{1,0:T(8,128)S(1)} %get-tuple-element.87), channel_id=1, source_target_pairs={{1,0},{2,1},{3,2},{0,3},{5,4},{6,5},{7,6},{4,7},{9,8},{10,9},{11,1... | collective-permute-start | bytes 36872 | tf_op jit(solution)/shard_map/ppermute | solution.py:442

commit v6 on v5

--- a/solution.py
+++ b/solution.py
@@ -11,7 +11,7 @@
 XR, XC = 24, 640
 FIELDS = 2 * LEV + 1
 EDGES = FIELDS + LEV // 2
-SPLITS = 4, 8
+SPLIT = 4
 BANDS, CAP = 32, 1024
 F32, BF16, I32 = jnp.float32, jnp.bfloat16, jnp.int32
 
@@ -238,23 +238,26 @@
     )
 
 
-def start_level(l, inc_ref, diff_ref, mask_ref, halo_ref, from_west_ref, from_east_ref, shape):
+def mask_products(mask_ref, halo_ref, from_west_ref, from_east_ref, shape):
+    sides = from_west_ref[:, 128:256], from_east_ref[:, 128:256]
+    mask = shape(extend(mask_ref[...], halo_ref[2 * LEV], side_column(0, WIDE, *sides)))
+    return mask * to_east(mask) * 0.5, mask * to_north(mask) * 0.5
+
+
+def start_level(l, masks, inc_ref, diff_ref, halo_ref, from_west_ref, from_east_ref, shape):
     sides = from_west_ref[:, 0:128], from_east_ref[:, 0:128]
-    other = from_west_ref[:, 128:256], from_east_ref[:, 128:256]
-    mask = shape(extend(mask_ref[...], halo_ref[2 * LEV], side_column(0, WIDE, *other)))
     diff = shape(extend(diff_ref[l], halo_ref[LEV + l], side_column(LEV + l, WIDE, *sides)))
     f = shape(extend(inc_ref[l], halo_ref[l], side_column(l, WIDE, *sides)))
-    c_east = mask * to_east(mask) * 0.5 * (diff + to_east(diff))
-    c_north = mask * to_north(mask) * 0.5 * (diff + to_north(diff))
-    return f, c_east, c_north
+    return f, masks[0] * (diff + to_east(diff)), masks[1] * (diff + to_north(diff))
 
 
 def first_surface(
     inc_ref, diff_ref, innov_ref, mask_ref, halo_ref, from_west_ref, from_east_ref,
     state_ref, surface_ref, c_east_ref, c_north_ref,
 ):
+    masks = mask_products(mask_ref, halo_ref, from_west_ref, from_east_ref, narrow)
     f, c_east, c_north = start_level(
-        0, inc_ref, diff_ref, mask_ref, halo_ref, from_west_ref, from_east_ref, narrow
+        0, masks, inc_ref, diff_ref, halo_ref, from_west_ref, from_east_ref, narrow
     )
     c_east_ref[...] = c_east
     c_north_ref[...] = c_north
@@ -267,27 +270,26 @@
 def rest_levels(low, high):
     def kernel(
         inc_ref, diff_ref, innov_ref, mask_ref, halo_ref, innov_halo_ref, from_west_ref,
-        from_east_ref, *refs,
+        from_east_ref, state_ref, gradient_ref, mask_east_ref, mask_north_ref,
     ):
-        state_ref, gradient_ref = refs[-2:]
         other = from_west_ref[0:XR, 128:256], from_east_ref[0:XR, 128:256]
+        mask_east_ref[...], mask_north_ref[...] = mask_products(
+            mask_ref, halo_ref, from_west_ref, from_east_ref, lambda x: x
+        )
 
         def level(l, carry):
+            masks = mask_east_ref[...], mask_north_ref[...]
             f, c_east, c_north = start_level(
-                l, inc_ref, diff_ref, mask_ref, halo_ref, from_west_ref, from_east_ref, lambda x: x
+                l, masks, inc_ref, diff_ref, halo_ref, from_west_ref, from_east_ref, lambda x: x
             )
             f = narrow(sweep(f, c_east, c_north))
-            state_ref[l] = f[:ROWS, :COLS]
+            state_ref[l - low] = f[:ROWS, :COLS]
             innov = extend(innov_ref[l], innov_halo_ref[l - 1], side_column(l, WIDE, *other))
             f = sweep(f - innov, narrow(c_east), narrow(c_north))
-            gradient_ref[l] = f[:ROWS, :COLS] + inc_ref[l]
+            gradient_ref[l - low] = f[:ROWS, :COLS] + inc_ref[l]
             return carry
 
         lax.fori_loop(low, high, level, 0)
-        if len(refs) == 4:
-            old_state_ref, old_gradient_ref = refs[:2]
-            state_ref[1:low] = old_state_ref[1:low]
-            gradient_ref[1:low] = old_gradient_ref[1:low]
 
     return kernel
 
@@ -306,24 +308,32 @@
 
 
 GROUP = 8
-SUMS = 8
-
-
-def gather_all(cells_of, table_ref, store):
+SUMS = 16
+
+
+def gather_all(cells_of, table_ref, weigh, buffer_ref, out_hbm, sem):
+    def copy(g):
+        rows = pl.ds(g * GROUP, GROUP)
+        return pltpu.make_async_copy(buffer_ref.at[rows], out_hbm.at[rows], sem.at[g])
+
     def group(g, carry):
-        for n in range(GROUP):
-            b = g * GROUP + n
-            store(b, gather_slots(row_of(table_ref), cells_of(b)))
+        bands = [g * GROUP + n for n in range(GROUP)]
+        cells = [cells_of(b) for b in bands]
+        found = [gather_slots(row_of(table_ref), at) for at in cells]
+        for b, x in zip(bands, found):
+            buffer_ref[b] = weigh(b, x)
+        copy(g).start()
         return carry
 
     lax.fori_loop(0, BANDS // GROUP, group, 0)
-
-
-def gather_kernel(cells_ref, table_ref, out_ref):
-    def store(b, found):
-        out_ref[b] = found
-
-    gather_all(lambda b: cells_ref[b], table_ref, store)
+    for g in range(BANDS // GROUP):
+        copy(g).wait()
+
+
+def gather_kernel(cells_ref, table_ref, out_hbm, buffer_ref, sem):
+    gather_all(
+        lambda b: cells_ref[b], table_ref, lambda b, found: found, buffer_ref, out_hbm, sem
+    )
 
 
 def scatter_band(cells, values):
@@ -370,7 +380,8 @@
 
 
 def couple_kernel(
-    values_ref, slots_ref, mask_ref, state_ref, linear_ref, out_ref, acc_ref, table_ref
+    values_ref, slots_ref, mask_ref, state_ref, linear_ref, out_hbm, acc_ref, table_ref,
+    buffer_ref, sem,
 ):
     def cells(b):
         return slots_ref[1, b].astype(I32)
@@ -383,10 +394,9 @@
     linear_ref[1] = residual
     table_ref[...] = mask * residual
 
-    def store(b, found):
-        out_ref[b] = slots_ref[0, b] * found
-
-    gather_all(cells, table_ref, store)
+    gather_all(
+        cells, table_ref, lambda b, found: slots_ref[0, b] * found, buffer_ref, out_hbm, sem
+    )
 
 
 def collect_kernel(values_ref, cells_ref, out_ref, acc_ref):
@@ -403,7 +413,7 @@
 
 
 def second_columns(
-    adj_ref, from_south_ref, from_north_ref, from_fold_ref, halo_ref, east_ref, west_ref
+    adj_ref, from_fold_ref, from_south_ref, from_north_ref, halo_ref, east_ref, west_ref
 ):
     halo, _ = split_pair(*taker(from_south_ref, from_north_ref, from_fold_ref)(0))
     halo_ref[...] = halo
@@ -414,12 +424,25 @@
 
 def second_surface(
     adj_ref, halo_ref, from_west_ref, from_east_ref, c_east_ref, c_north_ref, inc_ref, linear_ref,
-    state_any, gradient_any, state_ref, gradient_ref,
+    state_one, gradient_one, state_two, gradient_two, state_hbm, gradient_hbm, top_ref, sem,
 ):
+    copies = []
+
+    def store(source, target):
+        copies.append(pltpu.make_async_copy(source, target, sem.at[len(copies)]))
+        copies[-1].start()
+
+    store(linear_ref.at[0:1], state_hbm.at[0:1])
+    store(state_one, state_hbm.at[1:SPLIT])
+    store(gradient_one, gradient_hbm.at[1:SPLIT])
+    store(state_two, state_hbm.at[SPLIT:LEV])
+    store(gradient_two, gradient_hbm.at[SPLIT:LEV])
     side = side_column(0, HALO, from_west_ref[...], from_east_ref[...])
     f = sweep(extend(adj_ref[...], halo_ref[...], side), c_east_ref[...], c_north_ref[...])
-    gradient_ref[0] = f[:ROWS, :COLS] + inc_ref[0]
-    state_ref[0] = linear_ref[0]
+    top_ref[0] = f[:ROWS, :COLS] + inc_ref[...]
+    store(top_ref, gradient_hbm.at[0:1])
+    for copy in copies:
+        copy.wait()
 
 
 def across(value):
@@ -457,7 +480,6 @@
     slots = sds(BANDS, 8, 128)
     smem = pl.BlockSpec(memory_space=pltpu.SMEM)
     vmem = pl.BlockSpec(memory_space=pltpu.VMEM)
-    whole = pl.BlockSpec(memory_space=pl.ANY)
     params = pltpu.CompilerParams(vmem_limit_bytes=48 << 20)
     barrier = lax.optimization_barrier
 
@@ -506,70 +528,74 @@
     state, surface, c_east, c_north = call(
         first_surface, (pair, plane, wide, wide), "first_surface"
     )(inc, diff, innov, mask, halo, from_west, from_east)
-    sent = call(gather_kernel, slots, "gather_slots")(pulled, surface)
+    hbm = pl.BlockSpec(memory_space=pltpu.HBM)
+    groups = [pltpu.VMEM((BANDS, 8, 128), F32), pltpu.SemaphoreType.DMA((BANDS // GROUP,))]
+    sent = pl.pallas_call(
+        gather_kernel,
+        out_shape=slots,
+        in_specs=[vmem] * 2,
+        out_specs=hbm,
+        scratch_shapes=groups,
+        name="gather_slots",
+        compiler_params=params,
+    )(pulled, surface)
 
     sent, halo, state = barrier((sent, halo, state))
     values = exchange(sent)
     state = across(state)
-    shared = (inc, diff, innov, mask)
-    rest = call(rest_levels(1, SPLITS[0]), (field, field), "rest_one", nbytes=10000000)(
-        *shared, halo, innov_halo, from_west, from_east
-    )
-
-    values, *rest = barrier((values, *rest))
+    halo8, west8, east8 = halo, from_west, from_east
+
+    def levels(low, high, name):
+        some = sds(high - low, ROWS, COLS)
+        wide8 = pltpu.VMEM((32, XC), F32)
+        return call(rest_levels(low, high), (some, some), name, [wide8, wide8], nbytes=12000000)
+
+    rest_one = levels(1, SPLIT, "rest_one")(
+        inc, diff, innov, mask, halo8, innov_halo, west8, east8
+    )
+
+    values, *rest_one = barrier((values, *rest_one))
     acc = pltpu.VMEM((128, 128), F32)
-    linear, outgoing = call(
-        couple_kernel, (pair, slots), "couple", [acc, pltpu.VMEM((ROWS, COLS), F32)]
+    linear, outgoing = pl.pallas_call(
+        couple_kernel,
+        out_shape=(pair, slots),
+        in_specs=[vmem] * 4,
+        out_specs=(vmem, hbm),
+        scratch_shapes=[acc, pltpu.VMEM((ROWS, COLS), F32), *groups],
+        name="couple",
+        compiler_params=params,
     )(values, received, other_mask, state)
 
-    outgoing, linear, *rest = barrier((outgoing, linear, *rest))
+    outgoing, linear, halo8 = barrier((outgoing, linear, halo8))
     back = exchange(outgoing)
     linear = across(linear)
-
-    def more(low, high, name, rest):
-        return pl.pallas_call(
-            rest_levels(low, high),
-            out_shape=(field, field),
-            in_specs=[vmem] * 10,
-            out_specs=(vmem,) * 2,
-            input_output_aliases={8: 0, 9: 1},
-            name=name,
-            cost_estimate=pl.CostEstimate(flops=100000, bytes_accessed=9000000, transcendentals=0),
-            compiler_params=params,
-        )(inc, diff, innov, mask, halo8, innov_halo, west8, east8, *rest)
-
-    halo8, west8, east8 = halo, from_west, from_east
-    rest = more(SPLITS[0], SPLITS[1], "rest_two", rest)
-
-    back, *rest = barrier((back, *rest))
+    rest_two = levels(SPLIT, LEV, "rest_two")(
+        inc, diff, innov, mask, halo8, innov_halo, west8, east8
+    )
+
+    back, *rest_two = barrier((back, *rest_two))
     returned = call(collect_kernel, plane, "collect", [acc])(back, pulled)
     edge = sds(1, 8, COLS)
     adj, *edges = call(second_pack, (plane, edge, edge, edge), "second_pack")(
         linear, mask, returned
     )
     packed = sds(XR, 128)
+    south, north, fold = along(*edges)
     halo, east, west = call(second_columns, (sds(8, COLS), packed, packed), "second_columns")(
-        adj, *along(*edges)
+        adj, fold, south, north
     )
     from_west, from_east = around(east, west)
-    top = pl.BlockSpec((1, ROWS, COLS), lambda i: (0, 0, 0))
-
-    def full(*shape):
-        return pl.BlockSpec(shape, lambda i: (0,) * len(shape))
-
     state, gradient = pl.pallas_call(
         second_surface,
         out_shape=(field, field),
-        grid=(1,),
-        in_specs=[
-            full(ROWS, COLS), full(8, COLS), full(XR, 128), full(XR, 128), full(XR, XC),
-            full(XR, XC), top, top, whole, whole,
-        ],
-        out_specs=(top, top),
-        input_output_aliases={8: 0, 9: 1},
+        in_specs=[vmem] * 12,
+        out_specs=(hbm, hbm),
+        scratch_shapes=[pltpu.VMEM((1, ROWS, COLS), F32), pltpu.SemaphoreType.DMA((6,))],
         name="second_surface",
         compiler_params=params,
-    )(adj, halo, from_west, from_east, c_east, c_north, inc, linear, *rest)
+    )(
+        adj, halo, from_west, from_east, c_east, c_north, inc[0], linear, *rest_one, *rest_two
+    )
     return (state[None], gradient[None])
 
 

time: 89.7 us -> 89.3 us (level)
  Pallas kernels: 25 us -> 22 us
  waiting for transfers between devices: 26.5 us -> 28.9 us
    pallas_call x5, Pallas kernels: 19.3 us -> 16.7 us  [the longest x1 5.74 us: local(): pl.pallas_call(couple_kernel, out_shape=(pair, slots), in_specs=[vmem] *...]
    all_to_all x3, waiting for transfers between devices: 11.4 us -> 13.7 us  [exchange(): return lax.all_to_all(slots, 'lat', 0, 0, tiled=True)]
  transfers between devices with their start and end apart: 17 -> 17, of which waited for: 11 -> 11; matrix products, arithmetic and copies ran while one was open for 0% -> 0% of each run, Pallas kernels for 18% -> 15%
where the time goes in v6:
time: 89.3 us; the launch traced here: 89 us
  starting transfers between devices  37 us (41%)
  waiting for transfers between devices  28.9 us (32%)
  Pallas kernels  22 us (25%)
  between operations  1.01 us (1%)
    all_to_all x3, starting transfers between devices, exchange(): return lax.all_to_all(slots, 'lat', 0, 0, tiled=True)  17.9 us
    all_to_all x3, waiting for transfers between devices, exchange(): return lax.all_to_all(slots, 'lat', 0, 0, tiled=True)  13.7 us
    ppermute x2, starting transfers between devices, along(): lax.ppermute(head, 'lat', [((i + 1) % n, i) for i in range(n)])  10.7 us
    pallas_call x1, Pallas kernels, local(): pl.pallas_call(couple_kernel, out_shape=(pair, slots), in_specs=[vmem] *...  5.74 us
    ppermute x2, waiting for transfers between devices, along(): lax.ppermute(mirror, 'lon', [(i, m - 1 - i) for i in range(m)])  5.64 us
    pallas_call x1, Pallas kernels, local(): levels(SPLIT, LEV, 'rest_two')  3.78 us
    ppermute x2, starting transfers between devices, around(): lax.ppermute(west, 'lon', [((i + 1) % n, i) for i in range(n)])  3.52 us
    ppermute x2, waiting for transfers between devices, along(): lax.ppermute(tail, 'lat', [(i, (i + 1) % n) for i in range(n)])  3.39 us
  transfers between devices with their start and end apart: 17, of which 11 were waited for; matrix products, arithmetic and copies ran while one was open for 0% of the time, Pallas kernels for 15%

profile of v6, /device:TPU:6, one launch (start us, length us, event | category | flops | bytes accessed | tf_op | source)
XLA Modules:
  0.0 89.0 jit_solution(12883024196364343276)
XLA Ops:
  0.7 1.4 %first_pack.1 = (f32[21,8,512]{2,1,0:T(8,128)S(1)}, f32[21,8,512]{2,1,0:T(8,128)S(1)}, f32[21,8,512]{2,1,0:T(8,128)S(1)}, f32[16,512]{1,0:T(8,128)S(1)}, f32[16,...) custom-call(f32[8,16,512]{2,1,0:T(8,128)} %bitcast.11, f32[8,16,512]{2,1,0:T(8,128)} %bitcast.16, f32[8,16,512]{2,1,0:T(8,128)} %bitcast.21, ...), custom_call_target="tpu_custom_call" | custom-call | tf_op jit(solution)/shard_map/first_pack/pallas_call | solution.py:488
  2.2 2.0 %collective-permute-start.1 = (f32[21,8,512]{2,1,0:T(8,128)S(1)}, f32[21,8,512]{2,1,0:T(8,128)S(1)}, u32[]{:S(2)}, u32[]{:S(2)}) collective-permute-start(f32[21,8,512]{2,1,0:T(8,128)S(1)} %get-tuple-element.49), channel_id=1, source_target_pairs={{0,4},{4,8},{8,12},{12,16},{16,20},{20,24},{24,28},{28,32},{32,36}... | collective-permute-start | bytes 1032200 | tf_op jit(solution)/shard_map/ppermute | solution.py:455
  4.2 6.5 %collective-permute-start.2 = (f32[21,8,512]{2,1,0:T(8,128)S(1)}, f32[21,8,512]{2,1,0:T(8,128)S(1)}, u32[]{:S(2)}, u32[]{:S(2)}) collective-permute-start(f32[21,8,512]{2,1,0:T(8,128)S(1)} %get-tuple-element.50), channel_id=1, source_target_pairs={{4,0},{8,4},{12,8},{16,12},{20,16},{24,20},{28,24},{32,28},{36,32}... | collective-permute-start | bytes 1032200 | tf_op jit(solution)/shard_map/ppermute | solution.py:456
  10.6 0.5 collective-permute-start.3
  11.1 6.3 %all-to-all-start = ((s32[32,8,128]{2,1,0:T(8,128)}), s32[32,8,128]{2,1,0:T(8,128)S(1)}, u32[]{:S(2)}, u32[]{:S(2)}) async-start(s32[32,8,128]{2,1,0:T(8,128)} %collective-permute-done), calls=%async_computation | async-start | bytes 262144 | tf_op jit(solution)/shard_map/all_to_all | solution.py:470
  17.4 1.7 %collective-permute-done.1.from_south_ref = f32[21,8,512]{2,1,0:T(8,128)S(1)} collective-permute-done((f32[21,8,512]{2,1,0:T(8,128)S(1)}, f32[21,8,512]{2,1,0:T(8,128)S(1)}, u32[]{:S(2)}, u32[]{:S(2)}) %collective-permute-start.1) | collective-permute-done | bytes 344096 | tf_op jit(solution)/shard_map/ppermute | solution.py:455
  19.2 0.3 collective-permute-done.2.from_north_ref
  19.5 2.4 %collective-permute-done.3.from_fold_ref = f32[21,8,512]{2,1,0:T(8,128)S(1)} collective-permute-done((f32[21,8,512]{2,1,0:T(8,128)S(1)}, f32[21,8,512]{2,1,0:T(8,128)S(1)}, u32[]{:S(2)}, u32[]{:S(2)}) %collective-permute-start.3) | collective-permute-done | bytes 344096 | tf_op jit(solution)/shard_map/ppermute | solution.py:457
  22.2 0.6 collective-permute-start.4
  22.7 1.5 %collective-permute-start.5 = (f32[32,256]{1,0:T(8,128)S(1)}, f32[32,256]{1,0:T(8,128)S(1)}, u32[]{:S(2)}, u32[]{:S(2)}) collective-permute-start(f32[32,256]{1,0:T(8,128)S(1)} %get-tuple-element.56), channel_id=1, source_target_pairs={{1,0},{2,1},{3,2},{0,3},{5,4},{6,5},{7,6},{4,7},{9,8},{10,9},{11,1... | collective-permute-start | bytes 98312 | tf_op jit(solution)/shard_map/ppermute | solution.py:465
  24.3 0.6 receive.1
  25.0 1.2 %collective-permute-done.4.from_west_ref = f32[32,256]{1,0:T(8,128)S(1)} collective-permute-done((f32[32,256]{1,0:T(8,128)S(1)}, f32[32,256]{1,0:T(8,128)S(1)}, u32[]{:S(2)}, u32[]{:S(2)}) %collective-permute-start.4) | collective-permute-done | bytes 32800 | tf_op jit(solution)/shard_map/ppermute | solution.py:464
  26.1 1.7 %collective-permute-done.5.from_east_ref = f32[32,256]{1,0:T(8,128)S(1)} collective-permute-done((f32[32,256]{1,0:T(8,128)S(1)}, f32[32,256]{1,0:T(8,128)S(1)}, u32[]{:S(2)}, u32[]{:S(2)}) %collective-permute-start.5) | collective-permute-done | bytes 32800 | tf_op jit(solution)/shard_map/ppermute | solution.py:465
  27.8 0.5 first_surface.1
  28.3 3.2 %gather_slots.1 = f32[32,8,128]{2,1,0:T(8,128)} custom-call(s32[32,8,128]{2,1,0:T(8,128)S(1)} %all-to-all-done.cells_ref, f32[16,512]{1,0:T(8,128)S(1)} %get-tuple-element.57.table_ref), custom_call_target="tpu_custom_call" | custom-call | tf_op jit(solution)/shard_map/gather_slots/pallas_call | solution.py:533
  31.5 7.7 %all-to-all-start.1 = ((f32[32,8,128]{2,1,0:T(8,128)}), f32[32,8,128]{2,1,0:T(8,128)S(1)}, u32[]{:S(2)}, u32[]{:S(2)}) async-start(f32[32,8,128]{2,1,0:T(8,128)} %gather_slots.1), calls=%async_computation.1 | async-start | bytes 262144 | tf_op jit(solution)/shard_map/all_to_all | solution.py:470
  39.4 2.9 %rest_one.1 = (f32[3,16,512]{2,1,0:T(8,128)S(1)}, f32[3,16,512]{2,1,0:T(8,128)S(1)}) custom-call(f32[8,16,512]{2,1,0:T(8,128)S(1)} %bitcast.14, f32[8,16,512]{2,1,0:T(8,128)S(1)} %bitcast.19, f32[8,16,512]{2,1,0:T(8,128)S(1)} %bitcast.24, f32[16,512]{1,0:T(8,128)S(1)} %get-tuple-element.48.mask_ref, f32[17,16,512]{2,1,0:T(8,128)S(1)} %get-tuple-element.73.halo_ref, ...), custom_call_target="tpu_custom_call" | custom-call | flops 100000 | bytes 12000000 | tf_op jit(solution)/shard_map/rest_one/pallas_call | solution.py:553
  42.2 7.3 %all-to-all-done.1.values_ref = f32[32,8,128]{2,1,0:T(8,128)S(1)} async-done(((f32[32,8,128]{2,1,0:T(8,128)}), f32[32,8,128]{2,1,0:T(8,128)S(1)}, u32[]{:S(2)}, u32[]{:S(2)}) %all-to-all-start.1) | async-done | bytes 131104 | tf_op jit(solution)/shard_map/all_to_all | solution.py:470
  49.6 5.7 %couple.1 = (f32[2,16,512]{2,1,0:T(8,128)S(1)}, f32[32,8,128]{2,1,0:T(8,128)}) custom-call(f32[32,8,128]{2,1,0:T(8,128)S(1)} %all-to-all-done.1.values_ref, f32[2,32,8,128]{3,2,1,0:T(8,128)S(1)} %collective-permute-done.6.slots_ref, f32[16,512]{1,0:T(8,128)S(1)} %get-tuple-element.67.mask_ref, f32[2,16,512]{2,1,0:T(8,128)S(1)} %collective-permute-done.7.state_ref), custom_call_target="tpu_custom_call" | custom-call | tf_op jit(solution)/shard_map/couple/pallas_call | solution.py:559
  55.3 3.9 %all-to-all-start.2 = ((f32[32,8,128]{2,1,0:T(8,128)}), f32[32,8,128]{2,1,0:T(8,128)S(1)}, u32[]{:S(2)}, u32[]{:S(2)}) async-start(f32[32,8,128]{2,1,0:T(8,128)} %get-tuple-element.72), calls=%async_computation.2 | async-start | bytes 262144 | tf_op jit(solution)/shard_map/all_to_all | solution.py:470
  59.2 0.3 collective-permute-start.8
  59.5 3.8 %rest_two.1 = (f32[4,16,512]{2,1,0:T(8,128)S(1)}, f32[4,16,512]{2,1,0:T(8,128)S(1)}) custom-call(f32[8,16,512]{2,1,0:T(8,128)S(1)} %bitcast.15, f32[8,16,512]{2,1,0:T(8,128)S(1)} %bitcast.20, f32[8,16,512]{2,1,0:T(8,128)S(1)} %bitcast.25, f32[16,512]{1,0:T(8,128)S(1)} %get-tuple-element.48.mask_ref, f32[17,16,512]{2,1,0:T(8,128)S(1)} %get-tuple-element.73.halo_ref, ...), custom_call_target="tpu_custom_call" | custom-call | flops 100000 | bytes 12000000 | tf_op jit(solution)/shard_map/rest_two/pallas_call | solution.py:572
  63.3 6.4 %all-to-all-done.2.values_ref = f32[32,8,128]{2,1,0:T(8,128)S(1)} async-done(((f32[32,8,128]{2,1,0:T(8,128)}), f32[32,8,128]{2,1,0:T(8,128)S(1)}, u32[]{:S(2)}, u32[]{:S(2)}) %all-to-all-start.2) | async-done | bytes 131104 | tf_op jit(solution)/shard_map/all_to_all | solution.py:470
  69.7 2.5 %collect.1.returned_ref = f32[16,512]{1,0:T(8,128)S(1)} custom-call(f32[32,8,128]{2,1,0:T(8,128)S(1)} %all-to-all-done.2.values_ref, s32[32,8,128]{2,1,0:T(8,128)S(1)} %all-to-all-done.cells_ref), custom_call_target="tpu_custom_call" | custom-call | flops 100000 | bytes 1000000 | tf_op jit(solution)/shard_map/collect/pallas_call | solution.py:577
  72.2 1.2 %collective-permute-start.10 = (f32[1,8,512]{2,1,0:T(8,128)S(1)}, f32[1,8,512]{2,1,0:T(8,128)S(1)}, u32[]{:S(2)}, u32[]{:S(2)}) collective-permute-start(f32[1,8,512]{2,1,0:T(8,128)S(1)} %get-tuple-element.79), channel_id=1, source_target_pairs={{0,4},{4,8},{8,12},{12,16},{16,20},{20,24},{24,28},{28,32},{32,36}... | collective-permute-start | bytes 49160 | tf_op jit(solution)/shard_map/ppermute | solution.py:455
  73.4 4.2 %collective-permute-start.11 = (f32[1,8,512]{2,1,0:T(8,128)S(1)}, f32[1,8,512]{2,1,0:T(8,128)S(1)}, u32[]{:S(2)}, u32[]{:S(2)}) collective-permute-start(f32[1,8,512]{2,1,0:T(8,128)S(1)} %get-tuple-element.80), channel_id=1, source_target_pairs={{4,0},{8,4},{12,8},{16,12},{20,16},{24,20},{28,24},{32,28},{36,32}... | collective-permute-start | bytes 49160 | tf_op jit(solution)/shard_map/ppermute | solution.py:456
  77.7 1.7 %collective-permute-done.10.from_south_ref = f32[1,8,512]{2,1,0:T(8,128)S(1)} collective-permute-done((f32[1,8,512]{2,1,0:T(8,128)S(1)}, f32[1,8,512]{2,1,0:T(8,128)S(1)}, u32[]{:S(2)}, u32[]{:S(2)}) %collective-permute-start.10) | collective-permute-done | bytes 16416 | tf_op jit(solution)/shard_map/ppermute | solution.py:455
  79.4 3.2 %collective-permute-done.9.from_fold_ref = f32[1,8,512]{2,1,0:T(8,128)S(1)} collective-permute-done((f32[1,8,512]{2,1,0:T(8,128)S(1)}, f32[1,8,512]{2,1,0:T(8,128)S(1)}, u32[]{:S(2)}, u32[]{:S(2)}) %collective-permute-start.9) | collective-permute-done | bytes 16416 | tf_op jit(solution)/shard_map/ppermute | solution.py:457
  82.8 2.0 %collective-permute-start.13 = (f32[24,128]{1,0:T(8,128)S(1)}, f32[24,128]{1,0:T(8,128)S(1)}, u32[]{:S(2)}, u32[]{:S(2)}) collective-permute-start(f32[24,128]{1,0:T(8,128)S(1)} %get-tuple-element.83), channel_id=1, source_target_pairs={{1,0},{2,1},{3,2},{0,3},{5,4},{6,5},{7,6},{4,7},{9,8},{10,9},{11,1... | collective-permute-start | bytes 36872 | tf_op jit(solution)/shard_map/ppermute | solution.py:465
  84.7 1.7 %collective-permute-done.12.from_west_ref = f32[24,128]{1,0:T(8,128)S(1)} collective-permute-done((f32[24,128]{1,0:T(8,128)S(1)}, f32[24,128]{1,0:T(8,128)S(1)}, u32[]{:S(2)}, u32[]{:S(2)}) %collective-permute-start.12) | collective-permute-done | bytes 12320 | tf_op jit(solution)/shard_map/ppermute | solution.py:464
  86.4 1.3 %collective-permute-done.13.from_east_ref = f32[24,128]{1,0:T(8,128)S(1)} collective-permute-done((f32[24,128]{1,0:T(8,128)S(1)}, f32[24,128]{1,0:T(8,128)S(1)}, u32[]{:S(2)}, u32[]{:S(2)}) %collective-permute-start.13) | collective-permute-done | bytes 12320 | tf_op jit(solution)/shard_map/ppermute | solution.py:465
  87.7 1.1 %second_surface.1 = (f32[8,16,512]{2,1,0:T(8,128)}, f32[8,16,512]{2,1,0:T(8,128)}) custom-call(f32[16,512]{1,0:T(8,128)S(1)} %get-tuple-element.77.adj_ref, f32[8,512]{1,0:T(8,128)S(1)} %get-tuple-element.81.halo_ref, f32[24,128]{1,0:T(8,128)S(1)} %collective-permute-done.12.from_west_ref, f32[24,128]{1,0:T(8,128)S(1)} %collective-permute-done.13.from_east_ref, ...), custom_call_target="tpu_custom_call" | custom-call | tf_op jit(solution)/shard_map/second_surface/pallas_call | solution.py:588
  (27 shorter events, 0.8 us)
Async XLA Ops:
  0.6 21.2 %copy-start.1 = (f32[1,8,16,512]{3,2,1,0:T(8,128)S(1)}, f32[1,8,16,512]{3,2,1,0:T(8,128)}, u32[]{:S(2)}) copy-start(f32[1,8,16,512]{3,2,1,0:T(8,128)} %param.9) | copy-start | bytes 786436
  0.6 21.2 %copy-start.2 = (f32[1,8,16,512]{3,2,1,0:T(8,128)S(1)}, f32[1,8,16,512]{3,2,1,0:T(8,128)}, u32[]{:S(2)}) copy-start(f32[1,8,16,512]{3,2,1,0:T(8,128)} %param.10) | copy-start | bytes 786436
  2.0 19.8 %copy-start = (f32[1,8,16,512]{3,2,1,0:T(8,128)S(1)}, f32[1,8,16,512]{3,2,1,0:T(8,128)}, u32[]{:S(2)}) copy-start(f32[1,8,16,512]{3,2,1,0:T(8,128)} %param.8) | copy-start | bytes 786436
  2.1 9.1 %collective-permute-start = (s32[32,8,128]{2,1,0:T(8,128)S(1)}, s32[32,8,128]{2,1,0:T(8,128)}, u32[]{:S(2)}, u32[]{:S(2)}) collective-permute-start(s32[32,8,128]{2,1,0:T(8,128)S(1)} %get-tuple-element.47), channel_id=1, source_target_pairs={{0,128},{128,0},{1,129},{129,1},{2,130},{130,2},{3,131},{131,3},{4... | collective-permute-start | bytes 393224 | tf_op jit(solution)/shard_map/ppermute | solution.py:449
  2.2 17.0 %collective-permute-start.1 = (f32[21,8,512]{2,1,0:T(8,128)S(1)}, f32[21,8,512]{2,1,0:T(8,128)S(1)}, u32[]{:S(2)}, u32[]{:S(2)}) collective-permute-start(f32[21,8,512]{2,1,0:T(8,128)S(1)} %get-tuple-element.49), channel_id=1, source_target_pairs={{0,4},{4,8},{8,12},{12,16},{16,20},{20,24},{24,28},{28,32},{32,36}... | collective-permute-start | bytes 1032200 | tf_op jit(solution)/shard_map/ppermute | solution.py:455
  4.2 15.3 %collective-permute-start.2 = (f32[21,8,512]{2,1,0:T(8,128)S(1)}, f32[21,8,512]{2,1,0:T(8,128)S(1)}, u32[]{:S(2)}, u32[]{:S(2)}) collective-permute-start(f32[21,8,512]{2,1,0:T(8,128)S(1)} %get-tuple-element.50), channel_id=1, source_target_pairs={{4,0},{8,4},{12,8},{16,12},{20,16},{24,20},{28,24},{32,28},{36,32}... | collective-permute-start | bytes 1032200 | tf_op jit(solution)/shard_map/ppermute | solution.py:456
  10.6 11.2 %collective-permute-start.3 = (f32[21,8,512]{2,1,0:T(8,128)S(1)}, f32[21,8,512]{2,1,0:T(8,128)S(1)}, u32[]{:S(2)}, u32[]{:S(2)}) collective-permute-start(f32[21,8,512]{2,1,0:T(8,128)S(1)} %get-tuple-element.51), channel_id=1, source_target_pairs={{0,3},{1,2},{2,1},{3,0},{4,7},{5,6},{6,5},{7,4},{8,11},{9,10},{10,... | collective-permute-start | bytes 1032200 | tf_op jit(solution)/shard_map/ppermute | solution.py:457
  11.1 17.2 %all-to-all-start = ((s32[32,8,128]{2,1,0:T(8,128)}), s32[32,8,128]{2,1,0:T(8,128)S(1)}, u32[]{:S(2)}, u32[]{:S(2)}) async-start(s32[32,8,128]{2,1,0:T(8,128)} %collective-permute-done), calls=%async_computation | async-start | bytes 262144 | tf_op jit(solution)/shard_map/all_to_all | solution.py:470
  21.9 2.4 %copy-start.3 = (s32[1,1,1,32,1024]{4,3,2,1,0:T(8,128)S(1)}, s32[1,1,1,32,1024]{4,3,2,1,0:T(8,128)}, u32[]{:S(2)}) copy-start(s32[1,1,1,32,1024]{4,3,2,1,0:T(8,128)} %param.13) | copy-start | bytes 393220
  21.9 2.4 %copy-start.4 = (f32[1,1,1,32,1024]{4,3,2,1,0:T(8,128)S(1)}, f32[1,1,1,32,1024]{4,3,2,1,0:T(8,128)}, u32[]{:S(2)}) copy-start(f32[1,1,1,32,1024]{4,3,2,1,0:T(8,128)} %param.14) | copy-start | bytes 393220
  22.1 2.1 %copy-start.5 = (s32[1,1,1,32]{3,2,1,0:T(1,128)S(1)}, s32[1,1,1,32]{3,2,1,0:T(1,128)}, u32[]{:S(2)}) copy-start(s32[1,1,1,32]{3,2,1,0:T(1,128)} %param.15) | copy-start | bytes 388
  22.2 4.0 %collective-permute-start.4 = (f32[32,256]{1,0:T(8,128)S(1)}, f32[32,256]{1,0:T(8,128)S(1)}, u32[]{:S(2)}, u32[]{:S(2)}) collective-permute-start(f32[32,256]{1,0:T(8,128)S(1)} %get-tuple-element.55), channel_id=1, source_target_pairs={{0,1},{1,2},{2,3},{3,0},{4,5},{5,6},{6,7},{7,4},{8,9},{9,10},{10,1... | collective-permute-start | bytes 98312 | tf_op jit(solution)/shard_map/ppermute | solution.py:464
  22.7 5.1 %collective-permute-start.5 = (f32[32,256]{1,0:T(8,128)S(1)}, f32[32,256]{1,0:T(8,128)S(1)}, u32[]{:S(2)}, u32[]{:S(2)}) collective-permute-start(f32[32,256]{1,0:T(8,128)S(1)} %get-tuple-element.56), channel_id=1, source_target_pairs={{1,0},{2,1},{3,2},{0,3},{5,4},{6,5},{7,6},{4,7},{9,8},{10,9},{11,1... | collective-permute-start | bytes 98312 | tf_op jit(solution)/shard_map/ppermute | solution.py:465
  24.9 24.7 %collective-permute-start.6 = (f32[2,32,8,128]{3,2,1,0:T(8,128)S(1)}, f32[2,32,8,128]{3,2,1,0:T(8,128)S(1)}, u32[]{:S(2)}, u32[]{:S(2)}) collective-permute-start(f32[2,32,8,128]{3,2,1,0:T(8,128)S(1)} %receive.1), channel_id=1, source_target_pairs={{0,128},{128,0},{1,129},{129,1},{2,130},{130,2},{3,131},{131,3},{4... | collective-permute-start | bytes 786440 | tf_op jit(solution)/shard_map/ppermute | solution.py:449
  31.5 18.0 %all-to-all-start.1 = ((f32[32,8,128]{2,1,0:T(8,128)}), f32[32,8,128]{2,1,0:T(8,128)S(1)}, u32[]{:S(2)}, u32[]{:S(2)}) async-start(f32[32,8,128]{2,1,0:T(8,128)} %gather_slots.1), calls=%async_computation.1 | async-start | bytes 262144 | tf_op jit(solution)/shard_map/all_to_all | solution.py:470
  39.3 10.3 %collective-permute-start.7 = (f32[2,16,512]{2,1,0:T(8,128)S(1)}, f32[2,16,512]{2,1,0:T(8,128)S(1)}, u32[]{:S(2)}, u32[]{:S(2)}) collective-permute-start(f32[2,16,512]{2,1,0:T(8,128)S(1)} %get-tuple-element.68), channel_id=1, source_target_pairs={{0,128},{128,0},{1,129},{129,1},{2,130},{130,2},{3,131},{131,3},{4... | collective-permute-start | bytes 196616 | tf_op jit(solution)/shard_map/ppermute | solution.py:449
  55.3 14.3 %all-to-all-start.2 = ((f32[32,8,128]{2,1,0:T(8,128)}), f32[32,8,128]{2,1,0:T(8,128)S(1)}, u32[]{:S(2)}, u32[]{:S(2)}) async-start(f32[32,8,128]{2,1,0:T(8,128)} %get-tuple-element.72), calls=%async_computation.2 | async-start | bytes 262144 | tf_op jit(solution)/shard_map/all_to_all | solution.py:470
  59.2 13.0 %collective-permute-start.8 = (f32[2,16,512]{2,1,0:T(8,128)S(1)}, f32[2,16,512]{2,1,0:T(8,128)S(1)}, u32[]{:S(2)}, u32[]{:S(2)}) collective-permute-start(f32[2,16,512]{2,1,0:T(8,128)S(1)} %get-tuple-element.71), channel_id=1, source_target_pairs={{0,128},{128,0},{1,129},{129,1},{2,130},{130,2},{3,131},{131,3},{4... | collective-permute-start | bytes 196616 | tf_op jit(solution)/shard_map/ppermute | solution.py:449
  72.2 7.1 %collective-permute-start.10 = (f32[1,8,512]{2,1,0:T(8,128)S(1)}, f32[1,8,512]{2,1,0:T(8,128)S(1)}, u32[]{:S(2)}, u32[]{:S(2)}) collective-permute-start(f32[1,8,512]{2,1,0:T(8,128)S(1)} %get-tuple-element.79), channel_id=1, source_target_pairs={{0,4},{4,8},{8,12},{12,16},{16,20},{20,24},{24,28},{28,32},{32,36}... | collective-permute-start | bytes 49160 | tf_op jit(solution)/shard_map/ppermute | solution.py:455
  73.4 6.0 %collective-permute-start.11 = (f32[1,8,512]{2,1,0:T(8,128)S(1)}, f32[1,8,512]{2,1,0:T(8,128)S(1)}, u32[]{:S(2)}, u32[]{:S(2)}) collective-permute-start(f32[1,8,512]{2,1,0:T(8,128)S(1)} %get-tuple-element.80), channel_id=1, source_target_pairs={{4,0},{8,4},{12,8},{16,12},{20,16},{24,20},{28,24},{32,28},{36,32}... | collective-permute-start | bytes 49160 | tf_op jit(solution)/shard_map/ppermute | solution.py:456
  77.7 4.9 %collective-permute-start.9 = (f32[1,8,512]{2,1,0:T(8,128)S(1)}, f32[1,8,512]{2,1,0:T(8,128)S(1)}, u32[]{:S(2)}, u32[]{:S(2)}) collective-permute-start(f32[1,8,512]{2,1,0:T(8,128)S(1)} %get-tuple-element.78), channel_id=1, source_target_pairs={{0,3},{1,2},{2,1},{3,0},{4,7},{5,6},{6,5},{7,4},{8,11},{9,10},{10,... | collective-permute-start | bytes 49160 | tf_op jit(solution)/shard_map/ppermute | solution.py:457
  82.7 3.7 %collective-permute-start.12 = (f32[24,128]{1,0:T(8,128)S(1)}, f32[24,128]{1,0:T(8,128)S(1)}, u32[]{:S(2)}, u32[]{:S(2)}) collective-permute-start(f32[24,128]{1,0:T(8,128)S(1)} %get-tuple-element.82), channel_id=1, source_target_pairs={{0,1},{1,2},{2,3},{3,0},{4,5},{5,6},{6,7},{7,4},{8,9},{9,10},{10,1... | collective-permute-start | bytes 36872 | tf_op jit(solution)/shard_map/ppermute | solution.py:464
  82.8 4.9 %collective-permute-start.13 = (f32[24,128]{1,0:T(8,128)S(1)}, f32[24,128]{1,0:T(8,128)S(1)}, u32[]{:S(2)}, u32[]{:S(2)}) collective-permute-start(f32[24,128]{1,0:T(8,128)S(1)} %get-tuple-element.83), channel_id=1, source_target_pairs={{1,0},{2,1},{3,2},{0,3},{5,4},{6,5},{7,6},{4,7},{9,8},{10,9},{11,1... | collective-permute-start | bytes 36872 | tf_op jit(solution)/shard_map/ppermute | solution.py:465

commit v7 on v6

--- a/solution.py
+++ b/solution.py
@@ -11,7 +11,7 @@
 XR, XC = 24, 640
 FIELDS = 2 * LEV + 1
 EDGES = FIELDS + LEV // 2
-SPLIT = 4
+SPLIT = 5
 BANDS, CAP = 32, 1024
 F32, BF16, I32 = jnp.float32, jnp.bfloat16, jnp.int32
 

time: 89.3 us -> 89.2 us (level)
    pallas_call x1, Pallas kernels: 3.78 us -> 2.87 us  [local(): levels(SPLIT, LEV, 'rest_two')]
    pallas_call x1, Pallas kernels: 2.87 us -> 3.78 us  [local(): levels(1, SPLIT, 'rest_one')]
where the time goes in v7:
time: 89.2 us; the launch traced here: 88.9 us
  starting transfers between devices  37 us (41%)
  waiting for transfers between devices  28.9 us (32%)
  Pallas kernels  22 us (25%)
  between operations  1.01 us (1%)
    all_to_all x3, starting transfers between devices, exchange(): return lax.all_to_all(slots, 'lat', 0, 0, tiled=True)  17.9 us
    all_to_all x3, waiting for transfers between devices, exchange(): return lax.all_to_all(slots, 'lat', 0, 0, tiled=True)  13.7 us
    ppermute x2, starting transfers between devices, along(): lax.ppermute(head, 'lat', [((i + 1) % n, i) for i in range(n)])  10.5 us
    pallas_call x1, Pallas kernels, local(): pl.pallas_call(couple_kernel, out_shape=(pair, slots), in_specs=[vmem] *...  5.74 us
    ppermute x2, waiting for transfers between devices, along(): lax.ppermute(mirror, 'lon', [(i, m - 1 - i) for i in range(m)])  5.64 us
    pallas_call x1, Pallas kernels, local(): levels(1, SPLIT, 'rest_one')  3.78 us
    ppermute x2, starting transfers between devices, around(): lax.ppermute(west, 'lon', [((i + 1) % n, i) for i in range(n)])  3.56 us
    ppermute x2, waiting for transfers between devices, along(): lax.ppermute(tail, 'lat', [(i, (i + 1) % n) for i in range(n)])  3.44 us
  transfers between devices with their start and end apart: 17, of which 11 were waited for; matrix products, arithmetic and copies ran while one was open for 0% of the time, Pallas kernels for 15%

profile of v7, /device:TPU:6, one launch (start us, length us, event | category | flops | bytes accessed | tf_op | source)
XLA Modules:
  0.0 88.9 jit_solution(13082901296116654130)
XLA Ops:
  0.7 1.4 %first_pack.1 = (f32[21,8,512]{2,1,0:T(8,128)S(1)}, f32[21,8,512]{2,1,0:T(8,128)S(1)}, f32[21,8,512]{2,1,0:T(8,128)S(1)}, f32[16,512]{1,0:T(8,128)S(1)}, f32[16,...) custom-call(f32[8,16,512]{2,1,0:T(8,128)} %bitcast.11, f32[8,16,512]{2,1,0:T(8,128)} %bitcast.16, f32[8,16,512]{2,1,0:T(8,128)} %bitcast.21, ...), custom_call_target="tpu_custom_call" | custom-call | tf_op jit(solution)/shard_map/first_pack/pallas_call | solution.py:488
  2.2 2.0 %collective-permute-start.1 = (f32[21,8,512]{2,1,0:T(8,128)S(1)}, f32[21,8,512]{2,1,0:T(8,128)S(1)}, u32[]{:S(2)}, u32[]{:S(2)}) collective-permute-start(f32[21,8,512]{2,1,0:T(8,128)S(1)} %get-tuple-element.49), channel_id=1, source_target_pairs={{0,4},{4,8},{8,12},{12,16},{16,20},{20,24},{24,28},{28,32},{32,36}... | collective-permute-start | bytes 1032200 | tf_op jit(solution)/shard_map/ppermute | solution.py:455
  4.2 6.5 %collective-permute-start.2 = (f32[21,8,512]{2,1,0:T(8,128)S(1)}, f32[21,8,512]{2,1,0:T(8,128)S(1)}, u32[]{:S(2)}, u32[]{:S(2)}) collective-permute-start(f32[21,8,512]{2,1,0:T(8,128)S(1)} %get-tuple-element.50), channel_id=1, source_target_pairs={{4,0},{8,4},{12,8},{16,12},{20,16},{24,20},{28,24},{32,28},{36,32}... | collective-permute-start | bytes 1032200 | tf_op jit(solution)/shard_map/ppermute | solution.py:456
  10.6 0.5 collective-permute-start.3
  11.1 6.3 %all-to-all-start = ((s32[32,8,128]{2,1,0:T(8,128)}), s32[32,8,128]{2,1,0:T(8,128)S(1)}, u32[]{:S(2)}, u32[]{:S(2)}) async-start(s32[32,8,128]{2,1,0:T(8,128)} %collective-permute-done), calls=%async_computation | async-start | bytes 262144 | tf_op jit(solution)/shard_map/all_to_all | solution.py:470
  17.4 1.7 %collective-permute-done.1.from_south_ref = f32[21,8,512]{2,1,0:T(8,128)S(1)} collective-permute-done((f32[21,8,512]{2,1,0:T(8,128)S(1)}, f32[21,8,512]{2,1,0:T(8,128)S(1)}, u32[]{:S(2)}, u32[]{:S(2)}) %collective-permute-start.1) | collective-permute-done | bytes 344096 | tf_op jit(solution)/shard_map/ppermute | solution.py:455
  19.2 0.3 collective-permute-done.2.from_north_ref
  19.5 2.4 %collective-permute-done.3.from_fold_ref = f32[21,8,512]{2,1,0:T(8,128)S(1)} collective-permute-done((f32[21,8,512]{2,1,0:T(8,128)S(1)}, f32[21,8,512]{2,1,0:T(8,128)S(1)}, u32[]{:S(2)}, u32[]{:S(2)}) %collective-permute-start.3) | collective-permute-done | bytes 344096 | tf_op jit(solution)/shard_map/ppermute | solution.py:457
  22.2 0.6 collective-permute-start.4
  22.7 1.5 %collective-permute-start.5 = (f32[32,256]{1,0:T(8,128)S(1)}, f32[32,256]{1,0:T(8,128)S(1)}, u32[]{:S(2)}, u32[]{:S(2)}) collective-permute-start(f32[32,256]{1,0:T(8,128)S(1)} %get-tuple-element.56), channel_id=1, source_target_pairs={{1,0},{2,1},{3,2},{0,3},{5,4},{6,5},{7,6},{4,7},{9,8},{10,9},{11,1... | collective-permute-start | bytes 98312 | tf_op jit(solution)/shard_map/ppermute | solution.py:465
  24.3 0.6 receive.1
  25.0 1.2 %collective-permute-done.4.from_west_ref = f32[32,256]{1,0:T(8,128)S(1)} collective-permute-done((f32[32,256]{1,0:T(8,128)S(1)}, f32[32,256]{1,0:T(8,128)S(1)}, u32[]{:S(2)}, u32[]{:S(2)}) %collective-permute-start.4) | collective-permute-done | bytes 32800 | tf_op jit(solution)/shard_map/ppermute | solution.py:464
  26.1 1.7 %collective-permute-done.5.from_east_ref = f32[32,256]{1,0:T(8,128)S(1)} collective-permute-done((f32[32,256]{1,0:T(8,128)S(1)}, f32[32,256]{1,0:T(8,128)S(1)}, u32[]{:S(2)}, u32[]{:S(2)}) %collective-permute-start.5) | collective-permute-done | bytes 32800 | tf_op jit(solution)/shard_map/ppermute | solution.py:465
  27.8 0.5 first_surface.1
  28.3 3.2 %gather_slots.1 = f32[32,8,128]{2,1,0:T(8,128)} custom-call(s32[32,8,128]{2,1,0:T(8,128)S(1)} %all-to-all-done.cells_ref, f32[16,512]{1,0:T(8,128)S(1)} %get-tuple-element.57.table_ref), custom_call_target="tpu_custom_call" | custom-call | tf_op jit(solution)/shard_map/gather_slots/pallas_call | solution.py:533
  31.5 7.7 %all-to-all-start.1 = ((f32[32,8,128]{2,1,0:T(8,128)}), f32[32,8,128]{2,1,0:T(8,128)S(1)}, u32[]{:S(2)}, u32[]{:S(2)}) async-start(f32[32,8,128]{2,1,0:T(8,128)} %gather_slots.1), calls=%async_computation.1 | async-start | bytes 262144 | tf_op jit(solution)/shard_map/all_to_all | solution.py:470
  39.4 3.8 %rest_one.1 = (f32[4,16,512]{2,1,0:T(8,128)S(1)}, f32[4,16,512]{2,1,0:T(8,128)S(1)}) custom-call(f32[8,16,512]{2,1,0:T(8,128)S(1)} %bitcast.14, f32[8,16,512]{2,1,0:T(8,128)S(1)} %bitcast.19, f32[8,16,512]{2,1,0:T(8,128)S(1)} %bitcast.24, f32[16,512]{1,0:T(8,128)S(1)} %get-tuple-element.48.mask_ref, f32[17,16,512]{2,1,0:T(8,128)S(1)} %get-tuple-element.73.halo_ref, ...), custom_call_target="tpu_custom_call" | custom-call | flops 100000 | bytes 12000000 | tf_op jit(solution)/shard_map/rest_one/pallas_call | solution.py:553
  43.1 6.4 %all-to-all-done.1.values_ref = f32[32,8,128]{2,1,0:T(8,128)S(1)} async-done(((f32[32,8,128]{2,1,0:T(8,128)}), f32[32,8,128]{2,1,0:T(8,128)S(1)}, u32[]{:S(2)}, u32[]{:S(2)}) %all-to-all-start.1) | async-done | bytes 131104 | tf_op jit(solution)/shard_map/all_to_all | solution.py:470
  49.6 5.7 %couple.1 = (f32[2,16,512]{2,1,0:T(8,128)S(1)}, f32[32,8,128]{2,1,0:T(8,128)}) custom-call(f32[32,8,128]{2,1,0:T(8,128)S(1)} %all-to-all-done.1.values_ref, f32[2,32,8,128]{3,2,1,0:T(8,128)S(1)} %collective-permute-done.6.slots_ref, f32[16,512]{1,0:T(8,128)S(1)} %get-tuple-element.67.mask_ref, f32[2,16,512]{2,1,0:T(8,128)S(1)} %collective-permute-done.7.state_ref), custom_call_target="tpu_custom_call" | custom-call | tf_op jit(solution)/shard_map/couple/pallas_call | solution.py:559
  55.3 3.9 %all-to-all-start.2 = ((f32[32,8,128]{2,1,0:T(8,128)}), f32[32,8,128]{2,1,0:T(8,128)S(1)}, u32[]{:S(2)}, u32[]{:S(2)}) async-start(f32[32,8,128]{2,1,0:T(8,128)} %get-tuple-element.72), calls=%async_computation.2 | async-start | bytes 262144 | tf_op jit(solution)/shard_map/all_to_all | solution.py:470
  59.2 0.3 collective-permute-start.8
  59.5 2.9 %rest_two.1 = (f32[3,16,512]{2,1,0:T(8,128)S(1)}, f32[3,16,512]{2,1,0:T(8,128)S(1)}) custom-call(f32[8,16,512]{2,1,0:T(8,128)S(1)} %bitcast.15, f32[8,16,512]{2,1,0:T(8,128)S(1)} %bitcast.20, f32[8,16,512]{2,1,0:T(8,128)S(1)} %bitcast.25, f32[16,512]{1,0:T(8,128)S(1)} %get-tuple-element.48.mask_ref, f32[17,16,512]{2,1,0:T(8,128)S(1)} %get-tuple-element.73.halo_ref, ...), custom_call_target="tpu_custom_call" | custom-call | flops 100000 | bytes 12000000 | tf_op jit(solution)/shard_map/rest_two/pallas_call | solution.py:572
  62.4 7.2 %all-to-all-done.2.values_ref = f32[32,8,128]{2,1,0:T(8,128)S(1)} async-done(((f32[32,8,128]{2,1,0:T(8,128)}), f32[32,8,128]{2,1,0:T(8,128)S(1)}, u32[]{:S(2)}, u32[]{:S(2)}) %all-to-all-start.2) | async-done | bytes 131104 | tf_op jit(solution)/shard_map/all_to_all | solution.py:470
  69.6 2.5 %collect.1.returned_ref = f32[16,512]{1,0:T(8,128)S(1)} custom-call(f32[32,8,128]{2,1,0:T(8,128)S(1)} %all-to-all-done.2.values_ref, s32[32,8,128]{2,1,0:T(8,128)S(1)} %all-to-all-done.cells_ref), custom_call_target="tpu_custom_call" | custom-call | flops 100000 | bytes 1000000 | tf_op jit(solution)/shard_map/collect/pallas_call | solution.py:577
  72.2 1.4 %collective-permute-start.10 = (f32[1,8,512]{2,1,0:T(8,128)S(1)}, f32[1,8,512]{2,1,0:T(8,128)S(1)}, u32[]{:S(2)}, u32[]{:S(2)}) collective-permute-start(f32[1,8,512]{2,1,0:T(8,128)S(1)} %get-tuple-element.79), channel_id=1, source_target_pairs={{0,4},{4,8},{8,12},{12,16},{16,20},{20,24},{24,28},{28,32},{32,36}... | collective-permute-start | bytes 49160 | tf_op jit(solution)/shard_map/ppermute | solution.py:455
  73.5 4.1 %collective-permute-start.11 = (f32[1,8,512]{2,1,0:T(8,128)S(1)}, f32[1,8,512]{2,1,0:T(8,128)S(1)}, u32[]{:S(2)}, u32[]{:S(2)}) collective-permute-start(f32[1,8,512]{2,1,0:T(8,128)S(1)} %get-tuple-element.80), channel_id=1, source_target_pairs={{4,0},{8,4},{12,8},{16,12},{20,16},{24,20},{28,24},{32,28},{36,32}... | collective-permute-start | bytes 49160 | tf_op jit(solution)/shard_map/ppermute | solution.py:456
  77.6 1.7 %collective-permute-done.10.from_south_ref = f32[1,8,512]{2,1,0:T(8,128)S(1)} collective-permute-done((f32[1,8,512]{2,1,0:T(8,128)S(1)}, f32[1,8,512]{2,1,0:T(8,128)S(1)}, u32[]{:S(2)}, u32[]{:S(2)}) %collective-permute-start.10) | collective-permute-done | bytes 16416 | tf_op jit(solution)/shard_map/ppermute | solution.py:455
  79.3 3.2 %collective-permute-done.9.from_fold_ref = f32[1,8,512]{2,1,0:T(8,128)S(1)} collective-permute-done((f32[1,8,512]{2,1,0:T(8,128)S(1)}, f32[1,8,512]{2,1,0:T(8,128)S(1)}, u32[]{:S(2)}, u32[]{:S(2)}) %collective-permute-start.9) | collective-permute-done | bytes 16416 | tf_op jit(solution)/shard_map/ppermute | solution.py:457
  82.7 2.0 %collective-permute-start.13 = (f32[24,128]{1,0:T(8,128)S(1)}, f32[24,128]{1,0:T(8,128)S(1)}, u32[]{:S(2)}, u32[]{:S(2)}) collective-permute-start(f32[24,128]{1,0:T(8,128)S(1)} %get-tuple-element.83), channel_id=1, source_target_pairs={{1,0},{2,1},{3,2},{0,3},{5,4},{6,5},{7,6},{4,7},{9,8},{10,9},{11,1... | collective-permute-start | bytes 36872 | tf_op jit(solution)/shard_map/ppermute | solution.py:465
  84.7 1.7 %collective-permute-done.12.from_west_ref = f32[24,128]{1,0:T(8,128)S(1)} collective-permute-done((f32[24,128]{1,0:T(8,128)S(1)}, f32[24,128]{1,0:T(8,128)S(1)}, u32[]{:S(2)}, u32[]{:S(2)}) %collective-permute-start.12) | collective-permute-done | bytes 12320 | tf_op jit(solution)/shard_map/ppermute | solution.py:464
  86.4 1.3 %collective-permute-done.13.from_east_ref = f32[24,128]{1,0:T(8,128)S(1)} collective-permute-done((f32[24,128]{1,0:T(8,128)S(1)}, f32[24,128]{1,0:T(8,128)S(1)}, u32[]{:S(2)}, u32[]{:S(2)}) %collective-permute-start.13) | collective-permute-done | bytes 12320 | tf_op jit(solution)/shard_map/ppermute | solution.py:465
  87.7 1.1 %second_surface.1 = (f32[8,16,512]{2,1,0:T(8,128)}, f32[8,16,512]{2,1,0:T(8,128)}) custom-call(f32[16,512]{1,0:T(8,128)S(1)} %get-tuple-element.77.adj_ref, f32[8,512]{1,0:T(8,128)S(1)} %get-tuple-element.81.halo_ref, f32[24,128]{1,0:T(8,128)S(1)} %collective-permute-done.12.from_west_ref, f32[24,128]{1,0:T(8,128)S(1)} %collective-permute-done.13.from_east_ref, ...), custom_call_target="tpu_custom_call" | custom-call | tf_op jit(solution)/shard_map/second_surface/pallas_call | solution.py:588
  (27 shorter events, 0.7 us)
Async XLA Ops:
  0.6 21.2 %copy-start.1 = (f32[1,8,16,512]{3,2,1,0:T(8,128)S(1)}, f32[1,8,16,512]{3,2,1,0:T(8,128)}, u32[]{:S(2)}) copy-start(f32[1,8,16,512]{3,2,1,0:T(8,128)} %param.9) | copy-start | bytes 786436
  0.6 21.2 %copy-start.2 = (f32[1,8,16,512]{3,2,1,0:T(8,128)S(1)}, f32[1,8,16,512]{3,2,1,0:T(8,128)}, u32[]{:S(2)}) copy-start(f32[1,8,16,512]{3,2,1,0:T(8,128)} %param.10) | copy-start | bytes 786436
  2.0 19.8 %copy-start = (f32[1,8,16,512]{3,2,1,0:T(8,128)S(1)}, f32[1,8,16,512]{3,2,1,0:T(8,128)}, u32[]{:S(2)}) copy-start(f32[1,8,16,512]{3,2,1,0:T(8,128)} %param.8) | copy-start | bytes 786436
  2.1 9.1 %collective-permute-start = (s32[32,8,128]{2,1,0:T(8,128)S(1)}, s32[32,8,128]{2,1,0:T(8,128)}, u32[]{:S(2)}, u32[]{:S(2)}) collective-permute-start(s32[32,8,128]{2,1,0:T(8,128)S(1)} %get-tuple-element.47), channel_id=1, source_target_pairs={{0,128},{128,0},{1,129},{129,1},{2,130},{130,2},{3,131},{131,3},{4... | collective-permute-start | bytes 393224 | tf_op jit(solution)/shard_map/ppermute | solution.py:449
  2.2 17.0 %collective-permute-start.1 = (f32[21,8,512]{2,1,0:T(8,128)S(1)}, f32[21,8,512]{2,1,0:T(8,128)S(1)}, u32[]{:S(2)}, u32[]{:S(2)}) collective-permute-start(f32[21,8,512]{2,1,0:T(8,128)S(1)} %get-tuple-element.49), channel_id=1, source_target_pairs={{0,4},{4,8},{8,12},{12,16},{16,20},{20,24},{24,28},{28,32},{32,36}... | collective-permute-start | bytes 1032200 | tf_op jit(solution)/shard_map/ppermute | solution.py:455
  4.2 15.3 %collective-permute-start.2 = (f32[21,8,512]{2,1,0:T(8,128)S(1)}, f32[21,8,512]{2,1,0:T(8,128)S(1)}, u32[]{:S(2)}, u32[]{:S(2)}) collective-permute-start(f32[21,8,512]{2,1,0:T(8,128)S(1)} %get-tuple-element.50), channel_id=1, source_target_pairs={{4,0},{8,4},{12,8},{16,12},{20,16},{24,20},{28,24},{32,28},{36,32}... | collective-permute-start | bytes 1032200 | tf_op jit(solution)/shard_map/ppermute | solution.py:456
  10.6 11.2 %collective-permute-start.3 = (f32[21,8,512]{2,1,0:T(8,128)S(1)}, f32[21,8,512]{2,1,0:T(8,128)S(1)}, u32[]{:S(2)}, u32[]{:S(2)}) collective-permute-start(f32[21,8,512]{2,1,0:T(8,128)S(1)} %get-tuple-element.51), channel_id=1, source_target_pairs={{0,3},{1,2},{2,1},{3,0},{4,7},{5,6},{6,5},{7,4},{8,11},{9,10},{10,... | collective-permute-start | bytes 1032200 | tf_op jit(solution)/shard_map/ppermute | solution.py:457
  11.1 17.2 %all-to-all-start = ((s32[32,8,128]{2,1,0:T(8,128)}), s32[32,8,128]{2,1,0:T(8,128)S(1)}, u32[]{:S(2)}, u32[]{:S(2)}) async-start(s32[32,8,128]{2,1,0:T(8,128)} %collective-permute-done), calls=%async_computation | async-start | bytes 262144 | tf_op jit(solution)/shard_map/all_to_all | solution.py:470
  21.9 2.4 %copy-start.3 = (s32[1,1,1,32,1024]{4,3,2,1,0:T(8,128)S(1)}, s32[1,1,1,32,1024]{4,3,2,1,0:T(8,128)}, u32[]{:S(2)}) copy-start(s32[1,1,1,32,1024]{4,3,2,1,0:T(8,128)} %param.13) | copy-start | bytes 393220
  21.9 2.4 %copy-start.4 = (f32[1,1,1,32,1024]{4,3,2,1,0:T(8,128)S(1)}, f32[1,1,1,32,1024]{4,3,2,1,0:T(8,128)}, u32[]{:S(2)}) copy-start(f32[1,1,1,32,1024]{4,3,2,1,0:T(8,128)} %param.14) | copy-start | bytes 393220
  22.1 2.1 %copy-start.5 = (s32[1,1,1,32]{3,2,1,0:T(1,128)S(1)}, s32[1,1,1,32]{3,2,1,0:T(1,128)}, u32[]{:S(2)}) copy-start(s32[1,1,1,32]{3,2,1,0:T(1,128)} %param.15) | copy-start | bytes 388
  22.2 4.0 %collective-permute-start.4 = (f32[32,256]{1,0:T(8,128)S(1)}, f32[32,256]{1,0:T(8,128)S(1)}, u32[]{:S(2)}, u32[]{:S(2)}) collective-permute-start(f32[32,256]{1,0:T(8,128)S(1)} %get-tuple-element.55), channel_id=1, source_target_pairs={{0,1},{1,2},{2,3},{3,0},{4,5},{5,6},{6,7},{7,4},{8,9},{9,10},{10,1... | collective-permute-start | bytes 98312 | tf_op jit(solution)/shard_map/ppermute | solution.py:464
  22.7 5.1 %collective-permute-start.5 = (f32[32,256]{1,0:T(8,128)S(1)}, f32[32,256]{1,0:T(8,128)S(1)}, u32[]{:S(2)}, u32[]{:S(2)}) collective-permute-start(f32[32,256]{1,0:T(8,128)S(1)} %get-tuple-element.56), channel_id=1, source_target_pairs={{1,0},{2,1},{3,2},{0,3},{5,4},{6,5},{7,6},{4,7},{9,8},{10,9},{11,1... | collective-permute-start | bytes 98312 | tf_op jit(solution)/shard_map/ppermute | solution.py:465
  24.9 24.7 %collective-permute-start.6 = (f32[2,32,8,128]{3,2,1,0:T(8,128)S(1)}, f32[2,32,8,128]{3,2,1,0:T(8,128)S(1)}, u32[]{:S(2)}, u32[]{:S(2)}) collective-permute-start(f32[2,32,8,128]{3,2,1,0:T(8,128)S(1)} %receive.1), channel_id=1, source_target_pairs={{0,128},{128,0},{1,129},{129,1},{2,130},{130,2},{3,131},{131,3},{4... | collective-permute-start | bytes 786440 | tf_op jit(solution)/shard_map/ppermute | solution.py:449
  31.5 18.0 %all-to-all-start.1 = ((f32[32,8,128]{2,1,0:T(8,128)}), f32[32,8,128]{2,1,0:T(8,128)S(1)}, u32[]{:S(2)}, u32[]{:S(2)}) async-start(f32[32,8,128]{2,1,0:T(8,128)} %gather_slots.1), calls=%async_computation.1 | async-start | bytes 262144 | tf_op jit(solution)/shard_map/all_to_all | solution.py:470
  39.3 10.3 %collective-permute-start.7 = (f32[2,16,512]{2,1,0:T(8,128)S(1)}, f32[2,16,512]{2,1,0:T(8,128)S(1)}, u32[]{:S(2)}, u32[]{:S(2)}) collective-permute-start(f32[2,16,512]{2,1,0:T(8,128)S(1)} %get-tuple-element.68), channel_id=1, source_target_pairs={{0,128},{128,0},{1,129},{129,1},{2,130},{130,2},{3,131},{131,3},{4... | collective-permute-start | bytes 196616 | tf_op jit(solution)/shard_map/ppermute | solution.py:449
  55.3 14.3 %all-to-all-start.2 = ((f32[32,8,128]{2,1,0:T(8,128)}), f32[32,8,128]{2,1,0:T(8,128)S(1)}, u32[]{:S(2)}, u32[]{:S(2)}) async-start(f32[32,8,128]{2,1,0:T(8,128)} %get-tuple-element.72), calls=%async_computation.2 | async-start | bytes 262144 | tf_op jit(solution)/shard_map/all_to_all | solution.py:470
  59.2 12.9 %collective-permute-start.8 = (f32[2,16,512]{2,1,0:T(8,128)S(1)}, f32[2,16,512]{2,1,0:T(8,128)S(1)}, u32[]{:S(2)}, u32[]{:S(2)}) collective-permute-start(f32[2,16,512]{2,1,0:T(8,128)S(1)} %get-tuple-element.71), channel_id=1, source_target_pairs={{0,128},{128,0},{1,129},{129,1},{2,130},{130,2},{3,131},{131,3},{4... | collective-permute-start | bytes 196616 | tf_op jit(solution)/shard_map/ppermute | solution.py:449
  72.2 7.1 %collective-permute-start.10 = (f32[1,8,512]{2,1,0:T(8,128)S(1)}, f32[1,8,512]{2,1,0:T(8,128)S(1)}, u32[]{:S(2)}, u32[]{:S(2)}) collective-permute-start(f32[1,8,512]{2,1,0:T(8,128)S(1)} %get-tuple-element.79), channel_id=1, source_target_pairs={{0,4},{4,8},{8,12},{12,16},{16,20},{20,24},{24,28},{28,32},{32,36}... | collective-permute-start | bytes 49160 | tf_op jit(solution)/shard_map/ppermute | solution.py:455
  73.5 5.8 %collective-permute-start.11 = (f32[1,8,512]{2,1,0:T(8,128)S(1)}, f32[1,8,512]{2,1,0:T(8,128)S(1)}, u32[]{:S(2)}, u32[]{:S(2)}) collective-permute-start(f32[1,8,512]{2,1,0:T(8,128)S(1)} %get-tuple-element.80), channel_id=1, source_target_pairs={{4,0},{8,4},{12,8},{16,12},{20,16},{24,20},{28,24},{32,28},{36,32}... | collective-permute-start | bytes 49160 | tf_op jit(solution)/shard_map/ppermute | solution.py:456
  77.6 4.9 %collective-permute-start.9 = (f32[1,8,512]{2,1,0:T(8,128)S(1)}, f32[1,8,512]{2,1,0:T(8,128)S(1)}, u32[]{:S(2)}, u32[]{:S(2)}) collective-permute-start(f32[1,8,512]{2,1,0:T(8,128)S(1)} %get-tuple-element.78), channel_id=1, source_target_pairs={{0,3},{1,2},{2,1},{3,0},{4,7},{5,6},{6,5},{7,4},{8,11},{9,10},{10,... | collective-permute-start | bytes 49160 | tf_op jit(solution)/shard_map/ppermute | solution.py:457
  82.6 3.7 %collective-permute-start.12 = (f32[24,128]{1,0:T(8,128)S(1)}, f32[24,128]{1,0:T(8,128)S(1)}, u32[]{:S(2)}, u32[]{:S(2)}) collective-permute-start(f32[24,128]{1,0:T(8,128)S(1)} %get-tuple-element.82), channel_id=1, source_target_pairs={{0,1},{1,2},{2,3},{3,0},{4,5},{5,6},{6,7},{7,4},{8,9},{9,10},{10,1... | collective-permute-start | bytes 36872 | tf_op jit(solution)/shard_map/ppermute | solution.py:464
  82.7 5.0 %collective-permute-start.13 = (f32[24,128]{1,0:T(8,128)S(1)}, f32[24,128]{1,0:T(8,128)S(1)}, u32[]{:S(2)}, u32[]{:S(2)}) collective-permute-start(f32[24,128]{1,0:T(8,128)S(1)} %get-tuple-element.83), channel_id=1, source_target_pairs={{1,0},{2,1},{3,2},{0,3},{5,4},{6,5},{7,6},{4,7},{9,8},{10,9},{11,1... | collective-permute-start | bytes 36872 | tf_op jit(solution)/shard_map/ppermute | solution.py:465
